TPU v7x, 32 devices: a whole 2x2x4 slice. The times are simulated.
32 devices in a mesh: dev: 2 (over x), sa: 16 (over z, y, core).
Axes of the slice: x: 2, y: 2, z: 4, core: 2. Of those that a mesh axis runs over, the one named last changes fastest.
Arguments:
- patches: bfloat16 [8, 1024, 1152], P('dev', 'sa'), may hold values from -6 to 6
- patch_mask: int32 [8, 1024], P('dev', 'sa'), may hold values from 0 to 1, as said below
- cotangent: bfloat16 [8, 1024, 1152], P('dev', 'sa'), may hold values from -6 to 6
- w_qkv: bfloat16 [1152, 3456], P('sa', 'dev'), may hold values from -0.1875 to 0.1875
- w_out: bfloat16 [1152, 1152], P('sa', 'dev'), may hold values from -0.75 to 0.75
- w_up: bfloat16 [1152, 4304], P('sa', 'dev'), may hold values from -0.1875 to 0.1875
- w_down: bfloat16 [1152, 4304], P('sa', 'dev'), may hold values from -0.125 to 0.125
- gain_one: bfloat16 [1, 1152], P(None, 'dev'), may hold values from 0.25 to 1.75
- shift_one: bfloat16 [1, 1152], P(None, 'dev'), may hold values from -4 to 4
- gain_two: bfloat16 [1, 1152], P(None, 'dev'), may hold values from 0.25 to 1.75
- shift_two: bfloat16 [1, 1152], P(None, 'dev'), may hold values from -4 to 4
- bias_query: bfloat16 [1, 1152], P(None, 'dev'), may hold values from -4 to 4
- bias_value: bfloat16 [1, 1152], P(None, 'dev'), may hold values from -4 to 4
- bias_out: bfloat16 [1, 1152], P(None, 'dev'), may hold values from -4 to 4
- bias_up: bfloat16 [1, 4304], P(None, 'dev'), may hold values from -4 to 4
- bias_down: bfloat16 [1, 1152], P(None, 'dev'), may hold values from -4 to 4
Outputs:
- result: bfloat16 [8, 1024, 1152], P('dev', 'sa')
- grad_patches: bfloat16 [8, 1024, 1152], P('dev', 'sa')
- grad_w_qkv: float32 [1152, 3456], P('sa', 'dev')
- grad_w_out: float32 [1152, 1152], P('sa', 'dev')
- grad_w_up: float32 [1152, 4304], P('sa', 'dev')
- grad_w_down: float32 [1152, 4304], P('sa', 'dev')
- grad_gain_one: float32 [1, 1152], P(None, 'dev')
- grad_shift_one: float32 [1, 1152], P(None, 'dev')
- grad_gain_two: float32 [1, 1152], P(None, 'dev')
- grad_shift_two: float32 [1, 1152], P(None, 'dev')
- grad_bias_query: float32 [1, 1152], P(None, 'dev')
- grad_bias_value: float32 [1, 1152], P(None, 'dev')
- grad_bias_out: float32 [1, 1152], P(None, 'dev')
- grad_bias_up: float32 [1, 4304], P(None, 'dev')
- grad_bias_down: float32 [1, 1152], P(None, 'dev')
Inputs may be any that keep to these rules, and one draw needn't show every extreme that they name: `patch_mask`: each image's ones are its first patches, 256 of them or more.
All inputs are finite; a program needn't handle non-finite values.
Results may differ from a plain program's by a relative error of at most 0.018.
Values may be sent and summed in bfloat16 or wider, within the bound.
No kernel may reach another device: no remote copies, remote signals or barrier semaphores. Data moves between devices by JAX's collectives and lax.ppermute only.
A program may use at most 256 MiB of HBM per device.

v0:
```python
import functools

import jax
import jax.numpy as jnp
from jax import lax
from jax.experimental import pallas as pl
from jax.experimental.pallas import tpu as pltpu
from jax.experimental.layout import Layout, with_layout_constraint
from jax.sharding import Mesh
from jax.sharding import PartitionSpec as P

HEADS = 16
HEAD_DIM = 72
SCALE = HEAD_DIM ** (-0.5)
Q_BLOCK = 256
F32 = jnp.float32
BF16 = jnp.bfloat16


def dot(left, right):
    return jnp.dot(left, right, preferred_element_type=F32)


def dot_tn(left, right):
    return lax.dot_general(left, right, (((0,), (0,)), ((), ())), preferred_element_type=F32)


def dot_nt(left, right):
    return lax.dot_general(left, right, (((1,), (1,)), ((), ())), preferred_element_type=F32)


def row_major(values):
    return with_layout_constraint(values, Layout(tuple(range(values.ndim))))


def after(value, *others):
    if not others:
        return value
    return lax.optimization_barrier((value, *others))[0]


def attend_fwd_body(heads, qkv_ref, bias_ref, out_ref, lse_ref):
    width = heads * HEAD_DIM
    rows = pl.ds(pl.program_id(1) * Q_BLOCK, Q_BLOCK)
    bias = bias_ref[0]
    for head in range(heads):
        low = head * HEAD_DIM
        query = qkv_ref[0, rows, low : low + HEAD_DIM]
        keys = qkv_ref[0, :, width + low : width + low + HEAD_DIM]
        values = qkv_ref[0, :, 2 * width + low : 2 * width + low + HEAD_DIM]
        scores = dot_nt(keys, query) * SCALE + bias
        peak = jnp.max(scores, axis=0, keepdims=True)
        expo = jnp.exp(scores - peak)
        total = jnp.sum(expo, axis=0, keepdims=True)
        mixed = dot_tn(values, expo.astype(BF16)) / total
        out_ref[0, low : low + HEAD_DIM, :] = mixed.astype(BF16)
        lse_ref[0, head : head + 1, :] = peak + jnp.log(total)
    if heads < 8:
        lse_ref[0, heads:, :] = jnp.zeros((8 - heads, Q_BLOCK), F32)


def attend_bwd_body(
    heads, qkv_ref, bias_ref, lse_ref, branch_ref, w_ref, out_ref, key_acc, value_acc, grad_ref
):
    width = heads * HEAD_DIM
    step = pl.program_id(1)
    begin = step * Q_BLOCK
    bias = bias_ref[0]

    @pl.when(step == 0)
    def _():
        key_acc[...] = jnp.zeros_like(key_acc)
        value_acc[...] = jnp.zeros_like(value_acc)

    grad_ref[...] = dot_nt(branch_ref[0], w_ref[...]).astype(BF16)
    for head in range(heads):
        low = head * HEAD_DIM
        rows = pl.ds(begin, Q_BLOCK)
        query = qkv_ref[0, rows, low : low + HEAD_DIM]
        grad = grad_ref[:, low : low + HEAD_DIM]
        keys = qkv_ref[0, :, width + low : width + low + HEAD_DIM]
        values = qkv_ref[0, :, 2 * width + low : 2 * width + low + HEAD_DIM]
        scores = dot_nt(keys, query) * SCALE + bias
        probs = jnp.exp(scores - lse_ref[0, head : head + 1, :])
        value_acc[head] += dot(probs.astype(BF16), grad)
        grad_probs = dot_nt(values, grad)
        term = jnp.sum(probs * grad_probs, axis=0, keepdims=True)
        grad_scores = (probs * (grad_probs - term)).astype(BF16)
        key_acc[head] += dot(grad_scores, query)
        grad_query = dot_tn(grad_scores, keys) * SCALE
        out_ref[0, rows, low : low + HEAD_DIM] = grad_query.astype(BF16)

    @pl.when(step == pl.num_programs(1) - 1)
    def _():
        for head in range(heads):
            low = head * HEAD_DIM
            out_ref[0, :, width + low : width + low + HEAD_DIM] = (key_acc[head] * SCALE).astype(BF16)
            out_ref[0, :, 2 * width + low : 2 * width + low + HEAD_DIM] = value_acc[head].astype(BF16)


def run(body, name, steps, operands, specs, outs, out_specs, flops, scratch=(), pick=None):
    size = sum(item.size * item.dtype.itemsize for item in operands)
    picks = () if pick is None else (pick,)
    return pl.pallas_call(
        body,
        name=name,
        grid_spec=pltpu.PrefetchScalarGridSpec(
            num_scalar_prefetch=len(picks),
            grid=steps,
            in_specs=specs,
            out_specs=out_specs,
            scratch_shapes=scratch,
        ),
        out_shape=outs,
        cost_estimate=pl.CostEstimate(flops=flops, transcendentals=0, bytes_accessed=size),
        compiler_params=pltpu.CompilerParams(vmem_limit_bytes=50 << 20),
    )(*picks, *operands)


def rows_spec(wide):
    return pl.BlockSpec((Q_BLOCK, wide), lambda i, *_: (i, 0))


def fixed(item):
    shape = item.shape
    return pl.BlockSpec(shape, lambda *_: (0,) * len(shape))


def picked(item, wide):
    return pl.BlockSpec((item.shape[0], wide), lambda i, pick: (0, pick[0]))


def shaped(shape, dtype):
    return jax.ShapeDtypeStruct(shape, dtype)


def attend_fwd(qkv, bias, heads):
    images, seq, wide = qkv.shape
    width = heads * HEAD_DIM
    return run(
        functools.partial(attend_fwd_body, heads),
        "attend_fwd",
        (images, seq // Q_BLOCK),
        (qkv, bias),
        [
            pl.BlockSpec((1, seq, wide), lambda i, j: (i, 0, 0)),
            pl.BlockSpec((1, seq, 1), lambda i, j: (i, 0, 0)),
        ],
        [shaped((images, width, seq), BF16), shaped((images, 8, seq), F32)],
        [
            pl.BlockSpec((1, width, Q_BLOCK), lambda i, j: (i, 0, j)),
            pl.BlockSpec((1, 8, Q_BLOCK), lambda i, j: (i, 0, j)),
        ],
        4 * images * heads * seq * seq * 128,
    )


def attend_bwd(qkv, bias, lse, branch, w_rows, heads):
    images, seq, wide = qkv.shape
    return run(
        functools.partial(attend_bwd_body, heads),
        "attend_bwd",
        (images, seq // Q_BLOCK),
        (qkv, bias, lse, branch, w_rows),
        [
            pl.BlockSpec((1, seq, wide), lambda i, j: (i, 0, 0)),
            pl.BlockSpec((1, seq, 1), lambda i, j: (i, 0, 0)),
            pl.BlockSpec((1, 8, Q_BLOCK), lambda i, j: (i, 0, j)),
            pl.BlockSpec((1, Q_BLOCK, branch.shape[2]), lambda i, j: (i, j, 0)),
            fixed(w_rows),
        ],
        shaped((images, seq, wide), BF16),
        pl.BlockSpec((1, seq, wide), lambda i, j: (i, 0, 0)),
        10 * images * heads * seq * seq * 128,
        [
            pltpu.VMEM((heads, seq, HEAD_DIM), F32),
            pltpu.VMEM((heads, seq, HEAD_DIM), F32),
            pltpu.VMEM((Q_BLOCK, heads * HEAD_DIM), BF16),
        ],
    )


def centred(values):
    centre = values - jnp.mean(values, axis=-1, keepdims=True)
    spread = jnp.mean(centre * centre, axis=-1, keepdims=True)
    inverse = lax.rsqrt(spread + 1e-06)
    return centre * inverse, inverse


def project(pick, rows_all, gain, shift, weight, block, bias):
    count, width = rows_all.shape[0], gain.shape[1]
    wide = bias.shape[1]

    def body(_, rows_ref, gain_ref, shift_ref, weight_ref, bias_ref, normed_ref, out_ref):
        unit = centred(rows_ref[:, :width].astype(F32))[0]
        normed = (unit * gain_ref[...] + shift_ref[...]).astype(BF16)
        normed_ref[...] = normed
        out_ref[...] = (dot(normed, weight_ref[:, :wide]) + bias_ref[...]).astype(BF16)

    operands = (rows_all, gain, shift, weight, bias)
    return run(
        body,
        "project",
        (count // Q_BLOCK,),
        operands,
        [rows_spec(rows_all.shape[1]), fixed(gain), fixed(shift), picked(weight, block), fixed(bias)],
        [shaped((count, width), BF16), shaped((count, wide), BF16)],
        [rows_spec(width), rows_spec(wide)],
        2 * count * width * wide,
        pick=pick,
    )


def attend_out(pieces, weights, rows_all, bias, gain, shift):
    count, width = rows_all.shape[0], gain.shape[1]
    total = len(pieces)
    piece = pieces[0].shape[0]

    def body(*refs):
        piece_refs = refs[:total]
        weight_ref, rows_ref, bias_ref, gain_ref, shift_ref = refs[total:-2]
        middle_ref, normed_ref = refs[-2:]
        branch = dot_tn(piece_refs[0][...], weight_ref[0])
        for k in range(1, total):
            branch += dot_tn(piece_refs[k][...], weight_ref[k])
        middle = rows_ref[:, :width].astype(F32) + (branch + bias_ref[...])
        middle_ref[...] = middle
        normed_ref[...] = (centred(middle)[0] * gain_ref[...] + shift_ref[...]).astype(BF16)

    return run(
        body,
        "attend_out",
        (count // Q_BLOCK,),
        (*pieces, weights, rows_all, bias, gain, shift),
        [pl.BlockSpec((piece, Q_BLOCK), lambda i: (0, i))] * total
        + [fixed(weights), rows_spec(rows_all.shape[1])]
        + [fixed(bias), fixed(gain), fixed(shift)],
        [shaped((count, width), F32), shaped((count, width), BF16)],
        [rows_spec(width), rows_spec(width)],
        2 * count * width * width,
    )


def mlp_turn(pick, normed, grad, mlp, bias):
    count, width = normed.shape
    hidden = bias.shape[1]

    def body(_, normed_ref, grad_ref, mlp_ref, bias_ref, active_ref, slope_ref, back_ref, sums_ref):
        pre = dot(normed_ref[...], mlp_ref[:, :hidden]) + bias_ref[...]
        active, slope = gelu_pair(pre)
        active_ref[...] = active.astype(BF16)
        grad_hidden = (dot(grad_ref[...], mlp_ref[:, hidden : 2 * hidden]) * slope).astype(BF16)
        slope_ref[...] = grad_hidden
        back_ref[...] = dot_nt(grad_hidden, mlp_ref[:, :hidden]).astype(BF16)
        sums = jnp.sum(grad_hidden.astype(F32), axis=0, keepdims=True)

        @pl.when(pl.program_id(0) == 0)
        def _():
            sums_ref[...] = sums

        @pl.when(pl.program_id(0) > 0)
        def _():
            sums_ref[...] += sums

    return run(
        body,
        "mlp_turn",
        (count // Q_BLOCK,),
        (normed, grad, mlp, bias),
        [rows_spec(width), rows_spec(width), picked(mlp, 2 * hidden), fixed(bias)],
        [
            shaped((count, hidden), BF16),
            shaped((count, hidden), BF16),
            shaped((count, width), BF16),
            shaped((1, hidden), F32),
        ],
        [rows_spec(hidden), rows_spec(hidden), rows_spec(width), fixed(bias)],
        6 * count * width * hidden,
        pick=pick,
    )


def mlp_out(pick, active, mlp):
    count, hidden = active.shape
    width = mlp.shape[0]

    def body(_, active_ref, mlp_ref, out_ref):
        out_ref[...] = dot_nt(active_ref[...], mlp_ref[:, hidden : 2 * hidden]).astype(BF16)

    return run(
        body,
        "mlp_out",
        (count // Q_BLOCK,),
        (active, mlp),
        [rows_spec(hidden), picked(mlp, 2 * hidden)],
        shaped((count, width), BF16),
        rows_spec(width),
        2 * count * width * hidden,
        pick=pick,
    )


def weight_grads(lefts, rights, name):
    count, width = lefts[0].shape
    wides = [item.shape[1] for item in rights]
    tile = 384
    total = len(lefts)

    def body(*refs):
        out_ref = refs[-1]
        spot = 0
        for k in range(total):
            product = dot_tn(refs[k][...], refs[total + k][...])
            out_ref[:, spot : spot + wides[k]] = product.astype(BF16)
            spot += wides[k]

    return run(
        body,
        name,
        (width // tile,),
        (*lefts, *rights),
        [pl.BlockSpec((count, tile), lambda i, *_: (0, i))] * total + [fixed(item) for item in rights],
        shaped((width, sum(wides)), BF16),
        pl.BlockSpec((tile, sum(wides)), lambda i: (i, 0)),
        2 * count * width * sum(wides),
    )


def out_grads(pieces, branch):
    total = len(pieces)
    piece = pieces[0].shape[0]
    wide = branch.shape[1]

    def body(*refs):
        for k in range(total):
            product = dot(refs[k][...], refs[total][...])
            refs[-1][k * piece : (k + 1) * piece, :] = product.astype(BF16)

    operands = (*pieces, branch)
    out = shaped((total * piece, wide), BF16)
    return run(
        body,
        "out_grads",
        (1,),
        operands,
        [fixed(item) for item in operands],
        out,
        fixed(out),
        2 * branch.shape[0] * total * piece * wide,
    )


def project_back(pick, grad, weight, block, rows_all, width):
    count, wide = grad.shape

    def body(_, grad_ref, weight_ref, rows_ref, back_ref, norm_ref, bias_ref):
        back = dot_nt(grad_ref[...], weight_ref[:, :wide])
        back_ref[...] = back.astype(BF16)
        unit = centred(rows_ref[:, :width].astype(F32))[0]
        gain = jnp.sum(back * unit, axis=0, keepdims=True)
        shift = jnp.sum(back, axis=0, keepdims=True)
        bias = jnp.sum(grad_ref[...].astype(F32), axis=0, keepdims=True)

        @pl.when(pl.program_id(0) == 0)
        def _():
            norm_ref[...] = jnp.zeros_like(norm_ref)
            bias_ref[...] = jnp.zeros_like(bias_ref)

        norm_ref[0:1] += gain
        norm_ref[1:2] += shift
        bias_ref[...] += bias

    return run(
        body,
        "project_back",
        (count // Q_BLOCK,),
        (grad, weight, rows_all),
        [rows_spec(wide), picked(weight, block), rows_spec(rows_all.shape[1])],
        [shaped((count, width), BF16), shaped((2, width), F32), shaped((1, wide), F32)],
        [
            rows_spec(width),
            pl.BlockSpec((2, width), lambda *_: (0, 0)),
            pl.BlockSpec((1, wide), lambda *_: (0, 0)),
        ],
        2 * count * width * wide,
        pick=pick,
    )


class Native:
    def __init__(self, sizes, images, tokens):
        self.dev, self.zed, self.why = sizes
        self.images = images
        self.tokens = tokens
        self.team = self.dev * 2
        self.groups = self.zed * self.why
        self.each = images * self.dev // self.groups
        self.piece = tokens // self.dev
        self.rows = self.each * self.groups * self.piece

    def positions(self, row):
        place = row % self.piece
        group = (row // self.piece) % self.groups
        team = row // (self.piece * self.groups)
        owner = group * 2 + team % 2
        return owner * self.tokens + (team // 2) * self.piece + place

    def tokens_in(self, values):
        wide = values.shape[-1]
        split = values.reshape(self.images, self.dev, self.piece, wide)
        split = lax.all_to_all(split, "dev", 1, 0, tiled=True)
        split = split.reshape(self.groups, self.each, self.piece, wide)
        split = lax.all_to_all(split, ("z", "y"), 0, 0, tiled=True)
        return split.transpose(1, 0, 2, 3).reshape(self.rows, wide)

    def tokens_out(self, values):
        wide = values.shape[-1]
        split = values.reshape(self.each, self.groups, self.piece, wide).transpose(1, 0, 2, 3)
        split = lax.all_to_all(split, ("z", "y"), 0, 0, tiled=True)
        split = split.reshape(self.dev * self.images, 1, self.piece, wide)
        split = lax.all_to_all(split, "dev", 0, 1, tiled=True)
        return split.reshape(self.images, self.tokens, wide)

    def rows_gather(self, values, *gates):
        wide = values.shape[-1]
        whole = lax.all_gather(values, ("dev", "core"), axis=0, tiled=True)
        whole = whole.reshape(self.team, self.each, -1, wide).transpose(1, 0, 2, 3)
        return whole.reshape(self.team * self.rows, wide)

    def rows_scatter(self, values):
        wide = values.shape[-1]
        split = values.astype(BF16).reshape(self.each, self.team, -1, wide).transpose(1, 0, 2, 3)
        split = split.reshape(self.team * self.rows, wide)
        return lax.psum_scatter(
            split, ("dev", "core"), scatter_dimension=0, tiled=True
        ).astype(F32)

    def rows_near(self, values):
        return values, values

    def rows_end(self, sums):
        return self.rows_scatter(sums[0])

    def own_rows(self, values):
        wide = values.shape[-1]
        me = lax.axis_index(("dev", "core"))
        split = values.reshape(self.each, self.team, -1, wide)
        return lax.dynamic_slice_in_dim(split, me, 1, 1).reshape(self.rows, wide)

    def heads_gather(self, values):
        return [lax.all_gather(values, ("dev", "core"), axis=0, tiled=True)], [[0]]

    def weights(self, w_qkv, w_out, mlp, packed, *gates):
        whole = lax.all_gather(w_qkv, "dev", axis=1, tiled=True)
        rows, wide = whole.shape
        split = whole.reshape(rows, 3, self.team, wide // (3 * self.team))
        split = lax.dynamic_slice_in_dim(split, 2 * lax.axis_index("dev"), 2, 2)
        split = split.transpose(0, 2, 1, 3).reshape(rows, -1)
        split = lax.all_to_all(split, "core", 1, 0, tiled=True)
        full_qkv = lax.all_gather(split, ("z", "y"), axis=0, tiled=True)
        full_out = lax.all_gather(w_out, "dev", axis=1, tiled=True)
        full_out = lax.all_gather(full_out, ("z", "y", "core"), axis=0, tiled=True)
        mlp = jnp.concatenate(mlp, axis=1)
        mlp = lax.all_to_all(mlp, "core", 1, 0, tiled=True)
        mlp = lax.all_gather(mlp, ("z", "y"), axis=0, tiled=True)
        vectors = lax.all_gather(packed, "dev", axis=0, tiled=True)
        return full_qkv, full_qkv.shape[1], full_out, mlp, jnp.zeros((1,), jnp.int32), vectors

    def mlp_grads(self, grads):
        return lax.psum_scatter(grads, ("z", "y"), scatter_dimension=0, tiled=True)

    def mlp_halves(self, grads):
        grads = lax.all_to_all(grads, "core", 0, 1, tiled=True).astype(F32)
        half = grads.shape[1] // 2
        return grads[:, :half], grads[:, half:]

    def attention_grads(self, grad_qkv, grad_out, *gates):
        both = jnp.concatenate([grad_out, grad_qkv], axis=1)
        return lax.psum_scatter(both, ("z", "y"), scatter_dimension=0, tiled=True), both

    def attention_ends(self, both, block):
        out = lax.all_to_all(both[:, :block], "core", 0, 1, tiled=True)
        piece = lax.all_to_all(both[:, block:], "core", 0, 1, tiled=True)
        rows = piece.shape[0]
        piece = piece.reshape(rows, 2, 3, block).transpose(0, 2, 1, 3).reshape(rows, 3, 1, -1)
        whole = lax.all_gather(piece, "dev", axis=2, tiled=True)
        whole = whole.reshape(rows, self.dev, 6 * block)
        mine = lax.dynamic_slice_in_dim(whole, lax.axis_index("dev"), 1, 1)[:, 0]
        return mine.astype(F32), out.astype(F32)

    def total(self, values):
        return lax.psum(values, ("dev", "z", "y", "core"))


def joint(move):
    pairs = []
    for dev in range(2):
        for zed in range(4):
            for why in range(2):
                for core in range(2):
                    to = move(dev, zed, why, core)
                    source = ((dev * 4 + zed) * 2 + why) * 2 + core
                    pairs.append((source, ((to[0] * 4 + to[1]) * 2 + to[2]) * 2 + to[3]))
    return pairs


def send(values, move):
    return lax.ppermute(values, ("dev", "z", "y", "core"), joint(move))


def across(values):
    return send(values, lambda d, z, y, c: (1 - d, z, y, c))


def beside(values):
    return send(values, lambda d, z, y, c: (d, z, y, 1 - c))


class Paired(Native):
    def positions(self, row):
        place = row % self.tokens
        turn = (row // self.tokens) % 4
        team = row // (self.tokens * 4)
        zed = (lax.axis_index("z") - turn) % 4
        return ((zed * 2 + team // 2) * 2 + team % 2) * self.tokens + place

    def tokens_in(self, values):
        zed = lax.axis_index("z")
        pieces = []
        for turn in range(4):
            piece = lax.dynamic_slice_in_dim(values, (zed + turn) % 4, 1, 0)[0]
            pieces.append(send(piece, lambda d, z, y, c: (y, (z + turn) % 4, d, c)))
        return jnp.concatenate(pieces, axis=0)

    def tokens_out(self, values):
        zed = lax.axis_index("z")
        rows = self.tokens
        pieces = []
        for turn in range(4):
            piece = values[turn * rows : (turn + 1) * rows]
            pieces.append(send(piece, lambda d, z, y, c: (y, (z - turn) % 4, d, c)))
        order = (jnp.arange(4) - zed) % 4
        result = pieces[0][None]
        for turn in range(1, 4):
            result = jnp.where((order == turn)[:, None, None], pieces[turn][None], result)
        return result

    def rows_gather(self, values, *gates):
        me = lax.axis_index(("dev", "core"))
        rows, wide = values.shape
        mine = jnp.concatenate([values, after(across(values), *gates)], axis=0)
        whole = jnp.zeros((4 * rows, wide), values.dtype)
        for step, pair in enumerate((mine, beside(mine))):
            for far in range(2):
                piece = pair[far * rows : (far + 1) * rows]
                whole = lax.dynamic_update_slice(whole, piece, ((me ^ (step + 2 * far)) * rows, 0))
        return whole

    def rows_scatter(self, values):
        return self.rows_end(self.rows_near(values))

    def rows_near(self, values):
        rows = self.rows
        me = lax.axis_index(("dev", "core"))

        def part(step):
            return lax.dynamic_slice_in_dim(values, (me ^ step) * rows, rows, 0)

        near = jnp.concatenate([part(1), part(3)], axis=0)
        came = beside(near.astype(BF16))
        low, high = came[:rows].astype(F32), came[rows:].astype(F32)
        return part(0) + low, (part(2) + high).astype(BF16)

    def rows_end(self, sums):
        return sums[0] + across(sums[1]).astype(F32)

    def own_rows(self, values):
        me = lax.axis_index(("dev", "core"))
        return lax.dynamic_slice_in_dim(values, me * self.rows, self.rows, 0)

    def heads_gather(self, values):
        me = lax.axis_index(("dev", "core"))
        mine = jnp.concatenate([values, across(values)], axis=0)
        pieces = [mine, beside(mine)]
        block = values.shape[0]
        spots = [[(me ^ (step + 2 * far)) * block for far in range(2)] for step in range(2)]
        return pieces, spots

    def weights(self, w_qkv, w_out, mlp, packed, *gates):
        third = w_qkv.shape[1] // 3
        half = third // 2
        wide = w_out.shape[1]
        count = packed.shape[1]
        first = lax.axis_index("dev") == 0
        lines = -(-count // ((third + wide) * 8)) * 8
        sheet = jnp.pad(packed[0], (0, lines * (third + wide) - count)).reshape(lines, -1)
        message = jnp.concatenate([w_qkv[:, third : 2 * third], w_out], axis=1)
        came = across(jnp.concatenate([message, sheet], axis=0))
        rows = w_qkv.shape[0]
        vectors = came[rows:].reshape(1, -1)[:, :count]
        vectors = jnp.concatenate(
            [jnp.where(first, packed, vectors), jnp.where(first, vectors, packed)], axis=0
        )
        came_qkv, came_out = came[:rows, :third], came[:rows, third:]
        low, high = w_qkv[:, :third], w_qkv[:, 2 * third :]
        query = jnp.where(first, low, came_qkv)
        keys = jnp.where(first, high, low)
        values = jnp.where(first, came_qkv, high)
        blocks = [
            jnp.concatenate(
                [item[:, side * half : (side + 1) * half] for item in (query, keys, values)], axis=1
            )
            for side in range(2)
        ]
        block = -(-3 * half // 128) * 128
        blocks = [jnp.pad(item, ((0, 0), (0, block - 3 * half))) for item in blocks]
        everyone = ("z", "y", "core")
        outs = [jnp.where(first, w_out, came_out), jnp.where(first, came_out, w_out)]
        full_qkv = jnp.concatenate([*blocks, *outs], axis=1)
        full_qkv = lax.all_gather(full_qkv, everyone, axis=0, tiled=True)
        rest = after(jnp.concatenate(mlp, axis=1), full_qkv, *gates)
        rest = lax.all_gather(rest, everyone, axis=0, tiled=True)
        pick = lax.axis_index("core").reshape(1)
        return full_qkv, block, full_qkv[:, 2 * block :], rest, pick, vectors

    def turned(self):
        me = lax.axis_index(("dev", "core"))
        return [((k ^ me) % 2) * 2 + (k ^ me) // 2 for k in range(4)]

    def halve(self, block):
        upper = lax.axis_index("core") == 0
        rows = block.shape[0] // 2
        low, high = block[:rows], block[rows:]
        keep = jnp.where(upper, low, high)
        got = beside(jnp.where(upper, high, low).astype(BF16)).astype(F32)
        return jnp.where(upper, keep, got), jnp.where(upper, got, keep)

    def mlp_grads(self, grads):
        return lax.psum_scatter(grads, ("z", "y"), scatter_dimension=0, tiled=True)

    def mlp_halves(self, grads):
        return self.halve(grads.astype(F32))

    def attention_grads(self, grad_qkv, grad_out, *gates):
        block = grad_out.shape[1]
        rows = grad_qkv.shape[0] // 8
        order = grad_out.reshape(4, 2 * rows, block)
        order = jnp.stack([lax.dynamic_index_in_dim(order, k, 0, False) for k in self.turned()])
        both = jnp.concatenate([order.reshape(8 * rows, block), grad_qkv], axis=1)
        both = after(both, *gates)
        return lax.psum_scatter(both, ("z", "y"), scatter_dimension=0, tiled=True), both

    def attention_ends(self, both, block):
        first = lax.axis_index("dev") == 0
        left, right = self.halve(both.astype(F32))
        out = jnp.concatenate([left[:, :block], right[:, :block]], axis=1)
        query, keys, values = (
            jnp.concatenate([left[:, k * block : (k + 1) * block], right[:, k * block : (k + 1) * block]], axis=1)
            for k in (1, 2, 3)
        )
        came = across(jnp.where(first, values, query).astype(BF16)).astype(F32)
        return (
            jnp.concatenate(
                [jnp.where(first, query, keys), came, jnp.where(first, keys, values)], axis=1
            ),
            out,
        )

    def total(self, values):
        everyone = ("dev", "z", "y", "core")
        wide = values.shape[1]
        each = -(-wide // (32 * 128)) * 128
        parts = jnp.pad(values[0], (0, 32 * each - wide)).reshape(32, each)
        parts = lax.all_to_all(parts, everyone, 0, 0, tiled=True)
        mine = jnp.sum(parts, axis=0, keepdims=True)
        every = jnp.broadcast_to(mine, (32, each))
        return lax.all_to_all(every, everyone, 0, 0, tiled=True).reshape(1, -1)[:, :wide]


def norm_back(grad, unit, inverse, gain):
    scaled = grad * gain
    mean = jnp.mean(scaled, axis=-1, keepdims=True)
    along = jnp.mean(scaled * unit, axis=-1, keepdims=True)
    return (scaled - mean - unit * along) * inverse


def gelu_pair(hidden):
    root = 0.7978845608028654
    inner = jnp.tanh(root * (hidden + 0.044715 * hidden * hidden * hidden))
    half = 0.5 * (1.0 + inner)
    slope = half + 0.5 * hidden * (1.0 - inner * inner) * root * (
        1.0 + 3 * 0.044715 * hidden * hidden
    )
    return hidden * half, slope


def per_device(
    sizes,
    patches,
    patch_mask,
    cotangent,
    w_qkv,
    w_out,
    w_up,
    w_down,
    *vectors,
):
    images, tokens, width = patches.shape
    paired = sizes == (2, 4, 2) and images == 4 and Paired is not Native
    route = (Paired if paired else Native)(sizes, images, tokens)
    dev_count = sizes[0]
    team = route.team
    dev = lax.axis_index("dev")
    me = lax.axis_index(("dev", "core"))
    head_count = HEADS // team
    block = head_count * HEAD_DIM
    hidden = w_up.shape[1] // 2

    padded = -(-hidden // 128) * 128
    sides = [
        jnp.concatenate(
            [
                jnp.pad(item[:, side * hidden : (side + 1) * hidden], ((0, 0), (0, padded - hidden)))
                for item in (w_up, w_down)
            ],
            axis=1,
        )
        for side in range(2)
    ]
    marks = jnp.broadcast_to(patch_mask.astype(BF16)[:, :, None], (images, tokens, 128))
    own_in = route.tokens_in(jnp.concatenate([patches, marks, cotangent], axis=2))
    packed = jnp.concatenate(vectors, axis=1)
    own_qkv, qkv_block, full_out, mlp, pick, halves = route.weights(
        w_qkv, w_out, sides, packed, own_in
    )
    own_in, own_grad = own_in[:, : width + 128], own_in[:, width + 128 :]
    rows_all = route.rows_gather(own_in)
    halves = halves.astype(F32)
    full = []
    spot = 0
    for item in vectors:
        full.append(halves[:, spot : spot + item.shape[1]].reshape(1, -1))
        spot += item.shape[1]
    gain_one, shift_one, gain_two, shift_two = full[:4]
    bias_query, bias_value, bias_out, bias_up, bias_down = full[4:]

    qkv_bias = jnp.concatenate(
        [
            lax.dynamic_slice_in_dim(bias_query, me * block, block, 1),
            jnp.zeros((1, block), F32),
            lax.dynamic_slice_in_dim(bias_value, me * block, block, 1),
        ],
        axis=1,
    )
    normed_one, projected = project(
        pick, rows_all, gain_one, shift_one, own_qkv, qkv_block, qkv_bias
    )
    rows_grad = route.rows_gather(after(own_grad, projected))
    seq = projected.shape[0] // route.each
    projected = projected.reshape(route.each, seq, 3 * block)
    marks = rows_all[:, width : width + 1].astype(F32).reshape(route.each, seq, 1)
    length = jnp.sum(marks, axis=1, keepdims=True)
    spot = route.positions(lax.broadcasted_iota(jnp.int32, (route.each, seq, 1), 1))
    mask_bias = jnp.where(spot.astype(F32) < length, 0.0, -1e30).astype(F32)

    attended, lse = attend_fwd(projected, mask_bias, head_count)
    pieces, spots = route.heads_gather(attended.transpose(1, 0, 2).reshape(block, -1))

    def by_piece(whole):
        size = pieces[0].shape[0] // len(spots[0])
        return jnp.stack(
            [
                jnp.concatenate([lax.dynamic_slice_in_dim(whole, at, size, 0) for at in group])
                for group in spots
            ]
        )

    middle, normed_two = attend_out(
        pieces, by_piece(full_out), rows_all, bias_out, gain_two, shift_two
    )
    up_bias = lax.dynamic_slice_in_dim(bias_up, me * hidden, hidden, 1)
    up_bias = jnp.pad(up_bias, ((0, 0), (0, padded - hidden)))

    active, grad_hidden, grad_part_two, up_sums = mlp_turn(
        pick, normed_two, rows_grad, mlp, up_bias
    )
    near_two = route.rows_near(grad_part_two)
    grad_mlp = weight_grads(
        [rows_grad, normed_two], [active, grad_hidden], "mlp_grads"
    )
    sum_mlp = route.mlp_grads(grad_mlp)
    grad_normed_two = after(route.rows_end(near_two), grad_mlp)
    own_middle = route.own_rows(middle)
    own_unit_two, own_inverse_two = centred(own_middle)
    grad_middle = own_grad.astype(F32) + norm_back(
        grad_normed_two, own_unit_two, own_inverse_two, gain_two
    )
    own_branch = grad_middle.astype(BF16)
    mlp_part = mlp_out(pick, after(active, own_branch), mlp)
    grad_branch = route.rows_gather(own_branch, mlp_part)

    grad_projected = attend_bwd(
        projected,
        mask_bias,
        lse,
        grad_branch.reshape(route.each, seq, width),
        lax.dynamic_slice_in_dim(full_out, me * block, block, 0),
        head_count,
    ).reshape(-1, 3 * block)
    my_branch = lax.dynamic_slice_in_dim(after(grad_branch, grad_projected), me * block, block, 1)
    grad_out = out_grads(pieces, my_branch)
    grad_qkv = weight_grads([normed_one], [grad_projected], "qkv_grads")
    sums_out, sent = route.attention_grads(grad_qkv, grad_out, sum_mlp)
    grad_projected = after(grad_projected, grad_qkv, grad_out)

    grad_part_one, norm_sums, proj_sums = project_back(
        pick, grad_projected, own_qkv, qkv_block, rows_all, width
    )
    near_one = route.rows_near(grad_part_one)
    grad_normed_one = route.rows_end(near_one)
    mlp_near = route.rows_near(after(mlp_part, near_one[1]))
    result = (own_middle + route.rows_end(mlp_near) + bias_down).astype(BF16)
    result = route.tokens_out(result)

    own_unit_one, own_inverse_one = centred(
        route.own_rows(after(rows_all, near_one[1]))[:, :width].astype(F32)
    )
    grad_inputs = grad_middle + norm_back(
        grad_normed_one, own_unit_one, own_inverse_one, gain_one
    )
    grad_inputs = after(grad_inputs.astype(BF16), sent)
    grad_patches = route.tokens_out(grad_inputs)

    out_qkv, out_out = route.attention_ends(sums_out, block)
    out_mlp = route.mlp_halves(sum_mlp)
    out_down, out_up = (
        jnp.concatenate([side[:, spot : spot + hidden] for side in out_mlp], axis=1)
        for spot in (0, padded)
    )

    def spread(values, size):
        return lax.dynamic_update_slice(
            jnp.zeros((size,), F32), values, (me * values.shape[0],)
        )

    norm_sums, proj_sums, up_sums = (
        after(item, grad_inputs) for item in (norm_sums, proj_sums, up_sums)
    )
    sums = [
        norm_sums[0],
        norm_sums[1],
        jnp.sum(grad_normed_two * own_unit_two, axis=0),
        jnp.sum(grad_normed_two, axis=0),
        spread(proj_sums[0, :block], width),
        spread(proj_sums[0, 2 * block :], width),
        jnp.sum(own_branch.astype(F32), axis=0),
        spread(up_sums[0, :hidden], hidden * team),
        jnp.sum(after(cotangent, grad_inputs).astype(F32), axis=(0, 1)),
    ]
    flat = route.total(after(jnp.concatenate(sums)[None], grad_inputs))
    out_vectors = []
    spot = 0
    for item in sums:
        size = item.shape[0]
        half = size // dev_count
        out_vectors.append(lax.dynamic_slice(flat, (0, spot + dev * half), (1, half)))
        spot += size
    return (result, grad_patches, out_qkv, out_out, out_up, out_down, *out_vectors)


def solution(mesh):
    dev_count, sa_count = mesh.devices.shape

    def whole(*args):
        zed = args[0].shape[0] // dev_count
        why = sa_count // (2 * zed)
        sizes = (dev_count, zed, why)
        inner = Mesh(mesh.devices.reshape(dev_count, zed, why, 2), ("dev", "z", "y", "core"))
        rows = ("z", "y", "core")
        token = P("dev", rows, None)
        weight = P(rows, "dev")
        vector = P(None, "dev")
        return jax.shard_map(
            functools.partial(per_device, sizes),
            mesh=inner,
            in_specs=(token, P("dev", rows), token) + (weight,) * 4 + (vector,) * 9,
            out_specs=(token, token) + (weight,) * 4 + (vector,) * 9,
            check_vma=False,
        )(*args)

    return whole
```

profile of v0, /device:TPU:0, one launch (start us, length us, event | category | flops | bytes accessed | tf_op | source)
XLA Modules:
  0.0 446.7 jit_solution(803322838670391162)
XLA Ops:
  10.3 3.0 collective-permute-start.6
  13.3 4.6 %collective-permute-done.6 = bf16[80,1152]{1,0:T(8,128)(2,1)S(1)} collective-permute-done((bf16[80,1152]{1,0:T(8,128)(2,1)S(1)}, bf16[80,1152]{1,0:T(8,128)(2,1)S(1)}, u32[]{:S(2)}, u32[]{:S(2)}) %collective-permute-start.6) | collective-permute-done | bytes 184352 | tf_op jit(solution)/shard_map/ppermute | solution.py:508
  21.9 1.9 collective-permute-start.1
  23.8 2.6 collective-permute-start.2
  29.0 5.2 %collective-permute-done.1 = bf16[64,2432]{1,0:T(8,128)(2,1)S(1)} collective-permute-done((bf16[64,2432]{1,0:T(8,128)(2,1)S(1)}, bf16[64,2432]{1,0:T(8,128)(2,1)S(1)}, u32[]{:S(2)}, u32[]{:S(2)}) %collective-permute-start.1) | collective-permute-done | bytes 311328 | tf_op jit(solution)/shard_map/ppermute | solution.py:508
  34.3 22.9 %collective-permute-done.2 = bf16[64,2432]{1,0:T(8,128)(2,1)S(1)} collective-permute-done((bf16[64,2432]{1,0:T(8,128)(2,1)S(1)}, bf16[64,2432]{1,0:T(8,128)(2,1)S(1)}, u32[]{:S(2)}, u32[]{:S(2)}) %collective-permute-start.2) | collective-permute-done | bytes 311328 | tf_op jit(solution)/shard_map/ppermute | solution.py:508
  57.4 48.4 %all-gather.3.cloned.1.call-done.weight_ref = bf16[1152,2944]{1,0:T(8,128)(2,1)} async-done(((bf16[72,2944]{1,0:T(8,128)(2,1)}), bf16[1152,2944]{1,0:T(8,128)(2,1)}) %all-gather.3.cloned.1.call-update) | async-done | bytes 6782992 | tf_op jit(solution)/shard_map/all_gather | solution.py:620
  105.8 1.8 broadcast_in_dim.135
  110.9 14.5 %collective-permute-done.4 = bf16[256,1280]{1,0:T(8,128)(2,1)S(1)} collective-permute-done((bf16[256,1280]{1,0:T(8,128)(2,1)S(1)}, bf16[256,1280]{1,0:T(8,128)(2,1)S(1)}, u32[]{:S(2)}, u32[]{:S(2)}) %collective-permute-start.4) | collective-permute-done | bytes 655392 | tf_op jit(solution)/shard_map/ppermute | solution.py:508
  135.8 6.8 %project.1 = (bf16[1024,1152]{1,0:T(8,128)(2,1)}, bf16[1024,864]{1,0:T(8,128)(2,1)S(1)}) custom-call(s32[1]{0:T(128)} %bitcast._, bf16[1024,1280]{1,0:T(8,128)(2,1)} %slice_dynamic-update-slice_fusion.rows_ref.refs_3_, f32[1,1152]{1,0:T(1,128)S(1)} %reshape.509.gain_ref, f32[1,1152]{1,0:T(1,128)S(1)} %reshape.510.shift_ref, ...), custom_call_target="tpu_custom_call" | custom-call | flops 2038431744 | bytes 9417088 | tf_op jit(solution)/shard_map/project/pallas_call | solution.py:104
  142.6 12.4 %attend_fwd.1 = (bf16[1,288,1024]{2,1,0:T(8,128)(2,1)S(1)}, f32[1,8,1024]{2,1,0:T(8,128)S(1)}) custom-call(bf16[1,1024,864]{2,1,0:T(8,128)(2,1)S(1)} %bitcast.30, f32[1,1024,1]{2,1,0:T(8,128)S(1)} %fusion.42.bias_ref), custom_call_target="tpu_custom_call" | custom-call | flops 2147483648 | bytes 1773568 | tf_op jit(solution)/shard_map/attend_fwd/pallas_call | solution.py:104
  157.2 1.7 slice-done
  159.2 12.0 %collective-permute-done.7 = bf16[288,1024]{1,0:T(8,128)(2,1)S(1)} collective-permute-done((bf16[288,1024]{1,0:T(8,128)(2,1)S(1)}, bf16[288,1024]{1,0:T(8,128)(2,1)S(1)}, u32[]{:S(2)}, u32[]{:S(2)}) %collective-permute-start.7) | collective-permute-done | bytes 589856 | tf_op jit(solution)/shard_map/ppermute | solution.py:508
  171.4 12.1 %collective-permute-done.9 = bf16[256,1152]{1,0:T(8,128)(2,1)S(1)} collective-permute-done((bf16[256,1152]{1,0:T(8,128)(2,1)S(1)}, bf16[256,1152]{1,0:T(8,128)(2,1)S(1)}, u32[]{:S(2)}, u32[]{:S(2)}) %collective-permute-start.9) | collective-permute-done | bytes 589856 | tf_op jit(solution)/shard_map/ppermute | solution.py:508
  184.1 1.7 pad_maximum_fusion.refs_2_
  185.9 9.9 %attend_out.1 = (f32[1024,1152]{1,0:T(8,128)}, bf16[1024,1152]{1,0:T(8,128)(2,1)}) custom-call(bf16[576,1024]{1,0:T(8,128)(2,1)S(1)} %pad_maximum_fusion.4.refs_0_, bf16[576,1024]{1,0:T(8,128)(2,1)S(1)} %collective-permute-done.8.refs_1_, bf16[2,576,1152]{2,1,0:T(8,128)(2,1)} %pad_maximum_fusion.refs_2_, ...), custom_call_target="tpu_custom_call" | custom-call | flops 2717908992 | bytes 7648768 | tf_op jit(solution)/shard_map/attend_out/pallas_call | solution.py:104
  197.3 15.0 %mlp_turn.1 = (bf16[1024,1152]{1,0:T(8,128)(2,1)S(1)}, bf16[1024,1152]{1,0:T(8,128)(2,1)}, bf16[1024,1152]{1,0:T(8,128)(2,1)}, f32[1,1152]{1,0:T(1,128)S(1)}) custom-call(s32[1]{0:T(128)} %bitcast._, bf16[1024,1152]{1,0:T(8,128)(2,1)} %get-tuple-element.47.normed_ref.refs_1_, bf16[1024,1152]{1,0:T(8,128)(2,1)} %copy-done.4, ...), custom_call_target="tpu_custom_call" | custom-call | flops 8153726976 | bytes 15340032 | tf_op jit(solution)/shard_map/mlp_turn/pallas_call | solution.py:104
  212.3 2.2 constant_dynamic-slice_fusion.19
  219.0 2.0 add_convert_fusion.3
  223.1 10.8 %mlp_grads.1 = bf16[1152,2304]{1,0:T(8,128)(2,1)} custom-call(bf16[1024,1152]{1,0:T(8,128)(2,1)S(1)} %copy-done.5, bf16[1024,1152]{1,0:T(8,128)(2,1)} %get-tuple-element.47.normed_ref.refs_1_, bf16[1024,1152]{1,0:T(8,128)(2,1)} %copy-done.6, bf16[1024,1152]{1,0:T(8,128)(2,1)} %get-tuple-element.52.refs_3_), custom_call_target="tpu_custom_call" | custom-call | flops 5435817984 | bytes 9437184 | tf_op jit(solution)/shard_map/mlp_grads/pallas_call | solution.py:104
  234.2 2.8 collective-permute-done.12
  236.9 2.0 multiply_reduce_fusion.2
  239.0 2.5 multiply_reduce_fusion
  241.4 3.5 convert_reduce_fusion.2
  246.5 7.0 %mlp_out.1 = bf16[1024,1152]{1,0:T(8,128)(2,1)S(1)} custom-call(s32[1]{0:T(128)} %bitcast._, bf16[1024,1152]{1,0:T(8,128)(2,1)} %copy-done.6, bf16[1152,4608]{1,0:T(8,128)(2,1)} %all-gather.5.cloned.1.call-done.mlp_ref), custom_call_target="tpu_custom_call" | custom-call | flops 2717908992 | bytes 12976128 | tf_op jit(solution)/shard_map/mlp_out/pallas_call | solution.py:104
  253.5 6.6 %collective-permute-done.13 = bf16[256,1152]{1,0:T(8,128)(2,1)S(1)} collective-permute-done((bf16[256,1152]{1,0:T(8,128)(2,1)S(1)}, bf16[256,1152]{1,0:T(8,128)(2,1)S(1)}, u32[]{:S(2)}, u32[]{:S(2)}) %collective-permute-start.13) | collective-permute-done | bytes 589856 | tf_op jit(solution)/shard_map/ppermute | solution.py:508
  260.6 2.5 collective-permute-done.14
  264.6 23.0 %attend_bwd.1 = bf16[1,1024,864]{2,1,0:T(8,128)(2,1)S(1)} custom-call(bf16[1,1024,864]{2,1,0:T(8,128)(2,1)} %bitcast.31, f32[1,1024,1]{2,1,0:T(8,128)S(1)} %copy-done.12, f32[1,8,1024]{2,1,0:T(8,128)S(1)} %copy-done.17, bf16[1,1024,1152]{2,1,0:T(8,128)(2,1)} %bitcast.32, bf16[288,1152]{1,0:T(8,128)(2,1)S(1)} %copy-done.3), custom_call_target="tpu_custom_call" | custom-call | flops 5368709120 | bytes 4829184 | tf_op jit(solution)/shard_map/attend_bwd/pallas_call | solution.py:104
  291.6 4.3 qkv_grads.1
  297.3 7.3 %project_back.1 = (bf16[1024,1152]{1,0:T(8,128)(2,1)}, f32[2,1152]{1,0:T(2,128)S(1)}, f32[1,864]{1,0:T(1,128)S(1)}) custom-call(s32[1]{0:T(128)} %bitcast._, bf16[1024,864]{1,0:T(8,128)(2,1)S(1)} %bitcast.27, bf16[1152,2944]{1,0:T(8,128)(2,1)} %all-gather.3.cloned.1.call-done.weight_ref, bf16[1024,1280]{1,0:T(8,128)(2,1)} %slice_dynamic-update-slice_fusion.rows_ref.refs_3_), custom_call_target="tpu_custom_call" | custom-call | flops 2038431744 | bytes 11173888 | tf_op jit(solution)/shard_map/project_back/pallas_call | solution.py:104
  310.3 2.5 add_convert_fusion.2
  314.9 2.6 pad_maximum_fusion.1
  321.4 11.7 %collective-permute-done.22 = bf16[256,1152]{1,0:T(8,128)(2,1)S(1)} collective-permute-done((bf16[256,1152]{1,0:T(8,128)(2,1)}, bf16[256,1152]{1,0:T(8,128)(2,1)S(1)}, u32[]{:S(2)}, u32[]{:S(2)}) %collective-permute-start.22) | collective-permute-done | bytes 589856 | tf_op jit(solution)/shard_map/ppermute | solution.py:508
  333.1 2.0 fusion.59
  335.1 2.1 add_convert_fusion.1
  338.4 2.0 fusion.11
  340.5 11.5 %collective-permute-done.17 = bf16[256,1152]{1,0:T(8,128)(2,1)} collective-permute-done((bf16[256,1152]{1,0:T(8,128)(2,1)}, bf16[256,1152]{1,0:T(8,128)(2,1)}, u32[]{:S(2)}, u32[]{:S(2)}) %collective-permute-start.17) | collective-permute-done | bytes 589856 | tf_op jit(solution)/shard_map/ppermute | solution.py:508
  352.1 1.9 add_convert_fusion
  354.8 1.7 collective-permute-start.21
  364.4 10.5 %all-to-all-start = ((f32[32,1,512]{2,1,0:T(1,128)}), f32[32,1,512]{2,1,0:T(1,128)S(1)}, u32[]{:S(2)}, u32[]{:S(2)}) async-start(f32[32,1,512]{2,1,0:T(1,128)} %bitcast.13), calls=%async_computation.2 | async-start | bytes 131072 | tf_op jit(solution)/shard_map/all_to_all | solution.py:674
  375.1 3.7 collective-permute-start.25
  378.7 6.8 %collective-permute-done.19 = bf16[64,1152]{1,0:T(8,128)(2,1)S(1)} collective-permute-done((bf16[64,1152]{1,0:T(8,128)(2,1)}, bf16[64,1152]{1,0:T(8,128)(2,1)S(1)}, u32[]{:S(2)}, u32[]{:S(2)}) %collective-permute-start.19) | collective-permute-done | bytes 147488 | tf_op jit(solution)/shard_map/ppermute | solution.py:508
  385.6 2.2 all-to-all-done
  388.5 9.6 %all-to-all-start.1 = ((f32[32,1,512]{2,1,0:T(1,128)}), f32[32,1,512]{2,1,0:T(1,128)S(1)}, u32[]{:S(2)}, u32[]{:S(2)}) async-start(f32[32,1,512]{2,1,0:T(1,128)} %broadcast_in_dim.152), calls=%async_computation.3 | async-start | bytes 131072 | tf_op jit(solution)/shard_map/all_to_all | solution.py:677
  398.9 2.3 select_select_fusion
  401.2 4.3 all-to-all-done.1
  408.1 22.9 %reduce-scatter.5.cloned.1.call-done = bf16[144,1152]{1,0:T(8,128)(2,1)} async-done(((bf16[1152,1152]{1,0:T(8,128)(2,1)}), bf16[144,1152]{1,0:T(8,128)(2,1)}) %reduce-scatter.5.cloned.1.call-update) | async-done | bytes 331792 | tf_op jit(solution)/shard_map/reduce_scatter | solution.py:651
  436.2 2.6 collective-permute-done.28
  (273 shorter events, 75.4 us)
Async XLA Ops:
  7.2 98.6 %all-gather.3.cloned.1.call-start = ((), (), s32[]{:S(2)}) async-start(), calls=%async_computation.4 | async-start | bytes 7206912 | tf_op jit(solution)/shard_map/all_gather | solution.py:620
  10.3 7.6 %collective-permute-start.6 = (bf16[80,1152]{1,0:T(8,128)(2,1)S(1)}, bf16[80,1152]{1,0:T(8,128)(2,1)S(1)}, u32[]{:S(2)}, u32[]{:S(2)}) collective-permute-start(bf16[80,1152]{1,0:T(8,128)(2,1)S(1)} %fusion.49), channel_id=1, source_target_pairs={{0,16},{1,17},{2,18},{3,19},{4,20},{5,21},{6,22},{7,23},{8,24},{9,... | collective-permute-start | bytes 552968 | tf_op jit(solution)/shard_map/ppermute | solution.py:508
  20.6 175.4 %all-gather.5.cloned.1.call-start = ((), (), s32[]{:S(2)}) async-start(), calls=%async_computation.5 | async-start | bytes 11280384 | tf_op jit(solution)/shard_map/all_gather | solution.py:622
  21.1 7.9 %collective-permute-start = (bf16[64,2432]{1,0:T(8,128)(2,1)S(1)}, bf16[64,2432]{1,0:T(8,128)(2,1)S(1)}, u32[]{:S(2)}, u32[]{:S(2)}) collective-permute-start(bf16[64,2432]{1,0:T(8,128)(2,1)S(1)} %get-tuple-element.103), channel_id=1, source_target_pairs={{0,0},{1,1},{2,16},{3,17},{4,4},{5,5},{6,20},{7,21},{8,8},{9,9},{1... | collective-permute-start | bytes 933896 | tf_op jit(solution)/shard_map/ppermute | solution.py:508
  21.9 12.3 %collective-permute-start.1 = (bf16[64,2432]{1,0:T(8,128)(2,1)S(1)}, bf16[64,2432]{1,0:T(8,128)(2,1)S(1)}, u32[]{:S(2)}, u32[]{:S(2)}) collective-permute-start(bf16[64,2432]{1,0:T(8,128)(2,1)S(1)} %get-tuple-element.102), channel_id=1, source_target_pairs={{0,4},{1,5},{2,20},{3,21},{4,8},{5,9},{6,24},{7,25},{8,12},{9,13},... | collective-permute-start | bytes 933896 | tf_op jit(solution)/shard_map/ppermute | solution.py:508
  23.8 33.4 %collective-permute-start.2 = (bf16[64,2432]{1,0:T(8,128)(2,1)S(1)}, bf16[64,2432]{1,0:T(8,128)(2,1)S(1)}, u32[]{:S(2)}, u32[]{:S(2)}) collective-permute-start(bf16[64,2432]{1,0:T(8,128)(2,1)S(1)} %get-tuple-element.101), channel_id=1, source_target_pairs={{0,8},{1,9},{2,24},{3,25},{4,12},{5,13},{6,28},{7,29},{8,0},{9,1},... | collective-permute-start | bytes 933896 | tf_op jit(solution)/shard_map/ppermute | solution.py:508
  26.4 30.9 %collective-permute-start.3 = (bf16[64,2432]{1,0:T(8,128)(2,1)S(1)}, bf16[64,2432]{1,0:T(8,128)(2,1)S(1)}, u32[]{:S(2)}, u32[]{:S(2)}) collective-permute-start(bf16[64,2432]{1,0:T(8,128)(2,1)S(1)} %get-tuple-element.100), channel_id=1, source_target_pairs={{0,12},{1,13},{2,28},{3,29},{4,0},{5,1},{6,16},{7,17},{8,4},{9,5},... | collective-permute-start | bytes 933896 | tf_op jit(solution)/shard_map/ppermute | solution.py:508
  57.3 72.9 %copy-start.20 = (bf16[256,2432]{1,0:T(8,128)(2,1)}, bf16[256,2432]{1,0:T(8,128)(2,1)S(1)}, u32[]{:S(2)}) copy-start(bf16[256,2432]{1,0:T(8,128)(2,1)S(1)} %constant_dynamic-update-slice_fusion.6) | copy-start | bytes 3735556
  105.8 234.7 %reduce-scatter.3.cloned.1.call-start = ((), (), s32[]{:S(2)}) async-start(), calls=%async_computation.6 | async-start | bytes 5971968 | tf_op jit(solution)/shard_map/reduce_scatter | solution.py:639
  108.5 16.9 %collective-permute-start.4 = (bf16[256,1280]{1,0:T(8,128)(2,1)S(1)}, bf16[256,1280]{1,0:T(8,128)(2,1)S(1)}, u32[]{:S(2)}, u32[]{:S(2)}) collective-permute-start(bf16[256,1280]{1,0:T(8,128)(2,1)S(1)} %get-tuple-element.98), channel_id=1, source_target_pairs={{0,16},{1,17},{2,18},{3,19},{4,20},{5,21},{6,22},{7,23},{8,24},{9,... | collective-permute-start | bytes 1966088 | tf_op jit(solution)/shard_map/ppermute | solution.py:508
  126.6 4.6 %collective-permute-start.5 = (bf16[512,1280]{1,0:T(8,128)(2,1)}, bf16[512,1280]{1,0:T(8,128)(2,1)S(1)}, u32[]{:S(2)}, u32[]{:S(2)}) collective-permute-start(bf16[512,1280]{1,0:T(8,128)(2,1)} %pad_maximum_fusion.2), channel_id=1, source_target_pairs={{0,1},{1,0},{2,3},{3,2},{4,5},{5,4},{6,7},{7,6},{8,9},{9,8},{10,11... | collective-permute-start | bytes 3932168 | tf_op jit(solution)/shard_map/ppermute | solution.py:508
  142.6 12.4 %copy-start.15 = (bf16[1024,864]{1,0:T(8,128)(2,1)}, bf16[1024,864]{1,0:T(8,128)(2,1)S(1)}, u32[]{:S(2)}) copy-start(bf16[1024,864]{1,0:T(8,128)(2,1)S(1)} %get-tuple-element.44) | copy-start | bytes 5308420
  155.1 16.2 %collective-permute-start.7 = (bf16[288,1024]{1,0:T(8,128)(2,1)S(1)}, bf16[288,1024]{1,0:T(8,128)(2,1)S(1)}, u32[]{:S(2)}, u32[]{:S(2)}) collective-permute-start(bf16[288,1024]{1,0:T(8,128)(2,1)S(1)} %bitcast.28), channel_id=1, source_target_pairs={{0,16},{1,17},{2,18},{3,19},{4,20},{5,21},{6,22},{7,23},{8,24},{9,... | collective-permute-start | bytes 1769480 | tf_op jit(solution)/shard_map/ppermute | solution.py:508
  156.5 27.0 %collective-permute-start.9 = (bf16[256,1152]{1,0:T(8,128)(2,1)S(1)}, bf16[256,1152]{1,0:T(8,128)(2,1)S(1)}, u32[]{:S(2)}, u32[]{:S(2)}) collective-permute-start(bf16[256,1152]{1,0:T(8,128)(2,1)S(1)} %slice.309), channel_id=1, source_target_pairs={{0,16},{1,17},{2,18},{3,19},{4,20},{5,21},{6,22},{7,23},{8,24},{9,... | collective-permute-start | bytes 1769480 | tf_op jit(solution)/shard_map/ppermute | solution.py:508
  159.1 24.8 %copy-start.2 = (bf16[288,1152]{1,0:T(8,128)(2,1)}, bf16[288,1152]{1,0:T(8,128)(2,1)S(1)}, u32[]{:S(2)}) copy-start(bf16[288,1152]{1,0:T(8,128)(2,1)S(1)} %get-tuple-element.86.w_ref) | copy-start | bytes 1990660
  171.3 14.6 %collective-permute-start.8 = (bf16[576,1024]{1,0:T(8,128)(2,1)S(1)}, bf16[576,1024]{1,0:T(8,128)(2,1)S(1)}, u32[]{:S(2)}, u32[]{:S(2)}) collective-permute-start(bf16[576,1024]{1,0:T(8,128)(2,1)S(1)} %pad_maximum_fusion.4.refs_0_), channel_id=1, source_target_pairs={{0,1},{1,0},{2,3},{3,2},{4,5},{5,4},{6,7},{7,6},{8,9},{9,8},{10,11... | collective-permute-start | bytes 3538952 | tf_op jit(solution)/shard_map/ppermute | solution.py:508
  183.6 12.2 %collective-permute-start.10 = (bf16[512,1152]{1,0:T(8,128)(2,1)S(1)}, bf16[512,1152]{1,0:T(8,128)(2,1)S(1)}, u32[]{:S(2)}, u32[]{:S(2)}) collective-permute-start(bf16[512,1152]{1,0:T(8,128)(2,1)S(1)} %pad_maximum_fusion.5), channel_id=1, source_target_pairs={{0,1},{1,0},{2,3},{3,2},{4,5},{5,4},{6,7},{7,6},{8,9},{9,8},{10,11... | collective-permute-start | bytes 3538952 | tf_op jit(solution)/shard_map/ppermute | solution.py:508
  185.9 9.9 %copy-start.9 = (bf16[576,1024]{1,0:T(8,128)(2,1)}, bf16[576,1024]{1,0:T(8,128)(2,1)S(1)}, u32[]{:S(2)}) copy-start(bf16[576,1024]{1,0:T(8,128)(2,1)S(1)} %collective-permute-done.8.refs_1_) | copy-start | bytes 3538948
  215.7 3.3 collective-permute-start.11
  221.0 15.9 %collective-permute-start.12 = (bf16[256,1152]{1,0:T(8,128)(2,1)}, bf16[256,1152]{1,0:T(8,128)(2,1)}, u32[]{:S(2)}, u32[]{:S(2)}) collective-permute-start(bf16[256,1152]{1,0:T(8,128)(2,1)} %add_convert_fusion.3), channel_id=1, source_target_pairs={{0,16},{1,17},{2,18},{3,19},{4,20},{5,21},{6,22},{7,23},{8,24},{9,... | collective-permute-start | bytes 1769480 | tf_op jit(solution)/shard_map/ppermute | solution.py:508
  233.9 197.1 %reduce-scatter.5.cloned.1.call-start = ((), (), s32[]{:S(2)}) async-start(), calls=%async_computation.7 | async-start | bytes 2985984 | tf_op jit(solution)/shard_map/reduce_scatter | solution.py:651
  245.0 15.1 %collective-permute-start.13 = (bf16[256,1152]{1,0:T(8,128)(2,1)S(1)}, bf16[256,1152]{1,0:T(8,128)(2,1)S(1)}, u32[]{:S(2)}, u32[]{:S(2)}) collective-permute-start(bf16[256,1152]{1,0:T(8,128)(2,1)S(1)} %get-tuple-element.84), channel_id=1, source_target_pairs={{0,16},{1,17},{2,18},{3,19},{4,20},{5,21},{6,22},{7,23},{8,24},{9,... | collective-permute-start | bytes 1769480 | tf_op jit(solution)/shard_map/ppermute | solution.py:508
  260.2 2.9 collective-permute-start.14
  307.1 3.2 collective-permute-start.15
  314.1 21.0 %collective-permute-start.16 = (bf16[512,1152]{1,0:T(8,128)(2,1)}, bf16[512,1152]{1,0:T(8,128)(2,1)}, u32[]{:S(2)}, u32[]{:S(2)}) collective-permute-start(bf16[512,1152]{1,0:T(8,128)(2,1)} %pad_maximum_fusion.9), channel_id=1, source_target_pairs={{0,1},{1,0},{2,3},{3,2},{4,5},{5,4},{6,7},{7,6},{8,9},{9,8},{10,11... | collective-permute-start | bytes 3538952 | tf_op jit(solution)/shard_map/ppermute | solution.py:508
  317.5 15.5 %collective-permute-start.22 = (bf16[256,1152]{1,0:T(8,128)(2,1)}, bf16[256,1152]{1,0:T(8,128)(2,1)S(1)}, u32[]{:S(2)}, u32[]{:S(2)}) collective-permute-start(bf16[256,1152]{1,0:T(8,128)(2,1)} %add_convert_fusion.2), channel_id=1, source_target_pairs={{0,16},{1,17},{2,18},{3,19},{4,20},{5,21},{6,22},{7,23},{8,24},{9,... | collective-permute-start | bytes 1769480 | tf_op jit(solution)/shard_map/ppermute | solution.py:508
  337.2 14.9 %collective-permute-start.17 = (bf16[256,1152]{1,0:T(8,128)(2,1)}, bf16[256,1152]{1,0:T(8,128)(2,1)}, u32[]{:S(2)}, u32[]{:S(2)}) collective-permute-start(bf16[256,1152]{1,0:T(8,128)(2,1)} %add_convert_fusion.1), channel_id=1, source_target_pairs={{0,16},{1,17},{2,18},{3,19},{4,20},{5,21},{6,22},{7,23},{8,24},{9,... | collective-permute-start | bytes 1769480 | tf_op jit(solution)/shard_map/ppermute | solution.py:508
  354.0 9.3 %copy-start.22 = (bf16[4,64,1152]{2,1,0:T(8,128)(2,1)S(1)}, bf16[4,64,1152]{2,1,0:T(8,128)(2,1)}, u32[]{:S(2)}) copy-start(bf16[4,64,1152]{2,1,0:T(8,128)(2,1)} %param.18) | copy-start | bytes 1769476
  354.8 20.2 %collective-permute-start.21 = (bf16[64,1152]{1,0:T(8,128)(2,1)}, bf16[64,1152]{1,0:T(8,128)(2,1)S(1)}, u32[]{:S(2)}, u32[]{:S(2)}) collective-permute-start(bf16[64,1152]{1,0:T(8,128)(2,1)} %get-tuple-element.119), channel_id=1, source_target_pairs={{0,0},{1,1},{2,16},{3,17},{4,4},{5,5},{6,20},{7,21},{8,8},{9,9},{1... | collective-permute-start | bytes 442376 | tf_op jit(solution)/shard_map/ppermute | solution.py:508
  356.5 22.2 %collective-permute-start.20 = (bf16[64,1152]{1,0:T(8,128)(2,1)}, bf16[64,1152]{1,0:T(8,128)(2,1)S(1)}, u32[]{:S(2)}, u32[]{:S(2)}) collective-permute-start(bf16[64,1152]{1,0:T(8,128)(2,1)} %get-tuple-element.120), channel_id=1, source_target_pairs={{0,12},{1,13},{2,28},{3,29},{4,0},{5,1},{6,16},{7,17},{8,4},{9,5},... | collective-permute-start | bytes 442376 | tf_op jit(solution)/shard_map/ppermute | solution.py:508
  358.0 27.5 %collective-permute-start.19 = (bf16[64,1152]{1,0:T(8,128)(2,1)}, bf16[64,1152]{1,0:T(8,128)(2,1)S(1)}, u32[]{:S(2)}, u32[]{:S(2)}) collective-permute-start(bf16[64,1152]{1,0:T(8,128)(2,1)} %get-tuple-element.121), channel_id=1, source_target_pairs={{0,8},{1,9},{2,24},{3,25},{4,12},{5,13},{6,28},{7,29},{8,0},{9,1},... | collective-permute-start | bytes 442376 | tf_op jit(solution)/shard_map/ppermute | solution.py:508
  358.9 15.9 %copy-start.24 = (bf16[144,2304]{1,0:T(8,128)(2,1)S(1)}, bf16[144,2304]{1,0:T(8,128)(2,1)}, u32[]{:S(2)}) copy-start(bf16[144,2304]{1,0:T(8,128)(2,1)} %reduce-scatter.3.cloned.1.call-done) | copy-start | bytes 1990660
  358.9 39.1 %collective-permute-start.18 = (bf16[64,1152]{1,0:T(8,128)(2,1)}, bf16[64,1152]{1,0:T(8,128)(2,1)S(1)}, u32[]{:S(2)}, u32[]{:S(2)}) collective-permute-start(bf16[64,1152]{1,0:T(8,128)(2,1)} %get-tuple-element.118), channel_id=1, source_target_pairs={{0,4},{1,5},{2,20},{3,21},{4,8},{5,9},{6,24},{7,25},{8,12},{9,13},... | collective-permute-start | bytes 442376 | tf_op jit(solution)/shard_map/ppermute | solution.py:508
  360.7 37.7 %collective-permute-start.26 = (bf16[64,1152]{1,0:T(8,128)(2,1)}, bf16[64,1152]{1,0:T(8,128)(2,1)S(1)}, u32[]{:S(2)}, u32[]{:S(2)}) collective-permute-start(bf16[64,1152]{1,0:T(8,128)(2,1)} %get-tuple-element.115), channel_id=1, source_target_pairs={{0,0},{1,1},{2,16},{3,17},{4,4},{5,5},{6,20},{7,21},{8,8},{9,9},{1... | collective-permute-start | bytes 442376 | tf_op jit(solution)/shard_map/ppermute | solution.py:508
  363.5 11.5 %copy-start.31 = (bf16[64,1152]{1,0:T(8,128)(2,1)S(1)}, bf16[64,1152]{1,0:T(8,128)(2,1)}, u32[]{:S(2)}) copy-start(bf16[64,1152]{1,0:T(8,128)(2,1)} %get-tuple-element.116) | copy-start | bytes 442372
  363.5 15.2 %copy-start.30 = (bf16[64,1152]{1,0:T(8,128)(2,1)S(1)}, bf16[64,1152]{1,0:T(8,128)(2,1)}, u32[]{:S(2)}) copy-start(bf16[64,1152]{1,0:T(8,128)(2,1)} %get-tuple-element.117) | copy-start | bytes 442372
  363.5 22.0 %copy-start.29 = (bf16[64,1152]{1,0:T(8,128)(2,1)S(1)}, bf16[64,1152]{1,0:T(8,128)(2,1)}, u32[]{:S(2)}) copy-start(bf16[64,1152]{1,0:T(8,128)(2,1)} %get-tuple-element.114) | copy-start | bytes 442372
  364.4 23.4 %all-to-all-start = ((f32[32,1,512]{2,1,0:T(1,128)}), f32[32,1,512]{2,1,0:T(1,128)S(1)}, u32[]{:S(2)}, u32[]{:S(2)}) async-start(f32[32,1,512]{2,1,0:T(1,128)} %bitcast.13), calls=%async_computation.2 | async-start | bytes 131072 | tf_op jit(solution)/shard_map/all_to_all | solution.py:674
  374.9 24.0 %copy-start.42 = (pred[4]{0:T(512)(128)(4,1)S(1)}, pred[4]{0:T(512)(128)(4,1)}, u32[]{:S(2)}) copy-start(pred[4]{0:T(512)(128)(4,1)} %broadcast_compare_fusion.2) | copy-start | bytes 16
  374.9 24.0 %copy-start.43 = (pred[4]{0:T(512)(128)(4,1)S(1)}, pred[4]{0:T(512)(128)(4,1)}, u32[]{:S(2)}) copy-start(pred[4]{0:T(512)(128)(4,1)} %get-tuple-element.168) | copy-start | bytes 16
  374.9 24.0 %copy-start.44 = (pred[4]{0:T(512)(128)(4,1)S(1)}, pred[4]{0:T(512)(128)(4,1)}, u32[]{:S(2)}) copy-start(pred[4]{0:T(512)(128)(4,1)} %get-tuple-element.169) | copy-start | bytes 16
  375.1 23.4 %collective-permute-start.25 = (bf16[64,1152]{1,0:T(8,128)(2,1)S(1)}, bf16[64,1152]{1,0:T(8,128)(2,1)S(1)}, u32[]{:S(2)}, u32[]{:S(2)}) collective-permute-start(bf16[64,1152]{1,0:T(8,128)(2,1)S(1)} %copy-done.31), channel_id=1, source_target_pairs={{0,12},{1,13},{2,28},{3,29},{4,0},{5,1},{6,16},{7,17},{8,4},{9,5},... | collective-permute-start | bytes 442376 | tf_op jit(solution)/shard_map/ppermute | solution.py:508
  378.7 20.1 %collective-permute-start.24 = (bf16[64,1152]{1,0:T(8,128)(2,1)S(1)}, bf16[64,1152]{1,0:T(8,128)(2,1)S(1)}, u32[]{:S(2)}, u32[]{:S(2)}) collective-permute-start(bf16[64,1152]{1,0:T(8,128)(2,1)S(1)} %copy-done.30), channel_id=1, source_target_pairs={{0,8},{1,9},{2,24},{3,25},{4,12},{5,13},{6,28},{7,29},{8,0},{9,1},... | collective-permute-start | bytes 442376 | tf_op jit(solution)/shard_map/ppermute | solution.py:508
  385.5 13.4 %collective-permute-start.23 = (bf16[64,1152]{1,0:T(8,128)(2,1)S(1)}, bf16[64,1152]{1,0:T(8,128)(2,1)}, u32[]{:S(2)}, u32[]{:S(2)}) collective-permute-start(bf16[64,1152]{1,0:T(8,128)(2,1)S(1)} %copy-done.29), channel_id=1, source_target_pairs={{0,4},{1,5},{2,20},{3,21},{4,8},{5,9},{6,24},{7,25},{8,12},{9,13},... | collective-permute-start | bytes 442376 | tf_op jit(solution)/shard_map/ppermute | solution.py:508
  388.5 17.0 %all-to-all-start.1 = ((f32[32,1,512]{2,1,0:T(1,128)}), f32[32,1,512]{2,1,0:T(1,128)S(1)}, u32[]{:S(2)}, u32[]{:S(2)}) async-start(f32[32,1,512]{2,1,0:T(1,128)} %broadcast_in_dim.152), calls=%async_computation.3 | async-start | bytes 131072 | tf_op jit(solution)/shard_map/all_to_all | solution.py:677
  398.1 8.8 %collective-permute-start.29 = (bf16[72,2304]{1,0:T(8,128)(2,1)S(1)}, bf16[72,2304]{1,0:T(8,128)(2,1)S(1)}, u32[]{:S(2)}, u32[]{:S(2)}) collective-permute-start(bf16[72,2304]{1,0:T(8,128)(2,1)S(1)} %select_convert_fusion), channel_id=1, source_target_pairs={{0,1},{1,0},{2,3},{3,2},{4,5},{5,4},{6,7},{7,6},{8,9},{9,8},{10,11... | collective-permute-start | bytes 995336 | tf_op jit(solution)/shard_map/ppermute | solution.py:508
  432.0 1.5 collective-permute-start.27
  434.0 4.8 %collective-permute-start.28 = (bf16[72,576]{1,0:T(8,128)(2,1)S(1)}, bf16[72,576]{1,0:T(8,128)(2,1)S(1)}, u32[]{:S(2)}, u32[]{:S(2)}) collective-permute-start(bf16[72,576]{1,0:T(8,128)(2,1)S(1)} %select_convert_fusion.2), channel_id=1, source_target_pairs={{0,16},{1,17},{2,18},{3,19},{4,20},{5,21},{6,22},{7,23},{8,24},{9,... | collective-permute-start | bytes 248840 | tf_op jit(solution)/shard_map/ppermute | solution.py:508
  (34 other events, 121.4 us)
Sparse Core Ops, SparseCore 0:
  20.7 85.0 all-gather.2
  108.0 87.3 all-gather.4
  234.0 101.9 reduce-scatter.2
  340.7 90.2 reduce-scatter.4
where the time goes:
time: 452 us; the launch traced here: 447 us
  waiting for transfers between devices  197 us (44%)
  Pallas kernels  97.8 us (22%)
  starting transfers between devices  52.1 us (12%)
  other arithmetic  50.2 us (11%)
  local copies, waits for them, and re-layouts  34.6 us (8%)
  between operations  15.3 us (3%)
    ppermute x30, waiting for transfers between devices, send(): return lax.ppermute(values, ('dev', 'z', 'y', 'core'), joint(move))  119 us
    pallas_call x10, Pallas kernels, run(): pl.pallas_call(body, name=name, grid_spec=pltpu.PrefetchScalarGridSpec(nu...  97.8 us
    all_gather x1, waiting for transfers between devices, weights(): full_qkv = lax.all_gather(full_qkv, everyone, axis=0, tiled=True)  48.4 us
    ppermute x30, starting transfers between devices, send(): return lax.ppermute(values, ('dev', 'z', 'y', 'core'), joint(move))  31.6 us
    reduce_scatter x1, waiting for transfers between devices, attention_grads(): lax.psum_scatter(both, ('z', 'y'), scatter_dimension=0, tiled=True)  22.9 us
    all_to_all x1, starting transfers between devices, total(): parts = lax.all_to_all(parts, everyone, 0, 0, tiled=True)  10.5 us
    all_to_all x1, starting transfers between devices, total(): lax.all_to_all(every, everyone, 0, 0, tiled=True).reshape(1, -1)[:, :wide]  9.6 us
  transfers between devices with their start and end apart: 36, of which 22 were waited for; matrix products, arithmetic and copies ran while one was open for 14% of the time, Pallas kernels for 19%

commit v1 on v0

--- a/solution.py
+++ b/solution.py
@@ -13,6 +13,7 @@
 HEAD_DIM = 72
 SCALE = HEAD_DIM ** (-0.5)
 Q_BLOCK = 256
+BEHIND = ("mlp_out", "attend_bwd", "out_grads", "qkv_grads", "project_back")
 F32 = jnp.float32
 BF16 = jnp.bfloat16
 
@@ -99,6 +100,7 @@
 
 
 def run(body, name, steps, operands, specs, outs, out_specs, flops, scratch=(), pick=None):
+    share = 50 if name in BEHIND else 1
     size = sum(item.size * item.dtype.itemsize for item in operands)
     picks = () if pick is None else (pick,)
     return pl.pallas_call(
@@ -112,7 +114,9 @@
             scratch_shapes=scratch,
         ),
         out_shape=outs,
-        cost_estimate=pl.CostEstimate(flops=flops, transcendentals=0, bytes_accessed=size),
+        cost_estimate=pl.CostEstimate(
+            flops=flops // share, transcendentals=0, bytes_accessed=size // share
+        ),
         compiler_params=pltpu.CompilerParams(vmem_limit_bytes=50 << 20),
     )(*picks, *operands)
 
@@ -474,8 +478,11 @@
         half = grads.shape[1] // 2
         return grads[:, :half], grads[:, half:]
 
-    def attention_grads(self, grad_qkv, grad_out, *gates):
-        both = jnp.concatenate([grad_out, grad_qkv], axis=1)
+    def attention_grads(self, grad_qkv, grad_out):
+        return grad_qkv, grad_out
+
+    def attention_sums(self, parts, *gates):
+        both = jnp.concatenate([parts[1], parts[0]], axis=1)
         return lax.psum_scatter(both, ("z", "y"), scatter_dimension=0, tiled=True), both
 
     def attention_ends(self, both, block):
@@ -514,6 +521,10 @@
 
 def beside(values):
     return send(values, lambda d, z, y, c: (d, z, y, 1 - c))
+
+
+def upright(values):
+    return send(values, lambda d, z, y, c: (d, z, 1 - y, c))
 
 
 class Paired(Native):
@@ -641,14 +652,20 @@
     def mlp_halves(self, grads):
         return self.halve(grads.astype(F32))
 
-    def attention_grads(self, grad_qkv, grad_out, *gates):
+    def attention_grads(self, grad_qkv, grad_out):
         block = grad_out.shape[1]
         rows = grad_qkv.shape[0] // 8
-        order = grad_out.reshape(4, 2 * rows, block)
+        why = lax.axis_index("y")
+        order = grad_out.reshape(4, 2, rows, block)
         order = jnp.stack([lax.dynamic_index_in_dim(order, k, 0, False) for k in self.turned()])
-        both = jnp.concatenate([order.reshape(8 * rows, block), grad_qkv], axis=1)
-        both = after(both, *gates)
-        return lax.psum_scatter(both, ("z", "y"), scatter_dimension=0, tiled=True), both
+        both = jnp.concatenate([order, grad_qkv.reshape(4, 2, rows, -1)], axis=3)
+        mine = lax.dynamic_index_in_dim(both, why, 1, False)
+        return mine, upright(lax.dynamic_index_in_dim(both, 1 - why, 1, False))
+
+    def attention_sums(self, parts, *gates):
+        mine = parts[0].astype(F32) + after(parts[1], *gates).astype(F32)
+        mine = mine.astype(BF16).reshape(-1, mine.shape[2])
+        return lax.psum_scatter(mine, "z", scatter_dimension=0, tiled=True), mine
 
     def attention_ends(self, both, block):
         first = lax.axis_index("dev") == 0
@@ -810,8 +827,8 @@
     my_branch = lax.dynamic_slice_in_dim(after(grad_branch, grad_projected), me * block, block, 1)
     grad_out = out_grads(pieces, my_branch)
     grad_qkv = weight_grads([normed_one], [grad_projected], "qkv_grads")
-    sums_out, sent = route.attention_grads(grad_qkv, grad_out, sum_mlp)
-    grad_projected = after(grad_projected, grad_qkv, grad_out)
+    attn_parts = route.attention_grads(grad_qkv, grad_out)
+    grad_projected = after(grad_projected, attn_parts[0])
 
     grad_part_one, norm_sums, proj_sums = project_back(
         pick, grad_projected, own_qkv, qkv_block, rows_all, width
@@ -828,6 +845,7 @@
     grad_inputs = grad_middle + norm_back(
         grad_normed_one, own_unit_one, own_inverse_one, gain_one
     )
+    sums_out, sent = route.attention_sums(attn_parts, grad_inputs, sum_mlp)
     grad_inputs = after(grad_inputs.astype(BF16), sent)
     grad_patches = route.tokens_out(grad_inputs)
 

time: 452 us -> 444 us (0.982)
  waiting for transfers between devices: 197 us -> 185 us
  local copies, waits for them, and re-layouts: 34.6 us -> 40.5 us
    reduce_scatter x1, waiting for transfers between devices: 22.9 us -> 0.01 us  [attention_sums(): return (lax.psum_scatter(mine, 'z', scatter_dimension=0, tiled=True), mine)]
    ppermute x30 -> x31, waiting for transfers between devices: 119 us -> 134 us  [send(): return lax.ppermute(values, ('dev', 'z', 'y', 'core'), joint(move))]
    all_to_all x1, starting transfers between devices: 9.6 us -> 3.08 us  [total(): lax.all_to_all(every, everyone, 0, 0, tiled=True).reshape(1, -1)[:, :wide]]
    ppermute x30 -> x31, starting transfers between devices: 31.6 us -> 34.8 us  [send(): return lax.ppermute(values, ('dev', 'z', 'y', 'core'), joint(move))]
    unnamed x95 -> x91, local copies, waits for them, and re-layouts: 7.35 us -> 9.71 us
  transfers between devices with their start and end apart: 36 -> 37, of which waited for: 22 -> 19; matrix products, arithmetic and copies ran while one was open for 14% -> 16% of each run, Pallas kernels for 19% -> 19%
where the time goes in v1:
time: 444 us; the launch traced here: 436 us
  waiting for transfers between devices  185 us (42%)
  Pallas kernels  97.7 us (22%)
  starting transfers between devices  48.8 us (11%)
  other arithmetic  48.8 us (11%)
  local copies, waits for them, and re-layouts  40.5 us (9%)
  between operations  15.3 us (3%)
    ppermute x31, waiting for transfers between devices, send(): return lax.ppermute(values, ('dev', 'z', 'y', 'core'), joint(move))  134 us
    pallas_call x10, Pallas kernels, run(): pl.pallas_call(body, name=name, grid_spec=pltpu.PrefetchScalarGridSpec(nu...  97.7 us
    all_gather x1, waiting for transfers between devices, weights(): full_qkv = lax.all_gather(full_qkv, everyone, axis=0, tiled=True)  47.1 us
    ppermute x31, starting transfers between devices, send(): return lax.ppermute(values, ('dev', 'z', 'y', 'core'), joint(move))  34.8 us
    all_to_all x1, starting transfers between devices, total(): parts = lax.all_to_all(parts, everyone, 0, 0, tiled=True)  10.6 us
    unnamed x91, local copies, waits for them, and re-layouts  9.71 us
  transfers between devices with their start and end apart: 37, of which 19 were waited for; matrix products, arithmetic and copies ran while one was open for 16% of the time, Pallas kernels for 19%

profile of v1, /device:TPU:0, one launch (start us, length us, event | category | flops | bytes accessed | tf_op | source)
XLA Modules:
  0.0 435.7 jit_solution(7579193940234290574)
XLA Ops:
  10.3 3.0 collective-permute-start.6
  13.3 4.6 %collective-permute-done.6 = bf16[80,1152]{1,0:T(8,128)(2,1)S(1)} collective-permute-done((bf16[80,1152]{1,0:T(8,128)(2,1)S(1)}, bf16[80,1152]{1,0:T(8,128)(2,1)S(1)}, u32[]{:S(2)}, u32[]{:S(2)}) %collective-permute-start.6) | collective-permute-done | bytes 184352 | tf_op jit(solution)/shard_map/ppermute | solution.py:515
  21.8 1.9 collective-permute-start.1
  23.7 2.6 collective-permute-start.2
  29.6 4.5 %collective-permute-done.1 = bf16[64,2432]{1,0:T(8,128)(2,1)S(1)} collective-permute-done((bf16[64,2432]{1,0:T(8,128)(2,1)S(1)}, bf16[64,2432]{1,0:T(8,128)(2,1)S(1)}, u32[]{:S(2)}, u32[]{:S(2)}) %collective-permute-start.1) | collective-permute-done | bytes 311328 | tf_op jit(solution)/shard_map/ppermute | solution.py:515
  34.9 22.2 %collective-permute-done.2 = bf16[64,2432]{1,0:T(8,128)(2,1)S(1)} collective-permute-done((bf16[64,2432]{1,0:T(8,128)(2,1)S(1)}, bf16[64,2432]{1,0:T(8,128)(2,1)S(1)}, u32[]{:S(2)}, u32[]{:S(2)}) %collective-permute-start.2) | collective-permute-done | bytes 311328 | tf_op jit(solution)/shard_map/ppermute | solution.py:515
  58.6 47.1 %all-gather.3.cloned.1.call-done.weight_ref = bf16[1152,2944]{1,0:T(8,128)(2,1)} async-done(((bf16[72,2944]{1,0:T(8,128)(2,1)}), bf16[1152,2944]{1,0:T(8,128)(2,1)}) %all-gather.3.cloned.1.call-update) | async-done | bytes 6782992 | tf_op jit(solution)/shard_map/all_gather | solution.py:631
  105.9 2.0 fusion.59
  109.6 15.5 %collective-permute-done.4 = bf16[256,1280]{1,0:T(8,128)(2,1)S(1)} collective-permute-done((bf16[256,1280]{1,0:T(8,128)(2,1)}, bf16[256,1280]{1,0:T(8,128)(2,1)S(1)}, u32[]{:S(2)}, u32[]{:S(2)}) %collective-permute-start.4) | collective-permute-done | bytes 655392 | tf_op jit(solution)/shard_map/ppermute | solution.py:515
  125.1 2.3 pad_maximum_fusion.2
  138.2 6.8 %project.1 = (bf16[1024,1152]{1,0:T(8,128)(2,1)}, bf16[1024,864]{1,0:T(8,128)(2,1)S(1)}) custom-call(s32[1]{0:T(128)} %bitcast._, bf16[1024,1280]{1,0:T(8,128)(2,1)} %copy-done.13, f32[1,1152]{1,0:T(1,128)S(1)} %reshape.512.gain_ref, f32[1,1152]{1,0:T(1,128)S(1)} %reshape.513.shift_ref, bf16[1152,2944]{1,0:T(8,128)(2,1)} %all-gather.3.cloned.1.call-done.weight_ref, ...), custom_call_target="tpu_custom_call" | custom-call | flops 2038431744 | bytes 9417088 | tf_op jit(solution)/shard_map/project/pallas_call | solution.py:106
  145.0 12.2 %attend_fwd.1 = (bf16[1,288,1024]{2,1,0:T(8,128)(2,1)S(1)}, f32[1,8,1024]{2,1,0:T(8,128)S(1)}) custom-call(bf16[1,1024,864]{2,1,0:T(8,128)(2,1)S(1)} %bitcast.34, f32[1,1024,1]{2,1,0:T(8,128)S(1)} %fusion.41.bias_ref), custom_call_target="tpu_custom_call" | custom-call | flops 2147483648 | bytes 1773568 | tf_op jit(solution)/shard_map/attend_fwd/pallas_call | solution.py:106
  159.7 13.8 %collective-permute-done.7 = bf16[288,1024]{1,0:T(8,128)(2,1)S(1)} collective-permute-done((bf16[288,1024]{1,0:T(8,128)(2,1)S(1)}, bf16[288,1024]{1,0:T(8,128)(2,1)S(1)}, u32[]{:S(2)}, u32[]{:S(2)}) %collective-permute-start.7) | collective-permute-done | bytes 589856 | tf_op jit(solution)/shard_map/ppermute | solution.py:515
  173.6 12.1 %collective-permute-done.9 = bf16[256,1152]{1,0:T(8,128)(2,1)S(1)} collective-permute-done((bf16[256,1152]{1,0:T(8,128)(2,1)S(1)}, bf16[256,1152]{1,0:T(8,128)(2,1)S(1)}, u32[]{:S(2)}, u32[]{:S(2)}) %collective-permute-start.9) | collective-permute-done | bytes 589856 | tf_op jit(solution)/shard_map/ppermute | solution.py:515
  186.3 1.7 pad_maximum_fusion.refs_2_
  188.1 9.9 %attend_out.1 = (f32[1024,1152]{1,0:T(8,128)}, bf16[1024,1152]{1,0:T(8,128)(2,1)}) custom-call(bf16[576,1024]{1,0:T(8,128)(2,1)S(1)} %pad_maximum_fusion.4.refs_0_, bf16[576,1024]{1,0:T(8,128)(2,1)S(1)} %collective-permute-done.8.refs_1_, bf16[2,576,1152]{2,1,0:T(8,128)(2,1)} %pad_maximum_fusion.refs_2_, bf16[1024,1280]{1,0:T(8,128)(2,1)} %copy-done.13, ...), custom_call_target="tpu_custom_call" | custom-call | flops 2717908992 | bytes 7648768 | tf_op jit(solution)/shard_map/attend_out/pallas_call | solution.py:106
  200.3 15.0 %mlp_turn.1 = (bf16[1024,1152]{1,0:T(8,128)(2,1)S(1)}, bf16[1024,1152]{1,0:T(8,128)(2,1)}, bf16[1024,1152]{1,0:T(8,128)(2,1)}, f32[1,1152]{1,0:T(1,128)S(1)}) custom-call(s32[1]{0:T(128)} %bitcast._, bf16[1024,1152]{1,0:T(8,128)(2,1)} %get-tuple-element.47.normed_ref.refs_1_, bf16[1024,1152]{1,0:T(8,128)(2,1)} %copy-done.2, ...), custom_call_target="tpu_custom_call" | custom-call | flops 8153726976 | bytes 15340032 | tf_op jit(solution)/shard_map/mlp_turn/pallas_call | solution.py:106
  215.3 2.2 constant_dynamic-slice_fusion.19
  221.9 2.2 add_convert_fusion.4
  226.2 10.8 %mlp_grads.1 = bf16[1152,2304]{1,0:T(8,128)(2,1)} custom-call(bf16[1024,1152]{1,0:T(8,128)(2,1)S(1)} %copy-done.3, bf16[1024,1152]{1,0:T(8,128)(2,1)} %get-tuple-element.47.normed_ref.refs_1_, bf16[1024,1152]{1,0:T(8,128)(2,1)} %copy-done.4, bf16[1024,1152]{1,0:T(8,128)(2,1)} %get-tuple-element.52.refs_3_), custom_call_target="tpu_custom_call" | custom-call | flops 5435817984 | bytes 9437184 | tf_op jit(solution)/shard_map/mlp_grads/pallas_call | solution.py:106
  237.3 2.8 collective-permute-done.12
  240.1 2.2 multiply_reduce_fusion.2
  242.2 2.5 multiply_reduce_fusion
  244.7 3.5 convert_reduce_fusion.2
  249.7 7.0 %mlp_out.1 = bf16[1024,1152]{1,0:T(8,128)(2,1)S(1)} custom-call(s32[1]{0:T(128)} %bitcast._, bf16[1024,1152]{1,0:T(8,128)(2,1)} %copy-done.4, bf16[1152,4608]{1,0:T(8,128)(2,1)} %all-gather.5.cloned.1.call-done.mlp_ref), custom_call_target="tpu_custom_call" | custom-call | flops 54358180 | bytes 259522 | tf_op jit(solution)/shard_map/mlp_out/pallas_call | solution.py:106
  256.7 6.5 %collective-permute-done.13 = bf16[256,1152]{1,0:T(8,128)(2,1)S(1)} collective-permute-done((bf16[256,1152]{1,0:T(8,128)(2,1)S(1)}, bf16[256,1152]{1,0:T(8,128)(2,1)S(1)}, u32[]{:S(2)}, u32[]{:S(2)}) %collective-permute-start.13) | collective-permute-done | bytes 589856 | tf_op jit(solution)/shard_map/ppermute | solution.py:515
  265.8 1.9 collective-permute-done.14
  271.4 23.0 %attend_bwd.1 = bf16[1,1024,864]{2,1,0:T(8,128)(2,1)S(1)} custom-call(bf16[1,1024,864]{2,1,0:T(8,128)(2,1)} %bitcast.35, f32[1,1024,1]{2,1,0:T(8,128)S(1)} %fusion.41.bias_ref, f32[1,8,1024]{2,1,0:T(8,128)S(1)} %copy-done.9, bf16[1,1024,1152]{2,1,0:T(8,128)(2,1)} %bitcast.38, bf16[288,1152]{1,0:T(8,128)(2,1)S(1)} %get-tuple-element.88.w_ref), custom_call_target="tpu_custom_call" | custom-call | flops 107374184 | bytes 96583 | tf_op jit(solution)/shard_map/attend_bwd/pallas_call | solution.py:106
  294.4 1.7 constant_dynamic-slice_fusion.17.refs_2_
  297.5 4.3 qkv_grads.1
  303.4 1.8 dynamic-slice_bitcast_fusion
  305.1 7.3 %project_back.1 = (bf16[1024,1152]{1,0:T(8,128)(2,1)}, f32[2,1152]{1,0:T(2,128)S(1)}, f32[1,864]{1,0:T(1,128)S(1)}) custom-call(s32[1]{0:T(128)} %bitcast._, bf16[1024,864]{1,0:T(8,128)(2,1)S(1)} %bitcast.31, bf16[1152,2944]{1,0:T(8,128)(2,1)} %all-gather.3.cloned.1.call-done.weight_ref, bf16[1024,1280]{1,0:T(8,128)(2,1)} %copy-done.13), custom_call_target="tpu_custom_call" | custom-call | flops 40768632 | bytes 223477 | tf_op jit(solution)/shard_map/project_back/pallas_call | solution.py:106
  314.0 2.8 collective-permute-done.15
  325.0 11.3 %collective-permute-done.22 = bf16[256,1152]{1,0:T(8,128)(2,1)S(1)} collective-permute-done((bf16[256,1152]{1,0:T(8,128)(2,1)S(1)}, bf16[256,1152]{1,0:T(8,128)(2,1)S(1)}, u32[]{:S(2)}, u32[]{:S(2)}) %collective-permute-start.22) | collective-permute-done | bytes 589856 | tf_op jit(solution)/shard_map/ppermute | solution.py:515
  336.4 1.8 fusion.58
  341.2 1.9 fusion.10
  343.0 11.2 %collective-permute-done.17 = bf16[256,1152]{1,0:T(8,128)(2,1)S(1)} collective-permute-done((bf16[256,1152]{1,0:T(8,128)(2,1)S(1)}, bf16[256,1152]{1,0:T(8,128)(2,1)S(1)}, u32[]{:S(2)}, u32[]{:S(2)}) %collective-permute-start.17) | collective-permute-done | bytes 589856 | tf_op jit(solution)/shard_map/ppermute | solution.py:515
  354.3 1.7 add_convert_fusion.1
  358.3 2.0 collective-permute-start.20
  362.0 3.1 add_convert_fusion
  369.6 10.6 %all-to-all-start = ((f32[32,1,512]{2,1,0:T(1,128)}), f32[32,1,512]{2,1,0:T(1,128)S(1)}, u32[]{:S(2)}, u32[]{:S(2)}) async-start(f32[32,1,512]{2,1,0:T(1,128)} %bitcast.16), calls=%async_computation.2 | async-start | bytes 131072 | tf_op jit(solution)/shard_map/all_to_all | solution.py:691
  380.4 3.7 collective-permute-start.26
  385.2 3.3 all-to-all-done
  389.3 3.1 all-to-all-start.1
  394.3 20.1 %collective-permute-done.25 = bf16[64,1152]{1,0:T(8,128)(2,1)} collective-permute-done((bf16[64,1152]{1,0:T(8,128)(2,1)S(1)}, bf16[64,1152]{1,0:T(8,128)(2,1)}, u32[]{:S(2)}, u32[]{:S(2)}) %collective-permute-start.25) | collective-permute-done | bytes 147488 | tf_op jit(solution)/shard_map/ppermute | solution.py:515
  414.4 2.4 select_select_fusion
  422.5 2.4 collective-permute-start.29
  425.9 2.0 collective-permute-done.29
  (272 shorter events, 80.0 us)
Async XLA Ops:
  7.2 98.5 %all-gather.3.cloned.1.call-start = ((), (), s32[]{:S(2)}) async-start(), calls=%async_computation.4 | async-start | bytes 7206912 | tf_op jit(solution)/shard_map/all_gather | solution.py:631
  10.3 7.6 %collective-permute-start.6 = (bf16[80,1152]{1,0:T(8,128)(2,1)S(1)}, bf16[80,1152]{1,0:T(8,128)(2,1)S(1)}, u32[]{:S(2)}, u32[]{:S(2)}) collective-permute-start(bf16[80,1152]{1,0:T(8,128)(2,1)S(1)} %fusion.48), channel_id=1, source_target_pairs={{0,16},{1,17},{2,18},{3,19},{4,20},{5,21},{6,22},{7,23},{8,24},{9,... | collective-permute-start | bytes 552968 | tf_op jit(solution)/shard_map/ppermute | solution.py:515
  20.5 177.7 %all-gather.5.cloned.1.call-start = ((), (), s32[]{:S(2)}) async-start(), calls=%async_computation.5 | async-start | bytes 11280384 | tf_op jit(solution)/shard_map/all_gather | solution.py:633
  20.9 7.0 %copy-start.41 = (pred[1152]{0:T(1024)(128)(4,1)S(1)}, pred[1152]{0:T(1024)(128)(4,1)}, u32[]{:S(2)}) copy-start(pred[1152]{0:T(1024)(128)(4,1)} %constant.244.clone.1) | copy-start | bytes 3460
  21.0 7.9 %collective-permute-start = (bf16[64,2432]{1,0:T(8,128)(2,1)S(1)}, bf16[64,2432]{1,0:T(8,128)(2,1)S(1)}, u32[]{:S(2)}, u32[]{:S(2)}) collective-permute-start(bf16[64,2432]{1,0:T(8,128)(2,1)S(1)} %get-tuple-element.105), channel_id=1, source_target_pairs={{0,0},{1,1},{2,16},{3,17},{4,4},{5,5},{6,20},{7,21},{8,8},{9,9},{1... | collective-permute-start | bytes 933896 | tf_op jit(solution)/shard_map/ppermute | solution.py:515
  21.8 12.3 %collective-permute-start.1 = (bf16[64,2432]{1,0:T(8,128)(2,1)S(1)}, bf16[64,2432]{1,0:T(8,128)(2,1)S(1)}, u32[]{:S(2)}, u32[]{:S(2)}) collective-permute-start(bf16[64,2432]{1,0:T(8,128)(2,1)S(1)} %get-tuple-element.104), channel_id=1, source_target_pairs={{0,4},{1,5},{2,20},{3,21},{4,8},{5,9},{6,24},{7,25},{8,12},{9,13},... | collective-permute-start | bytes 933896 | tf_op jit(solution)/shard_map/ppermute | solution.py:515
  23.7 33.4 %collective-permute-start.2 = (bf16[64,2432]{1,0:T(8,128)(2,1)S(1)}, bf16[64,2432]{1,0:T(8,128)(2,1)S(1)}, u32[]{:S(2)}, u32[]{:S(2)}) collective-permute-start(bf16[64,2432]{1,0:T(8,128)(2,1)S(1)} %get-tuple-element.103), channel_id=1, source_target_pairs={{0,8},{1,9},{2,24},{3,25},{4,12},{5,13},{6,28},{7,29},{8,0},{9,1},... | collective-permute-start | bytes 933896 | tf_op jit(solution)/shard_map/ppermute | solution.py:515
  26.3 31.6 %collective-permute-start.3 = (bf16[64,2432]{1,0:T(8,128)(2,1)S(1)}, bf16[64,2432]{1,0:T(8,128)(2,1)S(1)}, u32[]{:S(2)}, u32[]{:S(2)}) collective-permute-start(bf16[64,2432]{1,0:T(8,128)(2,1)S(1)} %get-tuple-element.102), channel_id=1, source_target_pairs={{0,12},{1,13},{2,28},{3,29},{4,0},{5,1},{6,16},{7,17},{8,4},{9,5},... | collective-permute-start | bytes 933896 | tf_op jit(solution)/shard_map/ppermute | solution.py:515
  105.7 256.3 %reduce-scatter.3.cloned.1.call-start = ((), (), s32[]{:S(2)}) async-start(), calls=%async_computation.6 | async-start | bytes 5971968 | tf_op jit(solution)/shard_map/reduce_scatter | solution.py:650
  108.0 17.1 %collective-permute-start.4 = (bf16[256,1280]{1,0:T(8,128)(2,1)}, bf16[256,1280]{1,0:T(8,128)(2,1)S(1)}, u32[]{:S(2)}, u32[]{:S(2)}) collective-permute-start(bf16[256,1280]{1,0:T(8,128)(2,1)} %get-tuple-element.100), channel_id=1, source_target_pairs={{0,16},{1,17},{2,18},{3,19},{4,20},{5,21},{6,22},{7,23},{8,24},{9,... | collective-permute-start | bytes 1966088 | tf_op jit(solution)/shard_map/ppermute | solution.py:515
  127.4 5.1 %collective-permute-start.5 = (bf16[512,1280]{1,0:T(8,128)(2,1)}, bf16[512,1280]{1,0:T(8,128)(2,1)}, u32[]{:S(2)}, u32[]{:S(2)}) collective-permute-start(bf16[512,1280]{1,0:T(8,128)(2,1)} %pad_maximum_fusion.2), channel_id=1, source_target_pairs={{0,1},{1,0},{2,3},{3,2},{4,5},{5,4},{6,7},{7,6},{8,9},{9,8},{10,11... | collective-permute-start | bytes 3932168 | tf_op jit(solution)/shard_map/ppermute | solution.py:515
  145.0 12.2 %copy-start.5 = (bf16[1024,864]{1,0:T(8,128)(2,1)}, bf16[1024,864]{1,0:T(8,128)(2,1)S(1)}, u32[]{:S(2)}) copy-start(bf16[1024,864]{1,0:T(8,128)(2,1)S(1)} %get-tuple-element.44) | copy-start | bytes 5308420
  157.3 16.2 %collective-permute-start.7 = (bf16[288,1024]{1,0:T(8,128)(2,1)S(1)}, bf16[288,1024]{1,0:T(8,128)(2,1)S(1)}, u32[]{:S(2)}, u32[]{:S(2)}) collective-permute-start(bf16[288,1024]{1,0:T(8,128)(2,1)S(1)} %bitcast.36), channel_id=1, source_target_pairs={{0,16},{1,17},{2,18},{3,19},{4,20},{5,21},{6,22},{7,23},{8,24},{9,... | collective-permute-start | bytes 1769480 | tf_op jit(solution)/shard_map/ppermute | solution.py:515
  158.8 26.9 %collective-permute-start.9 = (bf16[256,1152]{1,0:T(8,128)(2,1)S(1)}, bf16[256,1152]{1,0:T(8,128)(2,1)S(1)}, u32[]{:S(2)}, u32[]{:S(2)}) collective-permute-start(bf16[256,1152]{1,0:T(8,128)(2,1)S(1)} %slice.309), channel_id=1, source_target_pairs={{0,16},{1,17},{2,18},{3,19},{4,20},{5,21},{6,22},{7,23},{8,24},{9,... | collective-permute-start | bytes 1769480 | tf_op jit(solution)/shard_map/ppermute | solution.py:515
  173.5 14.6 %copy-start = (bf16[576,1024]{1,0:T(8,128)(2,1)}, bf16[576,1024]{1,0:T(8,128)(2,1)S(1)}, u32[]{:S(2)}) copy-start(bf16[576,1024]{1,0:T(8,128)(2,1)S(1)} %pad_maximum_fusion.4.refs_0_) | copy-start | bytes 3538948
  173.5 14.5 %collective-permute-start.8 = (bf16[576,1024]{1,0:T(8,128)(2,1)S(1)}, bf16[576,1024]{1,0:T(8,128)(2,1)S(1)}, u32[]{:S(2)}, u32[]{:S(2)}) collective-permute-start(bf16[576,1024]{1,0:T(8,128)(2,1)S(1)} %pad_maximum_fusion.4.refs_0_), channel_id=1, source_target_pairs={{0,1},{1,0},{2,3},{3,2},{4,5},{5,4},{6,7},{7,6},{8,9},{9,8},{10,11... | collective-permute-start | bytes 3538952 | tf_op jit(solution)/shard_map/ppermute | solution.py:515
  185.8 12.2 %collective-permute-start.10 = (bf16[512,1152]{1,0:T(8,128)(2,1)S(1)}, bf16[512,1152]{1,0:T(8,128)(2,1)S(1)}, u32[]{:S(2)}, u32[]{:S(2)}) collective-permute-start(bf16[512,1152]{1,0:T(8,128)(2,1)S(1)} %pad_maximum_fusion.5), channel_id=1, source_target_pairs={{0,1},{1,0},{2,3},{3,2},{4,5},{5,4},{6,7},{7,6},{8,9},{9,8},{10,11... | collective-permute-start | bytes 3538952 | tf_op jit(solution)/shard_map/ppermute | solution.py:515
  188.1 9.9 %copy-start.6 = (bf16[576,1024]{1,0:T(8,128)(2,1)}, bf16[576,1024]{1,0:T(8,128)(2,1)S(1)}, u32[]{:S(2)}) copy-start(bf16[576,1024]{1,0:T(8,128)(2,1)S(1)} %collective-permute-done.8.refs_1_) | copy-start | bytes 3538948
  218.6 3.4 collective-permute-start.11
  224.1 15.9 %collective-permute-start.12 = (bf16[256,1152]{1,0:T(8,128)(2,1)}, bf16[256,1152]{1,0:T(8,128)(2,1)}, u32[]{:S(2)}, u32[]{:S(2)}) collective-permute-start(bf16[256,1152]{1,0:T(8,128)(2,1)} %add_convert_fusion.4), channel_id=1, source_target_pairs={{0,16},{1,17},{2,18},{3,19},{4,20},{5,21},{6,22},{7,23},{8,24},{9,... | collective-permute-start | bytes 1769480 | tf_op jit(solution)/shard_map/ppermute | solution.py:515
  237.0 182.4 %reduce-scatter.5.cloned.1.call-start = ((), (), s32[]{:S(2)}) async-start(), calls=%async_computation.7 | async-start | bytes 1658880 | tf_op jit(solution)/shard_map/reduce_scatter | solution.py:668
  248.3 15.0 %copy-start.15 = (bf16[256,1152]{1,0:T(8,128)(2,1)}, bf16[256,1152]{1,0:T(8,128)(2,1)S(1)}, u32[]{:S(2)}) copy-start(bf16[256,1152]{1,0:T(8,128)(2,1)S(1)} %get-tuple-element.84) | copy-start | bytes 1769476
  248.3 15.0 %collective-permute-start.13 = (bf16[256,1152]{1,0:T(8,128)(2,1)S(1)}, bf16[256,1152]{1,0:T(8,128)(2,1)S(1)}, u32[]{:S(2)}, u32[]{:S(2)}) collective-permute-start(bf16[256,1152]{1,0:T(8,128)(2,1)S(1)} %get-tuple-element.84), channel_id=1, source_target_pairs={{0,16},{1,17},{2,18},{3,19},{4,20},{5,21},{6,22},{7,23},{8,24},{9,... | collective-permute-start | bytes 1769480 | tf_op jit(solution)/shard_map/ppermute | solution.py:515
  264.4 3.2 collective-permute-start.14
  271.3 24.8 %copy-start.7 = (bf16[576,1024]{1,0:T(8,128)(2,1)S(1)}, bf16[576,1024]{1,0:T(8,128)(2,1)}, u32[]{:S(2)}) copy-start(bf16[576,1024]{1,0:T(8,128)(2,1)} %copy-done.6) | copy-start | bytes 3538948
  313.9 2.9 collective-permute-start.15
  320.3 17.9 %collective-permute-start.16 = (bf16[512,1152]{1,0:T(8,128)(2,1)}, bf16[512,1152]{1,0:T(8,128)(2,1)}, u32[]{:S(2)}, u32[]{:S(2)}) collective-permute-start(bf16[512,1152]{1,0:T(8,128)(2,1)} %pad_maximum_fusion.9), channel_id=1, source_target_pairs={{0,1},{1,0},{2,3},{3,2},{4,5},{5,4},{6,7},{7,6},{8,9},{9,8},{10,11... | collective-permute-start | bytes 3538952 | tf_op jit(solution)/shard_map/ppermute | solution.py:515
  320.7 15.7 %copy-start.19 = (bf16[512,1152]{1,0:T(8,128)(2,1)S(1)}, bf16[512,1152]{1,0:T(8,128)(2,1)}, u32[]{:S(2)}) copy-start(bf16[512,1152]{1,0:T(8,128)(2,1)} %copy-done.18) | copy-start | bytes 3538948
  320.7 41.3 %collective-permute-start.23 = (bf16[4,144,1152]{2,1,0:T(8,128)(2,1)}, bf16[4,144,1152]{2,1,0:T(8,128)(2,1)}, u32[]{:S(2)}, u32[]{:S(2)}) collective-permute-start(bf16[4,144,1152]{2,1,0:T(8,128)(2,1)} %get-tuple-element.86), channel_id=1, source_target_pairs={{0,2},{1,3},{2,0},{3,1},{4,6},{5,7},{6,4},{7,5},{8,10},{9,11},{10,... | collective-permute-start | bytes 3981320 | tf_op jit(solution)/shard_map/ppermute | solution.py:515
  320.9 15.4 %collective-permute-start.22 = (bf16[256,1152]{1,0:T(8,128)(2,1)S(1)}, bf16[256,1152]{1,0:T(8,128)(2,1)S(1)}, u32[]{:S(2)}, u32[]{:S(2)}) collective-permute-start(bf16[256,1152]{1,0:T(8,128)(2,1)S(1)} %add_convert_fusion.3), channel_id=1, source_target_pairs={{0,16},{1,17},{2,18},{3,19},{4,20},{5,21},{6,22},{7,23},{8,24},{9,... | collective-permute-start | bytes 1769480 | tf_op jit(solution)/shard_map/ppermute | solution.py:515
  339.5 14.8 %collective-permute-start.17 = (bf16[256,1152]{1,0:T(8,128)(2,1)S(1)}, bf16[256,1152]{1,0:T(8,128)(2,1)S(1)}, u32[]{:S(2)}, u32[]{:S(2)}) collective-permute-start(bf16[256,1152]{1,0:T(8,128)(2,1)S(1)} %add_convert_fusion.2), channel_id=1, source_target_pairs={{0,16},{1,17},{2,18},{3,19},{4,20},{5,21},{6,22},{7,23},{8,24},{9,... | collective-permute-start | bytes 1769480 | tf_op jit(solution)/shard_map/ppermute | solution.py:515
  356.8 23.5 %collective-permute-start.21 = (bf16[64,1152]{1,0:T(8,128)(2,1)}, bf16[64,1152]{1,0:T(8,128)(2,1)S(1)}, u32[]{:S(2)}, u32[]{:S(2)}) collective-permute-start(bf16[64,1152]{1,0:T(8,128)(2,1)} %get-tuple-element.121), channel_id=1, source_target_pairs={{0,0},{1,1},{2,16},{3,17},{4,4},{5,5},{6,20},{7,21},{8,8},{9,9},{1... | collective-permute-start | bytes 442376 | tf_op jit(solution)/shard_map/ppermute | solution.py:515
  358.3 25.7 %collective-permute-start.20 = (bf16[64,1152]{1,0:T(8,128)(2,1)}, bf16[64,1152]{1,0:T(8,128)(2,1)S(1)}, u32[]{:S(2)}, u32[]{:S(2)}) collective-permute-start(bf16[64,1152]{1,0:T(8,128)(2,1)} %get-tuple-element.122), channel_id=1, source_target_pairs={{0,12},{1,13},{2,28},{3,29},{4,0},{5,1},{6,16},{7,17},{8,4},{9,5},... | collective-permute-start | bytes 442376 | tf_op jit(solution)/shard_map/ppermute | solution.py:515
  360.4 23.7 %collective-permute-start.19 = (bf16[64,1152]{1,0:T(8,128)(2,1)}, bf16[64,1152]{1,0:T(8,128)(2,1)S(1)}, u32[]{:S(2)}, u32[]{:S(2)}) collective-permute-start(bf16[64,1152]{1,0:T(8,128)(2,1)} %get-tuple-element.123), channel_id=1, source_target_pairs={{0,8},{1,9},{2,24},{3,25},{4,12},{5,13},{6,28},{7,29},{8,0},{9,1},... | collective-permute-start | bytes 442376 | tf_op jit(solution)/shard_map/ppermute | solution.py:515
  360.9 31.4 %collective-permute-start.18 = (bf16[64,1152]{1,0:T(8,128)(2,1)S(1)}, bf16[64,1152]{1,0:T(8,128)(2,1)S(1)}, u32[]{:S(2)}, u32[]{:S(2)}) collective-permute-start(bf16[64,1152]{1,0:T(8,128)(2,1)S(1)} %get-tuple-element.120), channel_id=1, source_target_pairs={{0,4},{1,5},{2,20},{3,21},{4,8},{5,9},{6,24},{7,25},{8,12},{9,13},... | collective-permute-start | bytes 442376 | tf_op jit(solution)/shard_map/ppermute | solution.py:515
  365.2 15.1 %copy-start.24 = (bf16[144,2304]{1,0:T(8,128)(2,1)S(1)}, bf16[144,2304]{1,0:T(8,128)(2,1)}, u32[]{:S(2)}) copy-start(bf16[144,2304]{1,0:T(8,128)(2,1)} %reduce-scatter.3.cloned.1.call-done) | copy-start | bytes 1990660
  366.0 26.7 %collective-permute-start.27 = (bf16[64,1152]{1,0:T(8,128)(2,1)}, bf16[64,1152]{1,0:T(8,128)(2,1)S(1)}, u32[]{:S(2)}, u32[]{:S(2)}) collective-permute-start(bf16[64,1152]{1,0:T(8,128)(2,1)} %get-tuple-element.117), channel_id=1, source_target_pairs={{0,0},{1,1},{2,16},{3,17},{4,4},{5,5},{6,20},{7,21},{8,8},{9,9},{1... | collective-permute-start | bytes 442376 | tf_op jit(solution)/shard_map/ppermute | solution.py:515
  368.7 11.7 %copy-start.30 = (bf16[64,1152]{1,0:T(8,128)(2,1)S(1)}, bf16[64,1152]{1,0:T(8,128)(2,1)}, u32[]{:S(2)}) copy-start(bf16[64,1152]{1,0:T(8,128)(2,1)} %get-tuple-element.118) | copy-start | bytes 442372
  368.7 15.3 %copy-start.29 = (bf16[64,1152]{1,0:T(8,128)(2,1)S(1)}, bf16[64,1152]{1,0:T(8,128)(2,1)}, u32[]{:S(2)}) copy-start(bf16[64,1152]{1,0:T(8,128)(2,1)} %get-tuple-element.119) | copy-start | bytes 442372
  368.7 15.3 %copy-start.28 = (bf16[64,1152]{1,0:T(8,128)(2,1)S(1)}, bf16[64,1152]{1,0:T(8,128)(2,1)}, u32[]{:S(2)}) copy-start(bf16[64,1152]{1,0:T(8,128)(2,1)} %get-tuple-element.116) | copy-start | bytes 442372
  369.6 18.9 %all-to-all-start = ((f32[32,1,512]{2,1,0:T(1,128)}), f32[32,1,512]{2,1,0:T(1,128)S(1)}, u32[]{:S(2)}, u32[]{:S(2)}) async-start(f32[32,1,512]{2,1,0:T(1,128)} %bitcast.16), calls=%async_computation.2 | async-start | bytes 131072 | tf_op jit(solution)/shard_map/all_to_all | solution.py:691
  380.4 14.0 %collective-permute-start.26 = (bf16[64,1152]{1,0:T(8,128)(2,1)S(1)}, bf16[64,1152]{1,0:T(8,128)(2,1)}, u32[]{:S(2)}, u32[]{:S(2)}) collective-permute-start(bf16[64,1152]{1,0:T(8,128)(2,1)S(1)} %copy-done.30), channel_id=1, source_target_pairs={{0,12},{1,13},{2,28},{3,29},{4,0},{5,1},{6,16},{7,17},{8,4},{9,5},... | collective-permute-start | bytes 442376 | tf_op jit(solution)/shard_map/ppermute | solution.py:515
  384.0 30.4 %collective-permute-start.25 = (bf16[64,1152]{1,0:T(8,128)(2,1)S(1)}, bf16[64,1152]{1,0:T(8,128)(2,1)}, u32[]{:S(2)}, u32[]{:S(2)}) collective-permute-start(bf16[64,1152]{1,0:T(8,128)(2,1)S(1)} %copy-done.29), channel_id=1, source_target_pairs={{0,8},{1,9},{2,24},{3,25},{4,12},{5,13},{6,28},{7,29},{8,0},{9,1},... | collective-permute-start | bytes 442376 | tf_op jit(solution)/shard_map/ppermute | solution.py:515
  384.1 30.3 %collective-permute-start.24 = (bf16[64,1152]{1,0:T(8,128)(2,1)S(1)}, bf16[64,1152]{1,0:T(8,128)(2,1)}, u32[]{:S(2)}, u32[]{:S(2)}) collective-permute-start(bf16[64,1152]{1,0:T(8,128)(2,1)S(1)} %copy-done.28), channel_id=1, source_target_pairs={{0,4},{1,5},{2,20},{3,21},{4,8},{5,9},{6,24},{7,25},{8,12},{9,13},... | collective-permute-start | bytes 442376 | tf_op jit(solution)/shard_map/ppermute | solution.py:515
  389.3 27.6 %all-to-all-start.1 = ((f32[32,1,512]{2,1,0:T(1,128)}), f32[32,1,512]{2,1,0:T(1,128)S(1)}, u32[]{:S(2)}, u32[]{:S(2)}) async-start(f32[32,1,512]{2,1,0:T(1,128)} %broadcast_in_dim.152), calls=%async_computation.3 | async-start | bytes 131072 | tf_op jit(solution)/shard_map/all_to_all | solution.py:694
  392.4 25.9 %collective-permute-start.30 = (bf16[72,2304]{1,0:T(8,128)(2,1)S(1)}, bf16[72,2304]{1,0:T(8,128)(2,1)S(1)}, u32[]{:S(2)}, u32[]{:S(2)}) collective-permute-start(bf16[72,2304]{1,0:T(8,128)(2,1)S(1)} %select_convert_fusion), channel_id=1, source_target_pairs={{0,1},{1,0},{2,3},{3,2},{4,5},{5,4},{6,7},{7,6},{8,9},{9,8},{10,11... | collective-permute-start | bytes 995336 | tf_op jit(solution)/shard_map/ppermute | solution.py:515
  420.5 1.5 collective-permute-start.28
  422.5 5.4 %collective-permute-start.29 = (bf16[72,576]{1,0:T(8,128)(2,1)S(1)}, bf16[72,576]{1,0:T(8,128)(2,1)S(1)}, u32[]{:S(2)}, u32[]{:S(2)}) collective-permute-start(bf16[72,576]{1,0:T(8,128)(2,1)S(1)} %select_convert_fusion.2), channel_id=1, source_target_pairs={{0,16},{1,17},{2,18},{3,19},{4,20},{5,21},{6,22},{7,23},{8,24},{9,... | collective-permute-start | bytes 248840 | tf_op jit(solution)/shard_map/ppermute | solution.py:515
  (33 other events, 85.0 us)
Sparse Core Ops, SparseCore 0:
  20.6 85.0 all-gather.2
  108.0 87.2 all-gather.4
  237.1 101.9 reduce-scatter.2
  365.3 47.3 reduce-scatter.4

commit v2 on v1

--- a/solution.py
+++ b/solution.py
@@ -836,8 +836,6 @@
     near_one = route.rows_near(grad_part_one)
     grad_normed_one = route.rows_end(near_one)
     mlp_near = route.rows_near(after(mlp_part, near_one[1]))
-    result = (own_middle + route.rows_end(mlp_near) + bias_down).astype(BF16)
-    result = route.tokens_out(result)
 
     own_unit_one, own_inverse_one = centred(
         route.own_rows(after(rows_all, near_one[1]))[:, :width].astype(F32)
@@ -848,6 +846,10 @@
     sums_out, sent = route.attention_sums(attn_parts, grad_inputs, sum_mlp)
     grad_inputs = after(grad_inputs.astype(BF16), sent)
     grad_patches = route.tokens_out(grad_inputs)
+    mlp_near = (mlp_near[0], after(mlp_near[1], sent))
+    result = (own_middle + route.rows_end(mlp_near) + bias_down).astype(BF16)
+    leaving = result
+    result = route.tokens_out(result)
 
     out_qkv, out_out = route.attention_ends(sums_out, block)
     out_mlp = route.mlp_halves(sum_mlp)
@@ -875,7 +877,7 @@
         spread(up_sums[0, :hidden], hidden * team),
         jnp.sum(after(cotangent, grad_inputs).astype(F32), axis=(0, 1)),
     ]
-    flat = route.total(after(jnp.concatenate(sums)[None], grad_inputs))
+    flat = route.total(after(jnp.concatenate(sums)[None], grad_inputs, leaving))
     out_vectors = []
     spot = 0
     for item in sums:

time: 444 us -> 441 us (level)
    all_to_all x1, starting transfers between devices: 10.6 us -> 4.57 us  [total(): parts = lax.all_to_all(parts, everyone, 0, 0, tiled=True)]
    unnamed x91 -> x97, local copies, waits for them, and re-layouts: 9.71 us -> 10.2 us
  transfers between devices with their start and end apart: 37 -> 37, of which waited for: 19 -> 18; matrix products, arithmetic and copies ran while one was open for 16% -> 15% of each run, Pallas kernels for 19% -> 19%
where the time goes in v2:
time: 441 us; the launch traced here: 435 us
  waiting for transfers between devices  184 us (42%)
  Pallas kernels  97.9 us (22%)
  other arithmetic  49 us (11%)
  starting transfers between devices  48.3 us (11%)
  local copies, waits for them, and re-layouts  41 us (9%)
  between operations  15.4 us (3%)
    ppermute x31, waiting for transfers between devices, send(): return lax.ppermute(values, ('dev', 'z', 'y', 'core'), joint(move))  135 us
    pallas_call x10, Pallas kernels, run(): pl.pallas_call(body, name=name, grid_spec=pltpu.PrefetchScalarGridSpec(nu...  97.9 us
    all_gather x1, waiting for transfers between devices, weights(): full_qkv = lax.all_gather(full_qkv, everyone, axis=0, tiled=True)  47.1 us
    ppermute x31, starting transfers between devices, send(): return lax.ppermute(values, ('dev', 'z', 'y', 'core'), joint(move))  38.9 us
    unnamed x97, local copies, waits for them, and re-layouts  10.2 us
  transfers between devices with their start and end apart: 37, of which 18 were waited for; matrix products, arithmetic and copies ran while one was open for 15% of the time, Pallas kernels for 19%

profile of v2, /device:TPU:0, one launch (start us, length us, event | category | flops | bytes accessed | tf_op | source)
XLA Modules:
  0.0 435.3 jit_solution(11851823961841936332)
XLA Ops:
  10.3 3.0 collective-permute-start.6
  13.3 4.6 %collective-permute-done.6 = bf16[80,1152]{1,0:T(8,128)(2,1)S(1)} collective-permute-done((bf16[80,1152]{1,0:T(8,128)(2,1)S(1)}, bf16[80,1152]{1,0:T(8,128)(2,1)S(1)}, u32[]{:S(2)}, u32[]{:S(2)}) %collective-permute-start.6) | collective-permute-done | bytes 184352 | tf_op jit(solution)/shard_map/ppermute | solution.py:515
  21.8 1.9 collective-permute-start.1
  23.7 2.6 collective-permute-start.2
  29.6 4.6 %collective-permute-done.1 = bf16[64,2432]{1,0:T(8,128)(2,1)S(1)} collective-permute-done((bf16[64,2432]{1,0:T(8,128)(2,1)S(1)}, bf16[64,2432]{1,0:T(8,128)(2,1)S(1)}, u32[]{:S(2)}, u32[]{:S(2)}) %collective-permute-start.1) | collective-permute-done | bytes 311328 | tf_op jit(solution)/shard_map/ppermute | solution.py:515
  34.9 22.2 %collective-permute-done.2 = bf16[64,2432]{1,0:T(8,128)(2,1)S(1)} collective-permute-done((bf16[64,2432]{1,0:T(8,128)(2,1)S(1)}, bf16[64,2432]{1,0:T(8,128)(2,1)S(1)}, u32[]{:S(2)}, u32[]{:S(2)}) %collective-permute-start.2) | collective-permute-done | bytes 311328 | tf_op jit(solution)/shard_map/ppermute | solution.py:515
  58.6 47.1 %all-gather.3.cloned.1.call-done.weight_ref = bf16[1152,2944]{1,0:T(8,128)(2,1)} async-done(((bf16[72,2944]{1,0:T(8,128)(2,1)}), bf16[1152,2944]{1,0:T(8,128)(2,1)}) %all-gather.3.cloned.1.call-update) | async-done | bytes 6782992 | tf_op jit(solution)/shard_map/all_gather | solution.py:631
  105.9 2.1 fusion.59
  109.6 15.5 %collective-permute-done.4 = bf16[256,1280]{1,0:T(8,128)(2,1)S(1)} collective-permute-done((bf16[256,1280]{1,0:T(8,128)(2,1)}, bf16[256,1280]{1,0:T(8,128)(2,1)S(1)}, u32[]{:S(2)}, u32[]{:S(2)}) %collective-permute-start.4) | collective-permute-done | bytes 655392 | tf_op jit(solution)/shard_map/ppermute | solution.py:515
  125.1 2.2 pad_maximum_fusion.2
  137.1 6.8 %project.1 = (bf16[1024,1152]{1,0:T(8,128)(2,1)}, bf16[1024,864]{1,0:T(8,128)(2,1)S(1)}) custom-call(s32[1]{0:T(128)} %bitcast._, bf16[1024,1280]{1,0:T(8,128)(2,1)} %copy-done.13, f32[1,1152]{1,0:T(1,128)S(1)} %reshape.512.gain_ref, f32[1,1152]{1,0:T(1,128)S(1)} %reshape.513.shift_ref, bf16[1152,2944]{1,0:T(8,128)(2,1)} %all-gather.3.cloned.1.call-done.weight_ref, ...), custom_call_target="tpu_custom_call" | custom-call | flops 2038431744 | bytes 9417088 | tf_op jit(solution)/shard_map/project/pallas_call | solution.py:106
  143.9 12.4 %attend_fwd.1 = (bf16[1,288,1024]{2,1,0:T(8,128)(2,1)S(1)}, f32[1,8,1024]{2,1,0:T(8,128)S(1)}) custom-call(bf16[1,1024,864]{2,1,0:T(8,128)(2,1)S(1)} %bitcast.34, f32[1,1024,1]{2,1,0:T(8,128)S(1)} %fusion.41.bias_ref), custom_call_target="tpu_custom_call" | custom-call | flops 2147483648 | bytes 1773568 | tf_op jit(solution)/shard_map/attend_fwd/pallas_call | solution.py:106
  158.7 13.8 %collective-permute-done.7 = bf16[288,1024]{1,0:T(8,128)(2,1)S(1)} collective-permute-done((bf16[288,1024]{1,0:T(8,128)(2,1)S(1)}, bf16[288,1024]{1,0:T(8,128)(2,1)S(1)}, u32[]{:S(2)}, u32[]{:S(2)}) %collective-permute-start.7) | collective-permute-done | bytes 589856 | tf_op jit(solution)/shard_map/ppermute | solution.py:515
  172.7 12.1 %collective-permute-done.9 = bf16[256,1152]{1,0:T(8,128)(2,1)S(1)} collective-permute-done((bf16[256,1152]{1,0:T(8,128)(2,1)S(1)}, bf16[256,1152]{1,0:T(8,128)(2,1)S(1)}, u32[]{:S(2)}, u32[]{:S(2)}) %collective-permute-start.9) | collective-permute-done | bytes 589856 | tf_op jit(solution)/shard_map/ppermute | solution.py:515
  185.3 1.7 pad_maximum_fusion.refs_2_
  187.2 9.9 %attend_out.1 = (f32[1024,1152]{1,0:T(8,128)}, bf16[1024,1152]{1,0:T(8,128)(2,1)}) custom-call(bf16[576,1024]{1,0:T(8,128)(2,1)S(1)} %pad_maximum_fusion.4.refs_0_, bf16[576,1024]{1,0:T(8,128)(2,1)S(1)} %collective-permute-done.8.refs_1_, bf16[2,576,1152]{2,1,0:T(8,128)(2,1)} %pad_maximum_fusion.refs_2_, bf16[1024,1280]{1,0:T(8,128)(2,1)} %copy-done.13, ...), custom_call_target="tpu_custom_call" | custom-call | flops 2717908992 | bytes 7648768 | tf_op jit(solution)/shard_map/attend_out/pallas_call | solution.py:106
  199.3 15.0 %mlp_turn.1 = (bf16[1024,1152]{1,0:T(8,128)(2,1)S(1)}, bf16[1024,1152]{1,0:T(8,128)(2,1)}, bf16[1024,1152]{1,0:T(8,128)(2,1)}, f32[1,1152]{1,0:T(1,128)S(1)}) custom-call(s32[1]{0:T(128)} %bitcast._, bf16[1024,1152]{1,0:T(8,128)(2,1)} %get-tuple-element.48.normed_ref.refs_1_, bf16[1024,1152]{1,0:T(8,128)(2,1)} %copy-done.2, ...), custom_call_target="tpu_custom_call" | custom-call | flops 8153726976 | bytes 15340032 | tf_op jit(solution)/shard_map/mlp_turn/pallas_call | solution.py:106
  214.3 2.2 constant_dynamic-slice_fusion.19
  221.1 2.0 add_convert_fusion.4
  225.2 10.8 %mlp_grads.1 = bf16[1152,2304]{1,0:T(8,128)(2,1)} custom-call(bf16[1024,1152]{1,0:T(8,128)(2,1)S(1)} %copy-done.3, bf16[1024,1152]{1,0:T(8,128)(2,1)} %get-tuple-element.48.normed_ref.refs_1_, bf16[1024,1152]{1,0:T(8,128)(2,1)} %copy-done.4, bf16[1024,1152]{1,0:T(8,128)(2,1)} %get-tuple-element.53.refs_3_), custom_call_target="tpu_custom_call" | custom-call | flops 5435817984 | bytes 9437184 | tf_op jit(solution)/shard_map/mlp_grads/pallas_call | solution.py:106
  236.3 2.7 collective-permute-done.12
  239.0 2.0 multiply_reduce_fusion.2
  241.0 2.5 multiply_reduce_fusion
  243.5 3.5 convert_reduce_fusion.2
  248.6 7.0 %mlp_out.1 = bf16[1024,1152]{1,0:T(8,128)(2,1)S(1)} custom-call(s32[1]{0:T(128)} %bitcast._, bf16[1024,1152]{1,0:T(8,128)(2,1)} %copy-done.4, bf16[1152,4608]{1,0:T(8,128)(2,1)} %all-gather.5.cloned.1.call-done.mlp_ref), custom_call_target="tpu_custom_call" | custom-call | flops 54358180 | bytes 259522 | tf_op jit(solution)/shard_map/mlp_out/pallas_call | solution.py:106
  255.5 6.5 %collective-permute-done.13 = bf16[256,1152]{1,0:T(8,128)(2,1)S(1)} collective-permute-done((bf16[256,1152]{1,0:T(8,128)(2,1)S(1)}, bf16[256,1152]{1,0:T(8,128)(2,1)S(1)}, u32[]{:S(2)}, u32[]{:S(2)}) %collective-permute-start.13) | collective-permute-done | bytes 589856 | tf_op jit(solution)/shard_map/ppermute | solution.py:515
  264.6 1.9 collective-permute-done.14
  270.2 23.0 %attend_bwd.1 = bf16[1,1024,864]{2,1,0:T(8,128)(2,1)S(1)} custom-call(bf16[1,1024,864]{2,1,0:T(8,128)(2,1)} %bitcast.35, f32[1,1024,1]{2,1,0:T(8,128)S(1)} %fusion.41.bias_ref, f32[1,8,1024]{2,1,0:T(8,128)S(1)} %copy-done.9, bf16[1,1024,1152]{2,1,0:T(8,128)(2,1)} %bitcast.38, bf16[288,1152]{1,0:T(8,128)(2,1)S(1)} %get-tuple-element.90.w_ref), custom_call_target="tpu_custom_call" | custom-call | flops 107374184 | bytes 96583 | tf_op jit(solution)/shard_map/attend_bwd/pallas_call | solution.py:106
  293.2 1.7 constant_dynamic-slice_fusion.17.refs_2_
  296.3 4.3 qkv_grads.1
  302.1 1.8 dynamic-slice_bitcast_fusion
  303.9 7.3 %project_back.1 = (bf16[1024,1152]{1,0:T(8,128)(2,1)}, f32[2,1152]{1,0:T(2,128)S(1)}, f32[1,864]{1,0:T(1,128)S(1)}) custom-call(s32[1]{0:T(128)} %bitcast._, bf16[1024,864]{1,0:T(8,128)(2,1)S(1)} %bitcast.31, bf16[1152,2944]{1,0:T(8,128)(2,1)} %all-gather.3.cloned.1.call-done.weight_ref, bf16[1024,1280]{1,0:T(8,128)(2,1)} %copy-done.13), custom_call_target="tpu_custom_call" | custom-call | flops 40768632 | bytes 223477 | tf_op jit(solution)/shard_map/project_back/pallas_call | solution.py:106
  322.0 11.8 %collective-permute-done.18 = bf16[256,1152]{1,0:T(8,128)(2,1)S(1)} collective-permute-done((bf16[256,1152]{1,0:T(8,128)(2,1)S(1)}, bf16[256,1152]{1,0:T(8,128)(2,1)S(1)}, u32[]{:S(2)}, u32[]{:S(2)}) %collective-permute-start.18) | collective-permute-done | bytes 589856 | tf_op jit(solution)/shard_map/ppermute | solution.py:515
  333.8 1.7 fusion.58
  335.5 1.7 fusion.10
  339.2 11.5 %collective-permute-done.17 = bf16[4,144,1152]{2,1,0:T(8,128)(2,1)} collective-permute-done((bf16[4,144,1152]{2,1,0:T(8,128)(2,1)}, bf16[4,144,1152]{2,1,0:T(8,128)(2,1)}, u32[]{:S(2)}, u32[]{:S(2)}) %collective-permute-start.17) | collective-permute-done | bytes 1327136 | tf_op jit(solution)/shard_map/ppermute | solution.py:515
  350.8 3.1 add_convert_fusion
  356.3 3.3 collective-permute-start.26
  363.5 6.0 %collective-permute-start.19 = (bf16[256,1152]{1,0:T(8,128)(2,1)}, bf16[256,1152]{1,0:T(8,128)(2,1)S(1)}, u32[]{:S(2)}, u32[]{:S(2)}) collective-permute-start(bf16[256,1152]{1,0:T(8,128)(2,1)} %add_convert_fusion.2), channel_id=1, source_target_pairs={{0,16},{1,17},{2,18},{3,19},{4,20},{5,21},{6,22},{7,23},{8,24},{9,... | collective-permute-start | bytes 1769480 | tf_op jit(solution)/shard_map/ppermute | solution.py:515
  372.0 17.1 %collective-permute-done.19 = bf16[256,1152]{1,0:T(8,128)(2,1)S(1)} collective-permute-done((bf16[256,1152]{1,0:T(8,128)(2,1)}, bf16[256,1152]{1,0:T(8,128)(2,1)S(1)}, u32[]{:S(2)}, u32[]{:S(2)}) %collective-permute-start.19) | collective-permute-done | bytes 589856 | tf_op jit(solution)/shard_map/ppermute | solution.py:515
  392.3 4.6 %all-to-all-start = ((f32[32,1,512]{2,1,0:T(1,128)}), f32[32,1,512]{2,1,0:T(1,128)S(1)}, u32[]{:S(2)}, u32[]{:S(2)}) async-start(f32[32,1,512]{2,1,0:T(1,128)} %bitcast.16), calls=%async_computation.2 | async-start | bytes 131072 | tf_op jit(solution)/shard_map/all_to_all | solution.py:691
  396.9 3.7 collective-permute-start.22
  402.6 1.9 all-to-all-done
  405.3 4.5 %all-to-all-start.1 = ((f32[32,1,512]{2,1,0:T(1,128)}), f32[32,1,512]{2,1,0:T(1,128)S(1)}, u32[]{:S(2)}, u32[]{:S(2)}) async-start(f32[32,1,512]{2,1,0:T(1,128)} %broadcast_in_dim.152), calls=%async_computation.3 | async-start | bytes 131072 | tf_op jit(solution)/shard_map/all_to_all | solution.py:694
  409.8 5.9 %collective-permute-done.21 = bf16[64,1152]{1,0:T(8,128)(2,1)S(1)} collective-permute-done((bf16[64,1152]{1,0:T(8,128)(2,1)S(1)}, bf16[64,1152]{1,0:T(8,128)(2,1)S(1)}, u32[]{:S(2)}, u32[]{:S(2)}) %collective-permute-start.21) | collective-permute-done | bytes 147488 | tf_op jit(solution)/shard_map/ppermute | solution.py:515
  415.8 2.4 select_select_fusion
  421.3 2.8 collective-permute-start.29
  425.0 2.4 collective-permute-done.29
  (278 shorter events, 78.8 us)
Async XLA Ops:
  7.2 98.5 %all-gather.3.cloned.1.call-start = ((), (), s32[]{:S(2)}) async-start(), calls=%async_computation.4 | async-start | bytes 7206912 | tf_op jit(solution)/shard_map/all_gather | solution.py:631
  10.3 7.6 %collective-permute-start.6 = (bf16[80,1152]{1,0:T(8,128)(2,1)S(1)}, bf16[80,1152]{1,0:T(8,128)(2,1)S(1)}, u32[]{:S(2)}, u32[]{:S(2)}) collective-permute-start(bf16[80,1152]{1,0:T(8,128)(2,1)S(1)} %fusion.48), channel_id=1, source_target_pairs={{0,16},{1,17},{2,18},{3,19},{4,20},{5,21},{6,22},{7,23},{8,24},{9,... | collective-permute-start | bytes 552968 | tf_op jit(solution)/shard_map/ppermute | solution.py:515
  20.5 176.8 %all-gather.5.cloned.1.call-start = ((), (), s32[]{:S(2)}) async-start(), calls=%async_computation.5 | async-start | bytes 11280384 | tf_op jit(solution)/shard_map/all_gather | solution.py:633
  21.0 7.8 %collective-permute-start = (bf16[64,2432]{1,0:T(8,128)(2,1)S(1)}, bf16[64,2432]{1,0:T(8,128)(2,1)S(1)}, u32[]{:S(2)}, u32[]{:S(2)}) collective-permute-start(bf16[64,2432]{1,0:T(8,128)(2,1)S(1)} %get-tuple-element.107), channel_id=1, source_target_pairs={{0,0},{1,1},{2,16},{3,17},{4,4},{5,5},{6,20},{7,21},{8,8},{9,9},{1... | collective-permute-start | bytes 933896 | tf_op jit(solution)/shard_map/ppermute | solution.py:515
  21.8 12.3 %collective-permute-start.1 = (bf16[64,2432]{1,0:T(8,128)(2,1)S(1)}, bf16[64,2432]{1,0:T(8,128)(2,1)S(1)}, u32[]{:S(2)}, u32[]{:S(2)}) collective-permute-start(bf16[64,2432]{1,0:T(8,128)(2,1)S(1)} %get-tuple-element.106), channel_id=1, source_target_pairs={{0,4},{1,5},{2,20},{3,21},{4,8},{5,9},{6,24},{7,25},{8,12},{9,13},... | collective-permute-start | bytes 933896 | tf_op jit(solution)/shard_map/ppermute | solution.py:515
  23.7 33.4 %collective-permute-start.2 = (bf16[64,2432]{1,0:T(8,128)(2,1)S(1)}, bf16[64,2432]{1,0:T(8,128)(2,1)S(1)}, u32[]{:S(2)}, u32[]{:S(2)}) collective-permute-start(bf16[64,2432]{1,0:T(8,128)(2,1)S(1)} %get-tuple-element.105), channel_id=1, source_target_pairs={{0,8},{1,9},{2,24},{3,25},{4,12},{5,13},{6,28},{7,29},{8,0},{9,1},... | collective-permute-start | bytes 933896 | tf_op jit(solution)/shard_map/ppermute | solution.py:515
  26.3 31.6 %collective-permute-start.3 = (bf16[64,2432]{1,0:T(8,128)(2,1)S(1)}, bf16[64,2432]{1,0:T(8,128)(2,1)S(1)}, u32[]{:S(2)}, u32[]{:S(2)}) collective-permute-start(bf16[64,2432]{1,0:T(8,128)(2,1)S(1)} %get-tuple-element.104), channel_id=1, source_target_pairs={{0,12},{1,13},{2,28},{3,29},{4,0},{5,1},{6,16},{7,17},{8,4},{9,5},... | collective-permute-start | bytes 933896 | tf_op jit(solution)/shard_map/ppermute | solution.py:515
  105.7 245.0 %reduce-scatter.3.cloned.1.call-start = ((), (), s32[]{:S(2)}) async-start(), calls=%async_computation.6 | async-start | bytes 5971968 | tf_op jit(solution)/shard_map/reduce_scatter | solution.py:650
  108.0 17.1 %collective-permute-start.4 = (bf16[256,1280]{1,0:T(8,128)(2,1)}, bf16[256,1280]{1,0:T(8,128)(2,1)S(1)}, u32[]{:S(2)}, u32[]{:S(2)}) collective-permute-start(bf16[256,1280]{1,0:T(8,128)(2,1)} %get-tuple-element.102), channel_id=1, source_target_pairs={{0,16},{1,17},{2,18},{3,19},{4,20},{5,21},{6,22},{7,23},{8,24},{9,... | collective-permute-start | bytes 1966088 | tf_op jit(solution)/shard_map/ppermute | solution.py:515
  127.4 5.3 %collective-permute-start.5 = (bf16[512,1280]{1,0:T(8,128)(2,1)}, bf16[512,1280]{1,0:T(8,128)(2,1)}, u32[]{:S(2)}, u32[]{:S(2)}) collective-permute-start(bf16[512,1280]{1,0:T(8,128)(2,1)} %pad_maximum_fusion.2), channel_id=1, source_target_pairs={{0,1},{1,0},{2,3},{3,2},{4,5},{5,4},{6,7},{7,6},{8,9},{9,8},{10,11... | collective-permute-start | bytes 3932168 | tf_op jit(solution)/shard_map/ppermute | solution.py:515
  143.9 12.4 %copy-start.5 = (bf16[1024,864]{1,0:T(8,128)(2,1)}, bf16[1024,864]{1,0:T(8,128)(2,1)S(1)}, u32[]{:S(2)}) copy-start(bf16[1024,864]{1,0:T(8,128)(2,1)S(1)} %get-tuple-element.45) | copy-start | bytes 5308420
  156.3 16.2 %collective-permute-start.7 = (bf16[288,1024]{1,0:T(8,128)(2,1)S(1)}, bf16[288,1024]{1,0:T(8,128)(2,1)S(1)}, u32[]{:S(2)}, u32[]{:S(2)}) collective-permute-start(bf16[288,1024]{1,0:T(8,128)(2,1)S(1)} %bitcast.36), channel_id=1, source_target_pairs={{0,16},{1,17},{2,18},{3,19},{4,20},{5,21},{6,22},{7,23},{8,24},{9,... | collective-permute-start | bytes 1769480 | tf_op jit(solution)/shard_map/ppermute | solution.py:515
  157.8 26.9 %collective-permute-start.9 = (bf16[256,1152]{1,0:T(8,128)(2,1)S(1)}, bf16[256,1152]{1,0:T(8,128)(2,1)S(1)}, u32[]{:S(2)}, u32[]{:S(2)}) collective-permute-start(bf16[256,1152]{1,0:T(8,128)(2,1)S(1)} %slice.309), channel_id=1, source_target_pairs={{0,16},{1,17},{2,18},{3,19},{4,20},{5,21},{6,22},{7,23},{8,24},{9,... | collective-permute-start | bytes 1769480 | tf_op jit(solution)/shard_map/ppermute | solution.py:515
  172.6 14.6 %copy-start = (bf16[576,1024]{1,0:T(8,128)(2,1)}, bf16[576,1024]{1,0:T(8,128)(2,1)S(1)}, u32[]{:S(2)}) copy-start(bf16[576,1024]{1,0:T(8,128)(2,1)S(1)} %pad_maximum_fusion.4.refs_0_) | copy-start | bytes 3538948
  172.6 14.5 %collective-permute-start.8 = (bf16[576,1024]{1,0:T(8,128)(2,1)S(1)}, bf16[576,1024]{1,0:T(8,128)(2,1)S(1)}, u32[]{:S(2)}, u32[]{:S(2)}) collective-permute-start(bf16[576,1024]{1,0:T(8,128)(2,1)S(1)} %pad_maximum_fusion.4.refs_0_), channel_id=1, source_target_pairs={{0,1},{1,0},{2,3},{3,2},{4,5},{5,4},{6,7},{7,6},{8,9},{9,8},{10,11... | collective-permute-start | bytes 3538952 | tf_op jit(solution)/shard_map/ppermute | solution.py:515
  184.8 12.2 %collective-permute-start.10 = (bf16[512,1152]{1,0:T(8,128)(2,1)S(1)}, bf16[512,1152]{1,0:T(8,128)(2,1)S(1)}, u32[]{:S(2)}, u32[]{:S(2)}) collective-permute-start(bf16[512,1152]{1,0:T(8,128)(2,1)S(1)} %pad_maximum_fusion.5), channel_id=1, source_target_pairs={{0,1},{1,0},{2,3},{3,2},{4,5},{5,4},{6,7},{7,6},{8,9},{9,8},{10,11... | collective-permute-start | bytes 3538952 | tf_op jit(solution)/shard_map/ppermute | solution.py:515
  187.1 9.9 %copy-start.6 = (bf16[576,1024]{1,0:T(8,128)(2,1)}, bf16[576,1024]{1,0:T(8,128)(2,1)S(1)}, u32[]{:S(2)}) copy-start(bf16[576,1024]{1,0:T(8,128)(2,1)S(1)} %collective-permute-done.8.refs_1_) | copy-start | bytes 3538948
  217.7 3.4 collective-permute-start.11
  223.2 15.8 %collective-permute-start.12 = (bf16[256,1152]{1,0:T(8,128)(2,1)}, bf16[256,1152]{1,0:T(8,128)(2,1)}, u32[]{:S(2)}, u32[]{:S(2)}) collective-permute-start(bf16[256,1152]{1,0:T(8,128)(2,1)} %add_convert_fusion.4), channel_id=1, source_target_pairs={{0,16},{1,17},{2,18},{3,19},{4,20},{5,21},{6,22},{7,23},{8,24},{9,... | collective-permute-start | bytes 1769480 | tf_op jit(solution)/shard_map/ppermute | solution.py:515
  236.0 182.2 %reduce-scatter.5.cloned.1.call-start = ((), (), s32[]{:S(2)}) async-start(), calls=%async_computation.7 | async-start | bytes 1658880 | tf_op jit(solution)/shard_map/reduce_scatter | solution.py:668
  247.0 15.0 %copy-start.17 = (bf16[256,1152]{1,0:T(8,128)(2,1)}, bf16[256,1152]{1,0:T(8,128)(2,1)S(1)}, u32[]{:S(2)}) copy-start(bf16[256,1152]{1,0:T(8,128)(2,1)S(1)} %get-tuple-element.86) | copy-start | bytes 1769476
  247.0 15.0 %collective-permute-start.13 = (bf16[256,1152]{1,0:T(8,128)(2,1)S(1)}, bf16[256,1152]{1,0:T(8,128)(2,1)S(1)}, u32[]{:S(2)}, u32[]{:S(2)}) collective-permute-start(bf16[256,1152]{1,0:T(8,128)(2,1)S(1)} %get-tuple-element.86), channel_id=1, source_target_pairs={{0,16},{1,17},{2,18},{3,19},{4,20},{5,21},{6,22},{7,23},{8,24},{9,... | collective-permute-start | bytes 1769480 | tf_op jit(solution)/shard_map/ppermute | solution.py:515
  263.2 3.2 collective-permute-start.14
  270.2 24.7 %copy-start.7 = (bf16[576,1024]{1,0:T(8,128)(2,1)S(1)}, bf16[576,1024]{1,0:T(8,128)(2,1)}, u32[]{:S(2)}) copy-start(bf16[576,1024]{1,0:T(8,128)(2,1)} %copy-done.6) | copy-start | bytes 3538948
  313.7 3.2 collective-permute-start.15
  315.0 35.8 %collective-permute-start.17 = (bf16[4,144,1152]{2,1,0:T(8,128)(2,1)}, bf16[4,144,1152]{2,1,0:T(8,128)(2,1)}, u32[]{:S(2)}, u32[]{:S(2)}) collective-permute-start(bf16[4,144,1152]{2,1,0:T(8,128)(2,1)} %get-tuple-element.88), channel_id=1, source_target_pairs={{0,2},{1,3},{2,0},{3,1},{4,6},{5,7},{6,4},{7,5},{8,10},{9,11},{10,... | collective-permute-start | bytes 3981320 | tf_op jit(solution)/shard_map/ppermute | solution.py:515
  318.3 15.4 %collective-permute-start.18 = (bf16[256,1152]{1,0:T(8,128)(2,1)S(1)}, bf16[256,1152]{1,0:T(8,128)(2,1)S(1)}, u32[]{:S(2)}, u32[]{:S(2)}) collective-permute-start(bf16[256,1152]{1,0:T(8,128)(2,1)S(1)} %add_convert_fusion.3), channel_id=1, source_target_pairs={{0,16},{1,17},{2,18},{3,19},{4,20},{5,21},{6,22},{7,23},{8,24},{9,... | collective-permute-start | bytes 1769480 | tf_op jit(solution)/shard_map/ppermute | solution.py:515
  319.8 14.0 %copy-start.20 = (bf16[1024,1152]{1,0:T(8,128)(2,1)S(1)}, bf16[1024,1152]{1,0:T(8,128)(2,1)}, u32[]{:S(2)}) copy-start(bf16[1024,1152]{1,0:T(8,128)(2,1)} %get-tuple-element.61) | copy-start | bytes 7077892
  321.6 15.6 %collective-permute-start.16 = (bf16[512,1152]{1,0:T(8,128)(2,1)S(1)}, bf16[512,1152]{1,0:T(8,128)(2,1)S(1)}, u32[]{:S(2)}, u32[]{:S(2)}) collective-permute-start(bf16[512,1152]{1,0:T(8,128)(2,1)S(1)} %pad_maximum_fusion.9), channel_id=1, source_target_pairs={{0,1},{1,0},{2,3},{3,2},{4,5},{5,4},{6,7},{7,6},{8,9},{9,8},{10,11... | collective-permute-start | bytes 3538952 | tf_op jit(solution)/shard_map/ppermute | solution.py:515
  322.0 13.5 %copy-start.19 = (f32[256,1152]{1,0:T(8,128)S(1)}, f32[256,1152]{1,0:T(8,128)}, u32[]{:S(2)}) copy-start(f32[256,1152]{1,0:T(8,128)} %get-tuple-element.87) | copy-start | bytes 3538948
  354.7 42.1 %collective-permute-start.27 = (bf16[64,1152]{1,0:T(8,128)(2,1)}, bf16[64,1152]{1,0:T(8,128)(2,1)S(1)}, u32[]{:S(2)}, u32[]{:S(2)}) collective-permute-start(bf16[64,1152]{1,0:T(8,128)(2,1)} %get-tuple-element.119), channel_id=1, source_target_pairs={{0,0},{1,1},{2,16},{3,17},{4,4},{5,5},{6,20},{7,21},{8,8},{9,9},{1... | collective-permute-start | bytes 442376 | tf_op jit(solution)/shard_map/ppermute | solution.py:515
  356.3 44.2 %collective-permute-start.26 = (bf16[64,1152]{1,0:T(8,128)(2,1)}, bf16[64,1152]{1,0:T(8,128)(2,1)}, u32[]{:S(2)}, u32[]{:S(2)}) collective-permute-start(bf16[64,1152]{1,0:T(8,128)(2,1)} %get-tuple-element.120), channel_id=1, source_target_pairs={{0,12},{1,13},{2,28},{3,29},{4,0},{5,1},{6,16},{7,17},{8,4},{9,5},... | collective-permute-start | bytes 442376 | tf_op jit(solution)/shard_map/ppermute | solution.py:515
  359.6 40.9 %collective-permute-start.25 = (bf16[64,1152]{1,0:T(8,128)(2,1)}, bf16[64,1152]{1,0:T(8,128)(2,1)}, u32[]{:S(2)}, u32[]{:S(2)}) collective-permute-start(bf16[64,1152]{1,0:T(8,128)(2,1)} %get-tuple-element.121), channel_id=1, source_target_pairs={{0,8},{1,9},{2,24},{3,25},{4,12},{5,13},{6,28},{7,29},{8,0},{9,1},... | collective-permute-start | bytes 442376 | tf_op jit(solution)/shard_map/ppermute | solution.py:515
  359.6 50.1 %collective-permute-start.24 = (bf16[64,1152]{1,0:T(8,128)(2,1)}, bf16[64,1152]{1,0:T(8,128)(2,1)}, u32[]{:S(2)}, u32[]{:S(2)}) collective-permute-start(bf16[64,1152]{1,0:T(8,128)(2,1)} %get-tuple-element.118), channel_id=1, source_target_pairs={{0,4},{1,5},{2,20},{3,21},{4,8},{5,9},{6,24},{7,25},{8,12},{9,13},... | collective-permute-start | bytes 442376 | tf_op jit(solution)/shard_map/ppermute | solution.py:515
  361.7 1.8 collective-permute-start.30
  363.5 25.6 %collective-permute-start.19 = (bf16[256,1152]{1,0:T(8,128)(2,1)}, bf16[256,1152]{1,0:T(8,128)(2,1)S(1)}, u32[]{:S(2)}, u32[]{:S(2)}) collective-permute-start(bf16[256,1152]{1,0:T(8,128)(2,1)} %add_convert_fusion.2), channel_id=1, source_target_pairs={{0,16},{1,17},{2,18},{3,19},{4,20},{5,21},{6,22},{7,23},{8,24},{9,... | collective-permute-start | bytes 1769480 | tf_op jit(solution)/shard_map/ppermute | solution.py:515
  370.9 18.2 %copy-start.27 = (bf16[512,1152]{1,0:T(8,128)(2,1)S(1)}, bf16[512,1152]{1,0:T(8,128)(2,1)}, u32[]{:S(2)}) copy-start(bf16[512,1152]{1,0:T(8,128)(2,1)} %copy-done.26) | copy-start | bytes 3538948
  390.7 25.0 %copy-start.43 = (pred[4]{0:T(512)(128)(4,1)S(1)}, pred[4]{0:T(512)(128)(4,1)}, u32[]{:S(2)}) copy-start(pred[4]{0:T(512)(128)(4,1)} %broadcast_compare_fusion.2) | copy-start | bytes 16
  390.8 25.0 %copy-start.44 = (pred[4]{0:T(512)(128)(4,1)S(1)}, pred[4]{0:T(512)(128)(4,1)}, u32[]{:S(2)}) copy-start(pred[4]{0:T(512)(128)(4,1)} %get-tuple-element.172) | copy-start | bytes 16
  390.8 25.0 %copy-start.45 = (pred[4]{0:T(512)(128)(4,1)S(1)}, pred[4]{0:T(512)(128)(4,1)}, u32[]{:S(2)}) copy-start(pred[4]{0:T(512)(128)(4,1)} %get-tuple-element.173) | copy-start | bytes 16
  390.8 18.9 %collective-permute-start.23 = (bf16[64,1152]{1,0:T(8,128)(2,1)S(1)}, bf16[64,1152]{1,0:T(8,128)(2,1)S(1)}, u32[]{:S(2)}, u32[]{:S(2)}) collective-permute-start(bf16[64,1152]{1,0:T(8,128)(2,1)S(1)} %get-tuple-element.123), channel_id=1, source_target_pairs={{0,0},{1,1},{2,16},{3,17},{4,4},{5,5},{6,20},{7,21},{8,8},{9,9},{1... | collective-permute-start | bytes 442376 | tf_op jit(solution)/shard_map/ppermute | solution.py:515
  392.3 12.2 %all-to-all-start = ((f32[32,1,512]{2,1,0:T(1,128)}), f32[32,1,512]{2,1,0:T(1,128)S(1)}, u32[]{:S(2)}, u32[]{:S(2)}) async-start(f32[32,1,512]{2,1,0:T(1,128)} %bitcast.16), calls=%async_computation.2 | async-start | bytes 131072 | tf_op jit(solution)/shard_map/all_to_all | solution.py:691
  396.9 12.9 %collective-permute-start.22 = (bf16[64,1152]{1,0:T(8,128)(2,1)S(1)}, bf16[64,1152]{1,0:T(8,128)(2,1)S(1)}, u32[]{:S(2)}, u32[]{:S(2)}) collective-permute-start(bf16[64,1152]{1,0:T(8,128)(2,1)S(1)} %get-tuple-element.124), channel_id=1, source_target_pairs={{0,12},{1,13},{2,28},{3,29},{4,0},{5,1},{6,16},{7,17},{8,4},{9,5},... | collective-permute-start | bytes 442376 | tf_op jit(solution)/shard_map/ppermute | solution.py:515
  400.6 15.2 %collective-permute-start.21 = (bf16[64,1152]{1,0:T(8,128)(2,1)S(1)}, bf16[64,1152]{1,0:T(8,128)(2,1)S(1)}, u32[]{:S(2)}, u32[]{:S(2)}) collective-permute-start(bf16[64,1152]{1,0:T(8,128)(2,1)S(1)} %get-tuple-element.125), channel_id=1, source_target_pairs={{0,8},{1,9},{2,24},{3,25},{4,12},{5,13},{6,28},{7,29},{8,0},{9,1},... | collective-permute-start | bytes 442376 | tf_op jit(solution)/shard_map/ppermute | solution.py:515
  400.6 15.2 %collective-permute-start.20 = (bf16[64,1152]{1,0:T(8,128)(2,1)S(1)}, bf16[64,1152]{1,0:T(8,128)(2,1)S(1)}, u32[]{:S(2)}, u32[]{:S(2)}) collective-permute-start(bf16[64,1152]{1,0:T(8,128)(2,1)S(1)} %get-tuple-element.122), channel_id=1, source_target_pairs={{0,4},{1,5},{2,20},{3,21},{4,8},{5,9},{6,24},{7,25},{8,12},{9,13},... | collective-permute-start | bytes 442376 | tf_op jit(solution)/shard_map/ppermute | solution.py:515
  405.3 12.9 %all-to-all-start.1 = ((f32[32,1,512]{2,1,0:T(1,128)}), f32[32,1,512]{2,1,0:T(1,128)S(1)}, u32[]{:S(2)}, u32[]{:S(2)}) async-start(f32[32,1,512]{2,1,0:T(1,128)} %broadcast_in_dim.152), calls=%async_computation.3 | async-start | bytes 131072 | tf_op jit(solution)/shard_map/all_to_all | solution.py:694
  419.3 1.5 collective-permute-start.28
  421.3 6.1 %collective-permute-start.29 = (bf16[72,576]{1,0:T(8,128)(2,1)S(1)}, bf16[72,576]{1,0:T(8,128)(2,1)S(1)}, u32[]{:S(2)}, u32[]{:S(2)}) collective-permute-start(bf16[72,576]{1,0:T(8,128)(2,1)S(1)} %select_convert_fusion.2), channel_id=1, source_target_pairs={{0,16},{1,17},{2,18},{3,19},{4,20},{5,21},{6,22},{7,23},{8,24},{9,... | collective-permute-start | bytes 248840 | tf_op jit(solution)/shard_map/ppermute | solution.py:515
  (36 other events, 100.1 us)
Sparse Core Ops, SparseCore 0:
  20.6 85.0 all-gather.2
  108.0 87.2 all-gather.4
  236.1 103.7 reduce-scatter.2
  354.0 39.3 reduce-scatter.4

commit v3 on v2

--- a/solution.py
+++ b/solution.py
@@ -746,12 +746,12 @@
     ]
     marks = jnp.broadcast_to(patch_mask.astype(BF16)[:, :, None], (images, tokens, 128))
     own_in = route.tokens_in(jnp.concatenate([patches, marks, cotangent], axis=2))
+    own_in, own_grad = own_in[:, : width + 128], own_in[:, width + 128 :]
+    rows_all = route.rows_gather(own_in)
     packed = jnp.concatenate(vectors, axis=1)
     own_qkv, qkv_block, full_out, mlp, pick, halves = route.weights(
-        w_qkv, w_out, sides, packed, own_in
-    )
-    own_in, own_grad = own_in[:, : width + 128], own_in[:, width + 128 :]
-    rows_all = route.rows_gather(own_in)
+        w_qkv, w_out, sides, packed, rows_all
+    )
     halves = halves.astype(F32)
     full = []
     spot = 0

time: 441 us -> 437 us (level)
  waiting for transfers between devices: 184 us -> 178 us
    all_gather x1, waiting for transfers between devices: 47.1 us -> 19.7 us  [weights(): full_qkv = lax.all_gather(full_qkv, everyone, axis=0, tiled=True)]
    all_gather x1, waiting for transfers between devices: 0.02 us -> 21.4 us  [weights(): rest = lax.all_gather(rest, everyone, axis=0, tiled=True)]
  transfers between devices with their start and end apart: 37 -> 37, of which waited for: 18 -> 20; matrix products, arithmetic and copies ran while one was open for 15% -> 15% of each run, Pallas kernels for 19% -> 19%
where the time goes in v3:
time: 437 us; the launch traced here: 431 us
  waiting for transfers between devices  178 us (41%)
  Pallas kernels  98.1 us (22%)
  starting transfers between devices  51 us (12%)
  other arithmetic  49.7 us (11%)
  local copies, waits for them, and re-layouts  38.8 us (9%)
  between operations  15.4 us (4%)
    ppermute x31, waiting for transfers between devices, send(): return lax.ppermute(values, ('dev', 'z', 'y', 'core'), joint(move))  135 us
    pallas_call x10, Pallas kernels, run(): pl.pallas_call(body, name=name, grid_spec=pltpu.PrefetchScalarGridSpec(nu...  98.1 us
    ppermute x31, starting transfers between devices, send(): return lax.ppermute(values, ('dev', 'z', 'y', 'core'), joint(move))  41.5 us
    all_gather x1, waiting for transfers between devices, weights(): rest = lax.all_gather(rest, everyone, axis=0, tiled=True)  21.4 us
    all_gather x1, waiting for transfers between devices, weights(): full_qkv = lax.all_gather(full_qkv, everyone, axis=0, tiled=True)  19.7 us
  transfers between devices with their start and end apart: 37, of which 20 were waited for; matrix products, arithmetic and copies ran while one was open for 15% of the time, Pallas kernels for 19%

profile of v3, /device:TPU:0, one launch (start us, length us, event | category | flops | bytes accessed | tf_op | source)
XLA Modules:
  0.0 431.3 jit_solution(10607051491441564348)
XLA Ops:
  10.3 3.0 collective-permute-start.6
  13.3 4.6 %collective-permute-done.6 = bf16[80,1152]{1,0:T(8,128)(2,1)S(1)} collective-permute-done((bf16[80,1152]{1,0:T(8,128)(2,1)S(1)}, bf16[80,1152]{1,0:T(8,128)(2,1)S(1)}, u32[]{:S(2)}, u32[]{:S(2)}) %collective-permute-start.6) | collective-permute-done | bytes 184352 | tf_op jit(solution)/shard_map/ppermute | solution.py:515
  21.8 1.9 collective-permute-start.1
  23.6 2.6 collective-permute-start.2
  27.6 6.5 %collective-permute-done.1 = bf16[64,2432]{1,0:T(8,128)(2,1)S(1)} collective-permute-done((bf16[64,2432]{1,0:T(8,128)(2,1)S(1)}, bf16[64,2432]{1,0:T(8,128)(2,1)S(1)}, u32[]{:S(2)}, u32[]{:S(2)}) %collective-permute-start.1) | collective-permute-done | bytes 311328 | tf_op jit(solution)/shard_map/ppermute | solution.py:515
  34.1 22.3 %collective-permute-done.2 = bf16[64,2432]{1,0:T(8,128)(2,1)S(1)} collective-permute-done((bf16[64,2432]{1,0:T(8,128)(2,1)S(1)}, bf16[64,2432]{1,0:T(8,128)(2,1)S(1)}, u32[]{:S(2)}, u32[]{:S(2)}) %collective-permute-start.2) | collective-permute-done | bytes 311328 | tf_op jit(solution)/shard_map/ppermute | solution.py:515
  58.1 4.1 collective-permute-start.4
  62.2 14.6 %collective-permute-done.4 = bf16[256,1280]{1,0:T(8,128)(2,1)S(1)} collective-permute-done((bf16[256,1280]{1,0:T(8,128)(2,1)S(1)}, bf16[256,1280]{1,0:T(8,128)(2,1)S(1)}, u32[]{:S(2)}, u32[]{:S(2)}) %collective-permute-start.4) | collective-permute-done | bytes 655392 | tf_op jit(solution)/shard_map/ppermute | solution.py:515
  79.0 1.7 slice.251
  81.8 1.8 fusion.17
  85.9 19.7 %all-gather.3.cloned.1.call-done.weight_ref = bf16[1152,2944]{1,0:T(8,128)(2,1)} async-done(((bf16[72,2944]{1,0:T(8,128)(2,1)}), bf16[1152,2944]{1,0:T(8,128)(2,1)}) %all-gather.3.cloned.1.call-update) | async-done | bytes 6782992 | tf_op jit(solution)/shard_map/all_gather | solution.py:631
  113.7 6.9 %project.1 = (bf16[1024,1152]{1,0:T(8,128)(2,1)}, bf16[1024,864]{1,0:T(8,128)(2,1)S(1)}) custom-call(s32[1]{0:T(128)} %bitcast._, bf16[1024,1280]{1,0:T(8,128)(2,1)} %copy-done.13, f32[1,1152]{1,0:T(1,128)S(1)} %reshape.512.gain_ref, f32[1,1152]{1,0:T(1,128)S(1)} %reshape.513.shift_ref, bf16[1152,2944]{1,0:T(8,128)(2,1)} %all-gather.3.cloned.1.call-done.weight_ref, ...), custom_call_target="tpu_custom_call" | custom-call | flops 2038431744 | bytes 9417088 | tf_op jit(solution)/shard_map/project/pallas_call | solution.py:106
  120.7 12.4 %attend_fwd.1 = (bf16[1,288,1024]{2,1,0:T(8,128)(2,1)S(1)}, f32[1,8,1024]{2,1,0:T(8,128)S(1)}) custom-call(bf16[1,1024,864]{2,1,0:T(8,128)(2,1)S(1)} %bitcast.34, f32[1,1024,1]{2,1,0:T(8,128)S(1)} %fusion.41.bias_ref), custom_call_target="tpu_custom_call" | custom-call | flops 2147483648 | bytes 1773568 | tf_op jit(solution)/shard_map/attend_fwd/pallas_call | solution.py:106
  135.5 13.8 %collective-permute-done.7 = bf16[288,1024]{1,0:T(8,128)(2,1)S(1)} collective-permute-done((bf16[288,1024]{1,0:T(8,128)(2,1)S(1)}, bf16[288,1024]{1,0:T(8,128)(2,1)S(1)}, u32[]{:S(2)}, u32[]{:S(2)}) %collective-permute-start.7) | collective-permute-done | bytes 589856 | tf_op jit(solution)/shard_map/ppermute | solution.py:515
  149.5 11.8 %collective-permute-done.9 = bf16[256,1152]{1,0:T(8,128)(2,1)S(1)} collective-permute-done((bf16[256,1152]{1,0:T(8,128)(2,1)S(1)}, bf16[256,1152]{1,0:T(8,128)(2,1)S(1)}, u32[]{:S(2)}, u32[]{:S(2)}) %collective-permute-start.9) | collective-permute-done | bytes 589856 | tf_op jit(solution)/shard_map/ppermute | solution.py:515
  161.9 1.7 pad_maximum_fusion.refs_2_
  163.8 9.9 %attend_out.1 = (f32[1024,1152]{1,0:T(8,128)}, bf16[1024,1152]{1,0:T(8,128)(2,1)}) custom-call(bf16[576,1024]{1,0:T(8,128)(2,1)S(1)} %pad_maximum_fusion.4.refs_0_, bf16[576,1024]{1,0:T(8,128)(2,1)S(1)} %collective-permute-done.8.refs_1_, bf16[2,576,1152]{2,1,0:T(8,128)(2,1)} %pad_maximum_fusion.refs_2_, bf16[1024,1280]{1,0:T(8,128)(2,1)} %copy-done.13, ...), custom_call_target="tpu_custom_call" | custom-call | flops 2717908992 | bytes 7648768 | tf_op jit(solution)/shard_map/attend_out/pallas_call | solution.py:106
  173.8 21.4 %all-gather.5.cloned.1.call-done.mlp_ref = bf16[1152,4608]{1,0:T(8,128)(2,1)} async-done(((bf16[72,4608]{1,0:T(8,128)(2,1)}), bf16[1152,4608]{1,0:T(8,128)(2,1)}) %all-gather.5.cloned.1.call-update) | async-done | bytes 10616848 | tf_op jit(solution)/shard_map/all_gather | solution.py:633
  195.9 15.0 %mlp_turn.1 = (bf16[1024,1152]{1,0:T(8,128)(2,1)S(1)}, bf16[1024,1152]{1,0:T(8,128)(2,1)}, bf16[1024,1152]{1,0:T(8,128)(2,1)}, f32[1,1152]{1,0:T(1,128)S(1)}) custom-call(s32[1]{0:T(128)} %bitcast._, bf16[1024,1152]{1,0:T(8,128)(2,1)} %get-tuple-element.48.normed_ref.refs_1_, bf16[1024,1152]{1,0:T(8,128)(2,1)} %copy-done.2, ...), custom_call_target="tpu_custom_call" | custom-call | flops 8153726976 | bytes 15340032 | tf_op jit(solution)/shard_map/mlp_turn/pallas_call | solution.py:106
  210.9 2.2 constant_dynamic-slice_fusion.19
  217.5 2.0 add_convert_fusion.4
  221.6 10.8 %mlp_grads.1 = bf16[1152,2304]{1,0:T(8,128)(2,1)} custom-call(bf16[1024,1152]{1,0:T(8,128)(2,1)S(1)} %copy-done.3, bf16[1024,1152]{1,0:T(8,128)(2,1)} %get-tuple-element.48.normed_ref.refs_1_, bf16[1024,1152]{1,0:T(8,128)(2,1)} %copy-done.4, bf16[1024,1152]{1,0:T(8,128)(2,1)} %get-tuple-element.53.refs_3_), custom_call_target="tpu_custom_call" | custom-call | flops 5435817984 | bytes 9437184 | tf_op jit(solution)/shard_map/mlp_grads/pallas_call | solution.py:106
  232.7 2.7 collective-permute-done.12
  235.3 2.0 multiply_reduce_fusion.2
  237.4 2.5 multiply_reduce_fusion
  239.9 3.5 convert_reduce_fusion.2
  244.9 7.0 %mlp_out.1 = bf16[1024,1152]{1,0:T(8,128)(2,1)S(1)} custom-call(s32[1]{0:T(128)} %bitcast._, bf16[1024,1152]{1,0:T(8,128)(2,1)} %copy-done.4, bf16[1152,4608]{1,0:T(8,128)(2,1)} %all-gather.5.cloned.1.call-done.mlp_ref), custom_call_target="tpu_custom_call" | custom-call | flops 54358180 | bytes 259522 | tf_op jit(solution)/shard_map/mlp_out/pallas_call | solution.py:106
  251.8 6.4 %collective-permute-done.13 = bf16[256,1152]{1,0:T(8,128)(2,1)S(1)} collective-permute-done((bf16[256,1152]{1,0:T(8,128)(2,1)S(1)}, bf16[256,1152]{1,0:T(8,128)(2,1)S(1)}, u32[]{:S(2)}, u32[]{:S(2)}) %collective-permute-start.13) | collective-permute-done | bytes 589856 | tf_op jit(solution)/shard_map/ppermute | solution.py:515
  260.8 1.9 collective-permute-done.14
  266.4 23.0 %attend_bwd.1 = bf16[1,1024,864]{2,1,0:T(8,128)(2,1)S(1)} custom-call(bf16[1,1024,864]{2,1,0:T(8,128)(2,1)} %bitcast.35, f32[1,1024,1]{2,1,0:T(8,128)S(1)} %fusion.41.bias_ref, f32[1,8,1024]{2,1,0:T(8,128)S(1)} %copy-done.9, bf16[1,1024,1152]{2,1,0:T(8,128)(2,1)} %bitcast.38, bf16[288,1152]{1,0:T(8,128)(2,1)S(1)} %get-tuple-element.90.w_ref), custom_call_target="tpu_custom_call" | custom-call | flops 107374184 | bytes 96583 | tf_op jit(solution)/shard_map/attend_bwd/pallas_call | solution.py:106
  292.5 4.3 %qkv_grads.1 = bf16[1152,864]{1,0:T(8,128)(2,1)S(1)} custom-call(bf16[1024,1152]{1,0:T(8,128)(2,1)} %get-tuple-element.59.refs_0_, bf16[1024,864]{1,0:T(8,128)(2,1)S(1)} %bitcast.30), custom_call_target="tpu_custom_call" | custom-call | flops 40768632 | bytes 82575 | tf_op jit(solution)/shard_map/qkv_grads/pallas_call | solution.py:106
  298.3 1.8 dynamic-slice_bitcast_fusion
  300.1 7.3 %project_back.1 = (bf16[1024,1152]{1,0:T(8,128)(2,1)}, f32[2,1152]{1,0:T(2,128)S(1)}, f32[1,864]{1,0:T(1,128)S(1)}) custom-call(s32[1]{0:T(128)} %bitcast._, bf16[1024,864]{1,0:T(8,128)(2,1)S(1)} %bitcast.31, bf16[1152,2944]{1,0:T(8,128)(2,1)} %all-gather.3.cloned.1.call-done.weight_ref, bf16[1024,1280]{1,0:T(8,128)(2,1)} %copy-done.13), custom_call_target="tpu_custom_call" | custom-call | flops 40768632 | bytes 223477 | tf_op jit(solution)/shard_map/project_back/pallas_call | solution.py:106
  318.5 11.5 %collective-permute-done.18 = bf16[256,1152]{1,0:T(8,128)(2,1)S(1)} collective-permute-done((bf16[256,1152]{1,0:T(8,128)(2,1)S(1)}, bf16[256,1152]{1,0:T(8,128)(2,1)S(1)}, u32[]{:S(2)}, u32[]{:S(2)}) %collective-permute-start.18) | collective-permute-done | bytes 589856 | tf_op jit(solution)/shard_map/ppermute | solution.py:515
  331.7 1.7 fusion.10
  335.4 11.4 %collective-permute-done.17 = bf16[4,144,1152]{2,1,0:T(8,128)(2,1)} collective-permute-done((bf16[4,144,1152]{2,1,0:T(8,128)(2,1)}, bf16[4,144,1152]{2,1,0:T(8,128)(2,1)}, u32[]{:S(2)}, u32[]{:S(2)}) %collective-permute-start.17) | collective-permute-done | bytes 1327136 | tf_op jit(solution)/shard_map/ppermute | solution.py:515
  346.8 3.1 add_convert_fusion
  352.3 3.3 collective-permute-start.26
  359.5 6.0 %collective-permute-start.19 = (bf16[256,1152]{1,0:T(8,128)(2,1)}, bf16[256,1152]{1,0:T(8,128)(2,1)S(1)}, u32[]{:S(2)}, u32[]{:S(2)}) collective-permute-start(bf16[256,1152]{1,0:T(8,128)(2,1)} %add_convert_fusion.2), channel_id=1, source_target_pairs={{0,16},{1,17},{2,18},{3,19},{4,20},{5,21},{6,22},{7,23},{8,24},{9,... | collective-permute-start | bytes 1769480 | tf_op jit(solution)/shard_map/ppermute | solution.py:515
  368.1 17.1 %collective-permute-done.19 = bf16[256,1152]{1,0:T(8,128)(2,1)S(1)} collective-permute-done((bf16[256,1152]{1,0:T(8,128)(2,1)}, bf16[256,1152]{1,0:T(8,128)(2,1)S(1)}, u32[]{:S(2)}, u32[]{:S(2)}) %collective-permute-start.19) | collective-permute-done | bytes 589856 | tf_op jit(solution)/shard_map/ppermute | solution.py:515
  388.3 4.6 %all-to-all-start = ((f32[32,1,512]{2,1,0:T(1,128)}), f32[32,1,512]{2,1,0:T(1,128)S(1)}, u32[]{:S(2)}, u32[]{:S(2)}) async-start(f32[32,1,512]{2,1,0:T(1,128)} %bitcast.16), calls=%async_computation.2 | async-start | bytes 131072 | tf_op jit(solution)/shard_map/all_to_all | solution.py:691
  392.9 3.7 collective-permute-start.22
  398.7 1.9 all-to-all-done
  401.3 4.5 %all-to-all-start.1 = ((f32[32,1,512]{2,1,0:T(1,128)}), f32[32,1,512]{2,1,0:T(1,128)S(1)}, u32[]{:S(2)}, u32[]{:S(2)}) async-start(f32[32,1,512]{2,1,0:T(1,128)} %broadcast_in_dim.152), calls=%async_computation.3 | async-start | bytes 131072 | tf_op jit(solution)/shard_map/all_to_all | solution.py:694
  405.8 5.9 %collective-permute-done.21 = bf16[64,1152]{1,0:T(8,128)(2,1)S(1)} collective-permute-done((bf16[64,1152]{1,0:T(8,128)(2,1)S(1)}, bf16[64,1152]{1,0:T(8,128)(2,1)S(1)}, u32[]{:S(2)}, u32[]{:S(2)}) %collective-permute-start.21) | collective-permute-done | bytes 147488 | tf_op jit(solution)/shard_map/ppermute | solution.py:515
  411.8 2.4 select_select_fusion
  417.3 2.8 collective-permute-start.29
  421.1 2.4 collective-permute-done.29
  (278 shorter events, 80.3 us)
Async XLA Ops:
  7.2 98.5 %all-gather.3.cloned.1.call-start = ((), (), s32[]{:S(2)}) async-start(), calls=%async_computation.4 | async-start | bytes 7206912 | tf_op jit(solution)/shard_map/all_gather | solution.py:631
  10.3 7.6 %collective-permute-start.6 = (bf16[80,1152]{1,0:T(8,128)(2,1)S(1)}, bf16[80,1152]{1,0:T(8,128)(2,1)S(1)}, u32[]{:S(2)}, u32[]{:S(2)}) collective-permute-start(bf16[80,1152]{1,0:T(8,128)(2,1)S(1)} %fusion.48), channel_id=1, source_target_pairs={{0,16},{1,17},{2,18},{3,19},{4,20},{5,21},{6,22},{7,23},{8,24},{9,... | collective-permute-start | bytes 552968 | tf_op jit(solution)/shard_map/ppermute | solution.py:515
  20.6 174.6 %all-gather.5.cloned.1.call-start = ((), (), s32[]{:S(2)}) async-start(), calls=%async_computation.5 | async-start | bytes 11280384 | tf_op jit(solution)/shard_map/all_gather | solution.py:633
  21.1 6.5 %collective-permute-start = (bf16[64,2432]{1,0:T(8,128)(2,1)S(1)}, bf16[64,2432]{1,0:T(8,128)(2,1)S(1)}, u32[]{:S(2)}, u32[]{:S(2)}) collective-permute-start(bf16[64,2432]{1,0:T(8,128)(2,1)S(1)} %get-tuple-element.107), channel_id=1, source_target_pairs={{0,0},{1,1},{2,16},{3,17},{4,4},{5,5},{6,20},{7,21},{8,8},{9,9},{1... | collective-permute-start | bytes 933896 | tf_op jit(solution)/shard_map/ppermute | solution.py:515
  21.8 12.3 %collective-permute-start.1 = (bf16[64,2432]{1,0:T(8,128)(2,1)S(1)}, bf16[64,2432]{1,0:T(8,128)(2,1)S(1)}, u32[]{:S(2)}, u32[]{:S(2)}) collective-permute-start(bf16[64,2432]{1,0:T(8,128)(2,1)S(1)} %get-tuple-element.106), channel_id=1, source_target_pairs={{0,4},{1,5},{2,20},{3,21},{4,8},{5,9},{6,24},{7,25},{8,12},{9,13},... | collective-permute-start | bytes 933896 | tf_op jit(solution)/shard_map/ppermute | solution.py:515
  23.6 32.8 %collective-permute-start.2 = (bf16[64,2432]{1,0:T(8,128)(2,1)S(1)}, bf16[64,2432]{1,0:T(8,128)(2,1)S(1)}, u32[]{:S(2)}, u32[]{:S(2)}) collective-permute-start(bf16[64,2432]{1,0:T(8,128)(2,1)S(1)} %get-tuple-element.105), channel_id=1, source_target_pairs={{0,8},{1,9},{2,24},{3,25},{4,12},{5,13},{6,28},{7,29},{8,0},{9,1},... | collective-permute-start | bytes 933896 | tf_op jit(solution)/shard_map/ppermute | solution.py:515
  26.2 30.8 %collective-permute-start.3 = (bf16[64,2432]{1,0:T(8,128)(2,1)S(1)}, bf16[64,2432]{1,0:T(8,128)(2,1)S(1)}, u32[]{:S(2)}, u32[]{:S(2)}) collective-permute-start(bf16[64,2432]{1,0:T(8,128)(2,1)S(1)} %get-tuple-element.104), channel_id=1, source_target_pairs={{0,12},{1,13},{2,28},{3,29},{4,0},{5,1},{6,16},{7,17},{8,4},{9,5},... | collective-permute-start | bytes 933896 | tf_op jit(solution)/shard_map/ppermute | solution.py:515
  58.1 22.7 %copy-start.41 = (pred[1152]{0:T(1024)(128)(4,1)S(1)}, pred[1152]{0:T(1024)(128)(4,1)}, u32[]{:S(2)}) copy-start(pred[1152]{0:T(1024)(128)(4,1)} %constant.244.clone.1) | copy-start | bytes 3460
  58.1 18.8 %collective-permute-start.4 = (bf16[256,1280]{1,0:T(8,128)(2,1)S(1)}, bf16[256,1280]{1,0:T(8,128)(2,1)S(1)}, u32[]{:S(2)}, u32[]{:S(2)}) collective-permute-start(bf16[256,1280]{1,0:T(8,128)(2,1)S(1)} %get-tuple-element.102), channel_id=1, source_target_pairs={{0,16},{1,17},{2,18},{3,19},{4,20},{5,21},{6,22},{7,23},{8,24},{9,... | collective-permute-start | bytes 1966088 | tf_op jit(solution)/shard_map/ppermute | solution.py:515
  78.0 5.7 %collective-permute-start.5 = (bf16[512,1280]{1,0:T(8,128)(2,1)}, bf16[512,1280]{1,0:T(8,128)(2,1)}, u32[]{:S(2)}, u32[]{:S(2)}) collective-permute-start(bf16[512,1280]{1,0:T(8,128)(2,1)} %pad_maximum_fusion.2), channel_id=1, source_target_pairs={{0,1},{1,0},{2,3},{3,2},{4,5},{5,4},{6,7},{7,6},{8,9},{9,8},{10,11... | collective-permute-start | bytes 3932168 | tf_op jit(solution)/shard_map/ppermute | solution.py:515
  85.9 26.7 %copy-start.13 = (bf16[1024,1280]{1,0:T(8,128)(2,1)}, bf16[1024,1280]{1,0:T(8,128)(2,1)S(1)}, u32[]{:S(2)}) copy-start(bf16[1024,1280]{1,0:T(8,128)(2,1)S(1)} %slice_dynamic-update-slice_fusion.rows_ref.refs_3_) | copy-start | bytes 7864324
  105.7 241.1 %reduce-scatter.3.cloned.1.call-start = ((), (), s32[]{:S(2)}) async-start(), calls=%async_computation.6 | async-start | bytes 5971968 | tf_op jit(solution)/shard_map/reduce_scatter | solution.py:650
  133.1 16.2 %collective-permute-start.7 = (bf16[288,1024]{1,0:T(8,128)(2,1)S(1)}, bf16[288,1024]{1,0:T(8,128)(2,1)S(1)}, u32[]{:S(2)}, u32[]{:S(2)}) collective-permute-start(bf16[288,1024]{1,0:T(8,128)(2,1)S(1)} %bitcast.36), channel_id=1, source_target_pairs={{0,16},{1,17},{2,18},{3,19},{4,20},{5,21},{6,22},{7,23},{8,24},{9,... | collective-permute-start | bytes 1769480 | tf_op jit(solution)/shard_map/ppermute | solution.py:515
  134.7 26.6 %collective-permute-start.9 = (bf16[256,1152]{1,0:T(8,128)(2,1)S(1)}, bf16[256,1152]{1,0:T(8,128)(2,1)S(1)}, u32[]{:S(2)}, u32[]{:S(2)}) collective-permute-start(bf16[256,1152]{1,0:T(8,128)(2,1)S(1)} %slice.309), channel_id=1, source_target_pairs={{0,16},{1,17},{2,18},{3,19},{4,20},{5,21},{6,22},{7,23},{8,24},{9,... | collective-permute-start | bytes 1769480 | tf_op jit(solution)/shard_map/ppermute | solution.py:515
  149.4 14.3 %copy-start = (bf16[576,1024]{1,0:T(8,128)(2,1)}, bf16[576,1024]{1,0:T(8,128)(2,1)S(1)}, u32[]{:S(2)}) copy-start(bf16[576,1024]{1,0:T(8,128)(2,1)S(1)} %pad_maximum_fusion.4.refs_0_) | copy-start | bytes 3538948
  149.4 14.3 %collective-permute-start.8 = (bf16[576,1024]{1,0:T(8,128)(2,1)S(1)}, bf16[576,1024]{1,0:T(8,128)(2,1)S(1)}, u32[]{:S(2)}, u32[]{:S(2)}) collective-permute-start(bf16[576,1024]{1,0:T(8,128)(2,1)S(1)} %pad_maximum_fusion.4.refs_0_), channel_id=1, source_target_pairs={{0,1},{1,0},{2,3},{3,2},{4,5},{5,4},{6,7},{7,6},{8,9},{9,8},{10,11... | collective-permute-start | bytes 3538952 | tf_op jit(solution)/shard_map/ppermute | solution.py:515
  161.4 12.2 %collective-permute-start.10 = (bf16[512,1152]{1,0:T(8,128)(2,1)S(1)}, bf16[512,1152]{1,0:T(8,128)(2,1)S(1)}, u32[]{:S(2)}, u32[]{:S(2)}) collective-permute-start(bf16[512,1152]{1,0:T(8,128)(2,1)S(1)} %pad_maximum_fusion.5), channel_id=1, source_target_pairs={{0,1},{1,0},{2,3},{3,2},{4,5},{5,4},{6,7},{7,6},{8,9},{9,8},{10,11... | collective-permute-start | bytes 3538952 | tf_op jit(solution)/shard_map/ppermute | solution.py:515
  173.8 21.4 %copy-start.2 = (bf16[1024,1152]{1,0:T(8,128)(2,1)}, bf16[1024,1152]{1,0:T(8,128)(2,1)S(1)}, u32[]{:S(2)}) copy-start(bf16[1024,1152]{1,0:T(8,128)(2,1)S(1)} %slice_dynamic-update-slice_fusion.4.grad_ref.refs_0_) | copy-start | bytes 7077892
  214.3 3.2 collective-permute-start.11
  219.5 15.8 %collective-permute-start.12 = (bf16[256,1152]{1,0:T(8,128)(2,1)}, bf16[256,1152]{1,0:T(8,128)(2,1)}, u32[]{:S(2)}, u32[]{:S(2)}) collective-permute-start(bf16[256,1152]{1,0:T(8,128)(2,1)} %add_convert_fusion.4), channel_id=1, source_target_pairs={{0,16},{1,17},{2,18},{3,19},{4,20},{5,21},{6,22},{7,23},{8,24},{9,... | collective-permute-start | bytes 1769480 | tf_op jit(solution)/shard_map/ppermute | solution.py:515
  232.4 181.9 %reduce-scatter.5.cloned.1.call-start = ((), (), s32[]{:S(2)}) async-start(), calls=%async_computation.7 | async-start | bytes 1658880 | tf_op jit(solution)/shard_map/reduce_scatter | solution.py:668
  243.4 14.8 %copy-start.17 = (bf16[256,1152]{1,0:T(8,128)(2,1)}, bf16[256,1152]{1,0:T(8,128)(2,1)S(1)}, u32[]{:S(2)}) copy-start(bf16[256,1152]{1,0:T(8,128)(2,1)S(1)} %get-tuple-element.86) | copy-start | bytes 1769476
  243.4 14.8 %collective-permute-start.13 = (bf16[256,1152]{1,0:T(8,128)(2,1)S(1)}, bf16[256,1152]{1,0:T(8,128)(2,1)S(1)}, u32[]{:S(2)}, u32[]{:S(2)}) collective-permute-start(bf16[256,1152]{1,0:T(8,128)(2,1)S(1)} %get-tuple-element.86), channel_id=1, source_target_pairs={{0,16},{1,17},{2,18},{3,19},{4,20},{5,21},{6,22},{7,23},{8,24},{9,... | collective-permute-start | bytes 1769480 | tf_op jit(solution)/shard_map/ppermute | solution.py:515
  259.4 3.2 collective-permute-start.14
  266.4 24.7 %copy-start.7 = (bf16[576,1024]{1,0:T(8,128)(2,1)S(1)}, bf16[576,1024]{1,0:T(8,128)(2,1)}, u32[]{:S(2)}) copy-start(bf16[576,1024]{1,0:T(8,128)(2,1)} %copy-done.6) | copy-start | bytes 3538948
  309.9 3.2 collective-permute-start.15
  311.2 35.6 %collective-permute-start.17 = (bf16[4,144,1152]{2,1,0:T(8,128)(2,1)}, bf16[4,144,1152]{2,1,0:T(8,128)(2,1)}, u32[]{:S(2)}, u32[]{:S(2)}) collective-permute-start(bf16[4,144,1152]{2,1,0:T(8,128)(2,1)} %get-tuple-element.88), channel_id=1, source_target_pairs={{0,2},{1,3},{2,0},{3,1},{4,6},{5,7},{6,4},{7,5},{8,10},{9,11},{10,... | collective-permute-start | bytes 3981320 | tf_op jit(solution)/shard_map/ppermute | solution.py:515
  314.5 15.4 %collective-permute-start.18 = (bf16[256,1152]{1,0:T(8,128)(2,1)S(1)}, bf16[256,1152]{1,0:T(8,128)(2,1)S(1)}, u32[]{:S(2)}, u32[]{:S(2)}) collective-permute-start(bf16[256,1152]{1,0:T(8,128)(2,1)S(1)} %add_convert_fusion.3), channel_id=1, source_target_pairs={{0,16},{1,17},{2,18},{3,19},{4,20},{5,21},{6,22},{7,23},{8,24},{9,... | collective-permute-start | bytes 1769480 | tf_op jit(solution)/shard_map/ppermute | solution.py:515
  316.2 13.7 %copy-start.21 = (bf16[1024,1152]{1,0:T(8,128)(2,1)S(1)}, bf16[1024,1152]{1,0:T(8,128)(2,1)}, u32[]{:S(2)}) copy-start(bf16[1024,1152]{1,0:T(8,128)(2,1)} %get-tuple-element.61) | copy-start | bytes 7077892
  318.1 15.3 %collective-permute-start.16 = (bf16[512,1152]{1,0:T(8,128)(2,1)S(1)}, bf16[512,1152]{1,0:T(8,128)(2,1)S(1)}, u32[]{:S(2)}, u32[]{:S(2)}) collective-permute-start(bf16[512,1152]{1,0:T(8,128)(2,1)S(1)} %pad_maximum_fusion.9), channel_id=1, source_target_pairs={{0,1},{1,0},{2,3},{3,2},{4,5},{5,4},{6,7},{7,6},{8,9},{9,8},{10,11... | collective-permute-start | bytes 3538952 | tf_op jit(solution)/shard_map/ppermute | solution.py:515
  350.8 42.1 %collective-permute-start.27 = (bf16[64,1152]{1,0:T(8,128)(2,1)}, bf16[64,1152]{1,0:T(8,128)(2,1)S(1)}, u32[]{:S(2)}, u32[]{:S(2)}) collective-permute-start(bf16[64,1152]{1,0:T(8,128)(2,1)} %get-tuple-element.119), channel_id=1, source_target_pairs={{0,0},{1,1},{2,16},{3,17},{4,4},{5,5},{6,20},{7,21},{8,8},{9,9},{1... | collective-permute-start | bytes 442376 | tf_op jit(solution)/shard_map/ppermute | solution.py:515
  352.3 44.3 %collective-permute-start.26 = (bf16[64,1152]{1,0:T(8,128)(2,1)}, bf16[64,1152]{1,0:T(8,128)(2,1)}, u32[]{:S(2)}, u32[]{:S(2)}) collective-permute-start(bf16[64,1152]{1,0:T(8,128)(2,1)} %get-tuple-element.120), channel_id=1, source_target_pairs={{0,12},{1,13},{2,28},{3,29},{4,0},{5,1},{6,16},{7,17},{8,4},{9,5},... | collective-permute-start | bytes 442376 | tf_op jit(solution)/shard_map/ppermute | solution.py:515
  355.7 40.9 %collective-permute-start.25 = (bf16[64,1152]{1,0:T(8,128)(2,1)}, bf16[64,1152]{1,0:T(8,128)(2,1)}, u32[]{:S(2)}, u32[]{:S(2)}) collective-permute-start(bf16[64,1152]{1,0:T(8,128)(2,1)} %get-tuple-element.121), channel_id=1, source_target_pairs={{0,8},{1,9},{2,24},{3,25},{4,12},{5,13},{6,28},{7,29},{8,0},{9,1},... | collective-permute-start | bytes 442376 | tf_op jit(solution)/shard_map/ppermute | solution.py:515
  355.7 50.1 %collective-permute-start.24 = (bf16[64,1152]{1,0:T(8,128)(2,1)}, bf16[64,1152]{1,0:T(8,128)(2,1)}, u32[]{:S(2)}, u32[]{:S(2)}) collective-permute-start(bf16[64,1152]{1,0:T(8,128)(2,1)} %get-tuple-element.118), channel_id=1, source_target_pairs={{0,4},{1,5},{2,20},{3,21},{4,8},{5,9},{6,24},{7,25},{8,12},{9,13},... | collective-permute-start | bytes 442376 | tf_op jit(solution)/shard_map/ppermute | solution.py:515
  357.7 1.8 collective-permute-start.30
  359.5 25.6 %collective-permute-start.19 = (bf16[256,1152]{1,0:T(8,128)(2,1)}, bf16[256,1152]{1,0:T(8,128)(2,1)S(1)}, u32[]{:S(2)}, u32[]{:S(2)}) collective-permute-start(bf16[256,1152]{1,0:T(8,128)(2,1)} %add_convert_fusion.2), channel_id=1, source_target_pairs={{0,16},{1,17},{2,18},{3,19},{4,20},{5,21},{6,22},{7,23},{8,24},{9,... | collective-permute-start | bytes 1769480 | tf_op jit(solution)/shard_map/ppermute | solution.py:515
  367.0 18.2 %copy-start.28 = (bf16[512,1152]{1,0:T(8,128)(2,1)S(1)}, bf16[512,1152]{1,0:T(8,128)(2,1)}, u32[]{:S(2)}) copy-start(bf16[512,1152]{1,0:T(8,128)(2,1)} %copy-done.27) | copy-start | bytes 3538948
  386.8 25.0 %copy-start.43 = (pred[4]{0:T(512)(128)(4,1)S(1)}, pred[4]{0:T(512)(128)(4,1)}, u32[]{:S(2)}) copy-start(pred[4]{0:T(512)(128)(4,1)} %broadcast_compare_fusion.2) | copy-start | bytes 16
  386.8 25.0 %copy-start.44 = (pred[4]{0:T(512)(128)(4,1)S(1)}, pred[4]{0:T(512)(128)(4,1)}, u32[]{:S(2)}) copy-start(pred[4]{0:T(512)(128)(4,1)} %get-tuple-element.172) | copy-start | bytes 16
  386.8 25.0 %copy-start.45 = (pred[4]{0:T(512)(128)(4,1)S(1)}, pred[4]{0:T(512)(128)(4,1)}, u32[]{:S(2)}) copy-start(pred[4]{0:T(512)(128)(4,1)} %get-tuple-element.173) | copy-start | bytes 16
  386.9 19.0 %collective-permute-start.23 = (bf16[64,1152]{1,0:T(8,128)(2,1)S(1)}, bf16[64,1152]{1,0:T(8,128)(2,1)S(1)}, u32[]{:S(2)}, u32[]{:S(2)}) collective-permute-start(bf16[64,1152]{1,0:T(8,128)(2,1)S(1)} %get-tuple-element.123), channel_id=1, source_target_pairs={{0,0},{1,1},{2,16},{3,17},{4,4},{5,5},{6,20},{7,21},{8,8},{9,9},{1... | collective-permute-start | bytes 442376 | tf_op jit(solution)/shard_map/ppermute | solution.py:515
  388.3 12.2 %all-to-all-start = ((f32[32,1,512]{2,1,0:T(1,128)}), f32[32,1,512]{2,1,0:T(1,128)S(1)}, u32[]{:S(2)}, u32[]{:S(2)}) async-start(f32[32,1,512]{2,1,0:T(1,128)} %bitcast.16), calls=%async_computation.2 | async-start | bytes 131072 | tf_op jit(solution)/shard_map/all_to_all | solution.py:691
  392.9 12.9 %collective-permute-start.22 = (bf16[64,1152]{1,0:T(8,128)(2,1)S(1)}, bf16[64,1152]{1,0:T(8,128)(2,1)S(1)}, u32[]{:S(2)}, u32[]{:S(2)}) collective-permute-start(bf16[64,1152]{1,0:T(8,128)(2,1)S(1)} %get-tuple-element.124), channel_id=1, source_target_pairs={{0,12},{1,13},{2,28},{3,29},{4,0},{5,1},{6,16},{7,17},{8,4},{9,5},... | collective-permute-start | bytes 442376 | tf_op jit(solution)/shard_map/ppermute | solution.py:515
  396.6 15.2 %collective-permute-start.21 = (bf16[64,1152]{1,0:T(8,128)(2,1)S(1)}, bf16[64,1152]{1,0:T(8,128)(2,1)S(1)}, u32[]{:S(2)}, u32[]{:S(2)}) collective-permute-start(bf16[64,1152]{1,0:T(8,128)(2,1)S(1)} %get-tuple-element.125), channel_id=1, source_target_pairs={{0,8},{1,9},{2,24},{3,25},{4,12},{5,13},{6,28},{7,29},{8,0},{9,1},... | collective-permute-start | bytes 442376 | tf_op jit(solution)/shard_map/ppermute | solution.py:515
  396.6 15.2 %collective-permute-start.20 = (bf16[64,1152]{1,0:T(8,128)(2,1)S(1)}, bf16[64,1152]{1,0:T(8,128)(2,1)S(1)}, u32[]{:S(2)}, u32[]{:S(2)}) collective-permute-start(bf16[64,1152]{1,0:T(8,128)(2,1)S(1)} %get-tuple-element.122), channel_id=1, source_target_pairs={{0,4},{1,5},{2,20},{3,21},{4,8},{5,9},{6,24},{7,25},{8,12},{9,13},... | collective-permute-start | bytes 442376 | tf_op jit(solution)/shard_map/ppermute | solution.py:515
  401.3 12.9 %all-to-all-start.1 = ((f32[32,1,512]{2,1,0:T(1,128)}), f32[32,1,512]{2,1,0:T(1,128)S(1)}, u32[]{:S(2)}, u32[]{:S(2)}) async-start(f32[32,1,512]{2,1,0:T(1,128)} %broadcast_in_dim.152), calls=%async_computation.3 | async-start | bytes 131072 | tf_op jit(solution)/shard_map/all_to_all | solution.py:694
  415.3 1.5 collective-permute-start.28
  417.3 6.1 %collective-permute-start.29 = (bf16[72,576]{1,0:T(8,128)(2,1)S(1)}, bf16[72,576]{1,0:T(8,128)(2,1)S(1)}, u32[]{:S(2)}, u32[]{:S(2)}) collective-permute-start(bf16[72,576]{1,0:T(8,128)(2,1)S(1)} %select_convert_fusion.2), channel_id=1, source_target_pairs={{0,16},{1,17},{2,18},{3,19},{4,20},{5,21},{6,22},{7,23},{8,24},{9,... | collective-permute-start | bytes 248840 | tf_op jit(solution)/shard_map/ppermute | solution.py:515
  (36 other events, 113.4 us)
Sparse Core Ops, SparseCore 0:
  20.7 84.8 all-gather.2
  107.9 87.2 all-gather.4
  232.5 103.5 reduce-scatter.2
  350.1 39.3 reduce-scatter.4
